TPU v7x, 32 devices: a whole 2x2x4 slice. The times are simulated.
32 devices in a mesh: wide: 8 (over z, core), narrow: 4 (over y, x).
Axes of the slice: x: 2, y: 2, z: 4, core: 2. Of those that a mesh axis runs over, the one named last changes fastest.
Arguments:
- tokens: bfloat16 [16384, 2048], P('wide', 'narrow'), may hold values from -65 to 65
- segment_ids: int32 [16384], P('wide'), may hold values from 0 to 15, never falling along the last dimension, each value on 1 to 2000 neighbouring positions
- norm1_gain: float32 [2048], replicated, may hold values from 0.25 to 1.75
- in_weight: bfloat16 [2048, 3, 2048], P('wide', None, 'narrow'), may hold values from -0.125 to 0.125
- conv_weight: float32 [3, 2048], replicated, may hold values from -3 to 3
- out_weight: bfloat16 [2048, 2048], P('narrow', 'wide'), may hold values from -0.125 to 0.125
- norm2_gain: float32 [2048], replicated, may hold values from 0.25 to 1.75
- gate_weight: bfloat16 [2048, 8192], P('wide', 'narrow'), may hold values from -0.125 to 0.125
- up_weight: bfloat16 [2048, 8192], P('wide', 'narrow'), may hold values from -0.125 to 0.125
- down_weight: bfloat16 [8192, 2048], P('narrow', 'wide'), may hold values from -0.0625 to 0.0625
- cotangent: bfloat16 [16384, 2048], P('wide', 'narrow'), may hold values from -65 to 65
Outputs:
- block_out: bfloat16 [16384, 2048], P('wide', 'narrow')
- tokens_grad: bfloat16 [16384, 2048], P('wide', 'narrow')
- norm1_gain_grad: float32 [2048], P('narrow')
- in_weight_grad: float32 [2048, 3, 2048], P('wide', None, 'narrow')
- conv_weight_grad: float32 [3, 2048], P(None, 'narrow')
- out_weight_grad: float32 [2048, 2048], P('narrow', 'wide')
- norm2_gain_grad: float32 [2048], P('narrow')
- gate_weight_grad: float32 [2048, 8192], P('wide', 'narrow')
- up_weight_grad: float32 [2048, 8192], P('wide', 'narrow')
- down_weight_grad: float32 [8192, 2048], P('narrow', 'wide')
Inputs may be any that keep to these rules, and one draw needn't show every extreme that they name: `segment_ids`: along the tokens the segment ids never fall; each segment holds 1 to 2000 tokens, and one holds exactly 2000.
All inputs are finite; a program needn't handle non-finite values.
Results may differ from a plain program's by a relative error of at most 0.008.
Values may be sent and summed in bfloat16 or wider, within the bound.
A program may use at most 384 MiB of HBM per device.

v0:
```python
import jax
import jax.numpy as jnp
from jax import lax
from jax.sharding import PartitionSpec as P

CONV = 3


EPSILON = 1e-05


def matmul(left, right):
    return jnp.dot(left, right, preferred_element_type=jnp.float32)


def contract_rows(left, right):
    return lax.dot_general(
        left, right, (((0,), (0,)), ((), ())), preferred_element_type=jnp.float32
    )


def contract_cols(left, right):
    return lax.dot_general(
        left, right, (((1,), (1,)), ((), ())), preferred_element_type=jnp.float32
    )


def lagged(values, shift_by):
    head = jnp.zeros((shift_by,) + values.shape[1:], values.dtype)
    return jnp.concatenate([head, values[: values.shape[0] - shift_by]], axis=0)


def leading(values, shift_by):
    tail = jnp.zeros((shift_by,) + values.shape[1:], values.dtype)
    return jnp.concatenate([values[shift_by:], tail], axis=0)


def full_rows(piece_in):
    return lax.all_gather(piece_in, "narrow", axis=1, tiled=True)


def narrow_sums(terms):
    return lax.psum_scatter(terms, "narrow", scatter_dimension=1, tiled=True)


def row_stats(values):
    return lax.psum(values, "narrow")


def per_device(
    tokens,
    segment_ids,
    norm1_gain,
    in_weight,
    conv_weight,
    out_weight,
    norm2_gain,
    gate_weight,
    up_weight,
    down_weight,
    cotangent,
):
    full_width = norm1_gain.shape[0]
    part_width = tokens.shape[1]
    row_count = tokens.shape[0]
    offset = lax.axis_index("narrow") * part_width
    gain_one = lax.dynamic_slice_in_dim(norm1_gain, offset, part_width)
    gain_two = lax.dynamic_slice_in_dim(norm2_gain, offset, part_width)
    kernel = lax.dynamic_slice_in_dim(conv_weight, offset, part_width, 1)
    in_all, gate_all, up_all = (
        lax.all_gather(in_weight, "wide", axis=0, tiled=True),
        lax.all_gather(gate_weight, "wide", axis=0, tiled=True),
        lax.all_gather(up_weight, "wide", axis=0, tiled=True),
    )
    out_all, down_all = (
        lax.all_gather(out_weight, "wide", axis=1, tiled=True),
        lax.all_gather(down_weight, "wide", axis=1, tiled=True),
    )
    x_full = full_rows(tokens).astype(jnp.float32)
    x_part = tokens.astype(jnp.float32)
    scale_one = lax.rsqrt(jnp.mean(x_full * x_full, axis=1, keepdims=True) + EPSILON)
    normed_one = (x_full * scale_one * norm1_gain).astype(jnp.bfloat16)
    mixed_proj = matmul(normed_one, in_all.reshape(full_width, 3 * part_width)).reshape(
        row_count, 3, part_width
    )
    gate_b = mixed_proj[:, 0]
    gate_c = mixed_proj[:, 1]
    values_x = mixed_proj[:, 2]
    gated_in = gate_b * values_x
    positions = lax.broadcasted_iota(jnp.int32, (row_count,), 0)
    masks = []
    filtered = jnp.zeros_like(gated_in)
    for lag_step in range(CONV):
        keep_mask = (
            (positions >= lag_step) & (segment_ids == lagged(segment_ids, lag_step))
        ).astype(jnp.float32)[:, None]
        masks.append(keep_mask)
        filtered = filtered + kernel[lag_step] * keep_mask * lagged(gated_in, lag_step)
    mixer_low = (gate_c * filtered).astype(jnp.bfloat16)
    mixer_terms = matmul(mixer_low, out_all)
    branch_part = narrow_sums(mixer_terms)
    hidden_part = x_part + branch_part
    square_sum = row_stats(jnp.sum(hidden_part * hidden_part, axis=1, keepdims=True))
    scale_two = lax.rsqrt(square_sum / full_width + EPSILON)
    normed_two = full_rows((hidden_part * scale_two * gain_two).astype(jnp.bfloat16))
    gate_pre = matmul(normed_two, gate_all)
    up_pre = matmul(normed_two, up_all)
    sigmoid_gate = jax.nn.sigmoid(gate_pre)
    active = gate_pre * sigmoid_gate
    hidden_low = (active * up_pre).astype(jnp.bfloat16)
    ffn_part = narrow_sums(matmul(hidden_low, down_all))
    block_out = (hidden_part + ffn_part).astype(jnp.bfloat16)
    in_all, gate_all, up_all = (
        lax.all_gather(in_weight, "wide", axis=0, tiled=True),
        lax.all_gather(gate_weight, "wide", axis=0, tiled=True),
        lax.all_gather(up_weight, "wide", axis=0, tiled=True),
    )
    out_all, down_all = (
        lax.all_gather(out_weight, "wide", axis=1, tiled=True),
        lax.all_gather(down_weight, "wide", axis=1, tiled=True),
    )
    grad_full = full_rows(cotangent)
    d_hidden = contract_cols(grad_full, down_all)
    down_grad = contract_rows(hidden_low, grad_full)
    d_active = d_hidden * up_pre
    d_up = (d_hidden * active).astype(jnp.bfloat16)
    d_gate = (d_active * sigmoid_gate * (1.0 + gate_pre * (1.0 - sigmoid_gate))).astype(
        jnp.bfloat16
    )
    gate_grad = contract_rows(normed_two, d_gate)
    up_grad = contract_rows(normed_two, d_up)
    d_normed_terms = contract_cols(d_gate, gate_all) + contract_cols(d_up, up_all)
    d_normed_part = narrow_sums(d_normed_terms)
    scaled_two = d_normed_part * gain_two
    inner_two = row_stats(jnp.sum(scaled_two * hidden_part, axis=1, keepdims=True)) / full_width
    d_hidden_part = cotangent.astype(jnp.float32) + scale_two * (
        scaled_two - hidden_part * scale_two * scale_two * inner_two
    )
    d_hidden_low = full_rows(d_hidden_part.astype(jnp.bfloat16))
    gain_two_grad = jnp.sum(d_normed_part * hidden_part * scale_two, axis=0)
    out_grad = contract_rows(mixer_low, d_hidden_low)
    d_mixer = contract_cols(d_hidden_low, out_all)
    d_gate_c = d_mixer * filtered
    d_filtered = d_mixer * gate_c
    d_gated = jnp.zeros_like(d_filtered)
    kernel_rows = []
    for lag_step in range(CONV):
        masked = d_filtered * masks[lag_step]
        d_gated = d_gated + kernel[lag_step] * leading(masked, lag_step)
        kernel_rows.append(jnp.sum(masked * lagged(gated_in, lag_step), axis=0))
    kernel_grad = jnp.stack(kernel_rows, axis=0)
    d_mixed = jnp.stack([d_gated * values_x, d_gate_c, d_gated * gate_b], axis=1).astype(
        jnp.bfloat16
    )
    d_flat = d_mixed.reshape(row_count, 3 * part_width)
    in_grad = contract_rows(normed_one, d_flat).reshape(full_width, 3, part_width)
    d_normed_one = narrow_sums(contract_cols(d_flat, in_all.reshape(full_width, 3 * part_width)))
    scaled_one = d_normed_one * gain_one
    inner_one = row_stats(jnp.sum(scaled_one * x_part, axis=1, keepdims=True)) / full_width
    tokens_grad = (
        d_hidden_part + scale_one * (scaled_one - x_part * scale_one * scale_one * inner_one)
    ).astype(jnp.bfloat16)
    gain_one_grad = jnp.sum(d_normed_one * x_part * scale_one, axis=0)
    in_grad, gate_grad, up_grad = (
        lax.psum_scatter(in_grad, "wide", scatter_dimension=0, tiled=True),
        lax.psum_scatter(gate_grad, "wide", scatter_dimension=0, tiled=True),
        lax.psum_scatter(up_grad, "wide", scatter_dimension=0, tiled=True),
    )
    out_grad, down_grad = (
        lax.psum_scatter(out_grad, "wide", scatter_dimension=1, tiled=True),
        lax.psum_scatter(down_grad, "wide", scatter_dimension=1, tiled=True),
    )
    gain_one_grad, gain_two_grad, kernel_grad = lax.psum(
        (gain_one_grad, gain_two_grad, kernel_grad), "wide"
    )
    return (
        block_out,
        tokens_grad,
        gain_one_grad,
        in_grad,
        kernel_grad,
        out_grad,
        gain_two_grad,
        gate_grad,
        up_grad,
        down_grad,
    )


def solution(mesh):
    in_specs = (
        P("wide", "narrow"),
        P("wide"),
        P(),
        P("wide", None, "narrow"),
        P(),
        P("narrow", "wide"),
        P(),
        P("wide", "narrow"),
        P("wide", "narrow"),
        P("narrow", "wide"),
        P("wide", "narrow"),
    )
    out_specs = (
        P("wide", "narrow"),
        P("wide", "narrow"),
        P("narrow"),
        P("wide", None, "narrow"),
        P(None, "narrow"),
        P("narrow", "wide"),
        P("narrow"),
        P("wide", "narrow"),
        P("wide", "narrow"),
        P("narrow", "wide"),
    )
    return jax.shard_map(
        per_device, mesh=mesh, in_specs=in_specs, out_specs=out_specs, check_vma=False
    )
```

profile of v0, /device:TPU:0, one launch (start us, length us, event | category | flops | bytes accessed | tf_op | source)
XLA Modules:
  0.0 2191.3 jit_solution(4574187801180246266)
XLA Ops:
  11.3 65.8 %all-gather.12.cloned.1.call-done = bf16[2048,3,512]{2,0,1:T(8,128)(2,1)} async-done(((bf16[256,3,512]{2,0,1:T(8,128)(2,1)}), bf16[2048,3,512]{2,0,1:T(8,128)(2,1)}) %all-gather.12.cloned.1.call-update) | async-done | bytes 6291472 | tf_op jit(solution)/shard_map/all_gather | solution.py:71
  77.1 9.0 copy.23
  86.0 79.0 %all-gather.10.cloned.1.call-done = bf16[2048,2048]{1,0:T(8,128)(2,1)} async-done(((bf16[2048,512]{1,0:T(8,128)(2,1)}), bf16[2048,2048]{1,0:T(8,128)(2,1)}) %all-gather.10.cloned.1.call-update) | async-done | bytes 8388624 | tf_op jit(solution)/shard_map/all_gather | solution.py:39
  165.1 5.2 fusion
  170.9 15.6 fusion.7
  187.7 3.3 copy-done.2
  192.5 5.1 multiply_convert_fusion.4
  197.6 10.5 fusion.28
  210.0 152.2 %reduce-scatter.10.cloned.1.call-done = f32[2048,512]{1,0:T(8,128)} async-done(((f32[2048,2048]{1,0:T(8,128)}), f32[2048,512]{1,0:T(8,128)}) %reduce-scatter.10.cloned.1.call-update) | async-done | bytes 4194320 | tf_op jit(solution)/shard_map/reduce_scatter | solution.py:43
  362.2 4.8 multiply_reduce_fusion.5
  366.9 9.0 psum.42
  376.6 3.9 multiply_convert_fusion.3
  382.8 62.9 %all-gather.18.cloned.1.call-done = bf16[2048,2048]{1,0:T(8,128)(2,1)} async-done(((bf16[256,2048]{1,0:T(8,128)(2,1)}), bf16[2048,2048]{1,0:T(8,128)(2,1)}) %all-gather.18.cloned.1.call-update) | async-done | bytes 8388624 | tf_op jit(solution)/shard_map/all_gather | solution.py:72
  445.7 88.3 %all-gather.16.cloned.1.call-done = bf16[2048,2048]{1,0:T(8,128)(2,1)} async-done(((bf16[2048,512]{1,0:T(8,128)(2,1)}), bf16[2048,2048]{1,0:T(8,128)(2,1)}) %all-gather.16.cloned.1.call-update) | async-done | bytes 8388624 | tf_op jit(solution)/shard_map/all_gather | solution.py:39
  534.0 24.2 %fusion.29 = f32[2048,2048]{1,0:T(8,128)} fusion(bf16[2048,2048]{1,0:T(8,128)(2,1)} %all-gather.16.cloned.1.call-done, bf16[2048,2048]{1,0:T(8,128)(2,1)} %all-gather.18.cloned.1.call-done), kind=kOutput, calls=%fused_computation.69 | convolution fusion | flops 17179869184 | bytes 33554432 | tf_op jit(solution)/shard_map/dot_general | solution.py:13
  558.1 59.5 %all-gather.20.cloned.1.call-done = bf16[2048,2048]{1,0:T(8,128)(2,1)} async-done(((bf16[256,2048]{1,0:T(8,128)(2,1)}), bf16[2048,2048]{1,0:T(8,128)(2,1)}) %all-gather.20.cloned.1.call-update) | async-done | bytes 8388624 | tf_op jit(solution)/shard_map/all_gather | solution.py:73
  617.7 24.2 %fusion.30 = f32[2048,2048]{1,0:T(8,128)} fusion(bf16[2048,2048]{1,0:T(8,128)(2,1)} %all-gather.16.cloned.1.call-done, bf16[2048,2048]{1,0:T(8,128)(2,1)} %all-gather.20.cloned.1.call-done), kind=kOutput, calls=%fused_computation.70 | convolution fusion | flops 17179869184 | bytes 33554432 | tf_op jit(solution)/shard_map/dot_general | solution.py:13
  641.8 63.7 %all-gather.24.cloned.1.call-done = bf16[2048,2048]{1,0:T(8,128)(2,1)} async-done(((bf16[2048,512]{1,0:T(8,128)(2,1)}), bf16[2048,2048]{1,0:T(8,128)(2,1)}) %all-gather.24.cloned.1.call-update) | async-done | bytes 8388624 | tf_op jit(solution)/shard_map/all_gather | solution.py:39
  705.5 84.1 %all-gather.22.cloned.1.call-done = bf16[2048,2048]{1,0:T(8,128)(2,1)} async-done(((bf16[2048,256]{1,0:T(8,128)(2,1)}), bf16[2048,2048]{1,0:T(8,128)(2,1)}) %all-gather.22.cloned.1.call-update) | async-done | bytes 8388624 | tf_op jit(solution)/shard_map/all_gather | solution.py:77
  789.7 36.6 %multiply_convert_fusion = (bf16[2048,2048]{1,0:T(8,128)(2,1)}, bf16[2048,2048]{1,0:T(8,128)(2,1)}, bf16[2048,2048]{1,0:T(8,128)(2,1)}) fusion(f32[2048,2048]{1,0:T(8,128)} %fusion.29, f32[2048,2048]{1,0:T(8,128)} %fusion.30, bf16[2048,2048]{1,0:T(8,128)(2,1)} %all-gather.24.cloned.1.call-done, bf16[2048,2048]{1,0:T(8,128)(2,1)} %all-gather.22.cloned.1.call-done), kind=kOutput, calls=%fused_computation.5 | convolution fusion | flops 17242783744 | bytes 75497472 | tf_op jit(solution)/shard_map/dot_general | solution.py:23
  826.3 24.3 %fusion.32 = f32[2048,2048]{1,0:T(8,128)} fusion(bf16[2048,2048]{1,0:T(8,128)(2,1)} %get-tuple-element.30, bf16[2048,2048]{1,0:T(8,128)(2,1)} %all-gather.18.cloned.1.call-done), kind=kOutput, calls=%fused_computation.72 | convolution fusion | flops 17179869184 | bytes 33554432 | tf_op jit(solution)/shard_map/dot_general | solution.py:23
  850.6 26.5 %convolution_add_fusion = f32[2048,2048]{1,0:T(8,128)} fusion(f32[2048,2048]{1,0:T(8,128)} %fusion.32, bf16[2048,2048]{1,0:T(8,128)(2,1)} %get-tuple-element.29, bf16[2048,2048]{1,0:T(8,128)(2,1)} %all-gather.20.cloned.1.call-done), kind=kOutput, calls=%fused_computation.11 | convolution fusion | flops 17184063488 | bytes 50331648 | tf_op jit(solution)/shard_map/dot_general | solution.py:23
  877.2 152.1 %reduce-scatter.14.cloned.1.call-done = f32[2048,512]{1,0:T(8,128)} async-done(((f32[2048,2048]{1,0:T(8,128)}), f32[2048,512]{1,0:T(8,128)}) %reduce-scatter.14.cloned.1.call-update) | async-done | bytes 4194320 | tf_op jit(solution)/shard_map/reduce_scatter | solution.py:43
  1029.3 4.6 multiply_reduce_fusion
  1033.9 9.1 psum.43
  1043.6 5.1 fusion.26
  1048.8 87.4 %all-gather.26.cloned.1.call-done = bf16[2048,2048]{1,0:T(8,128)(2,1)} async-done(((bf16[2048,512]{1,0:T(8,128)(2,1)}), bf16[2048,2048]{1,0:T(8,128)(2,1)}) %all-gather.26.cloned.1.call-update) | async-done | bytes 8388624 | tf_op jit(solution)/shard_map/all_gather | solution.py:39
  1136.2 13.8 multiply_reduce_fusion.3
  1150.1 4.3 multiply_reduce_fusion.2
  1162.4 2.0 multiply_bitcast_fusion.1
  1164.6 17.0 convolution_bitcast_fusion
  1181.7 24.4 %fusion.31 = f32[2048,2048]{1,0:T(8,128)} fusion(bf16[2048,2048]{1,0:T(8,128)(2,1)} %get-tuple-element.31, bf16[2048,2048]{1,0:T(8,128)(2,1)} %all-gather.22.cloned.1.call-done), kind=kOutput, calls=%fused_computation.71 | convolution fusion | flops 17179869184 | bytes 33554432 | tf_op jit(solution)/shard_map/dot_general | solution.py:13
  1206.2 24.6 %fusion.34 = f32[2048,2048]{1,0:T(8,128)} fusion(bf16[2048,2048]{1,0:T(8,128)(2,1)} %all-gather.16.cloned.1.call-done, bf16[2048,2048]{1,0:T(8,128)(2,1)} %get-tuple-element.30), kind=kOutput, calls=%fused_computation.74 | convolution fusion | flops 17179869184 | bytes 33554432 | tf_op jit(solution)/shard_map/dot_general | solution.py:17
  1230.8 24.9 %fusion.35 = f32[2048,2048]{1,0:T(8,128)} fusion(bf16[2048,2048]{1,0:T(8,128)(2,1)} %all-gather.16.cloned.1.call-done, bf16[2048,2048]{1,0:T(8,128)(2,1)} %get-tuple-element.29), kind=kOutput, calls=%fused_computation.75 | convolution fusion | flops 17179869184 | bytes 33554432 | tf_op jit(solution)/shard_map/dot_general | solution.py:17
  1255.8 24.9 %fusion.36 = f32[2048,2048]{1,0:T(8,128)} fusion(bf16[2048,2048]{1,0:T(8,128)(2,1)} %get-tuple-element.31, bf16[2048,2048]{1,0:T(8,128)(2,1)} %all-gather.24.cloned.1.call-done), kind=kOutput, calls=%fused_computation.76 | convolution fusion | flops 17179869184 | bytes 33554432 | tf_op jit(solution)/shard_map/dot_general | solution.py:17
  1280.7 10.6 fusion.33
  1292.0 21.0 fusion.5
  1313.8 21.9 reduce-scatter.16.cloned.1.call-done
  1335.6 3.3 fusion.19
  1338.9 28.5 %all-reduce.5 = (f32[512]{0:T(512)}, f32[3,512]{1,0:T(4,128)}, f32[512]{0:T(512)}) all-reduce(f32[512]{0:T(512)S(1)} %get-tuple-element.12, f32[3,512]{1,0:T(4,128)S(1)} %pad_maximum_fusion, f32[512]{0:T(512)S(1)} %copy-done.33), channel_id=1, replica_groups=mesh['wide'=8,'narrow'=4] {'wide'}, use_global_device_ids=true, to_apply=%region_12.0 | all-reduce | flops 2560 | bytes 20480 | tf_op jit(solution)/shard_map/psum | solution.py:173
  1367.4 9.5 psum.44
  1376.9 116.0 %reduce-scatter.12.cloned.1.call-done = f32[2048,512]{1,0:T(8,128)} async-done(((f32[2048,2048]{1,0:T(8,128)}), f32[2048,512]{1,0:T(8,128)}) %reduce-scatter.12.cloned.1.call-update) | async-done | bytes 4194320 | tf_op jit(solution)/shard_map/reduce_scatter | solution.py:43
  1492.9 9.9 fusion.16
  1502.8 161.2 %reduce-scatter.22.cloned.1.call-done = f32[256,2048]{1,0:T(8,128)} async-done(((f32[2048,2048]{1,0:T(8,128)}), f32[256,2048]{1,0:T(8,128)}) %reduce-scatter.22.cloned.1.call-update) | async-done | bytes 2097168 | tf_op jit(solution)/shard_map/reduce_scatter | solution.py:166
  1664.0 169.4 %reduce-scatter.24.cloned.1.call-done = f32[256,2048]{1,0:T(8,128)} async-done(((f32[2048,2048]{1,0:T(8,128)}), f32[256,2048]{1,0:T(8,128)}) %reduce-scatter.24.cloned.1.call-update) | async-done | bytes 2097168 | tf_op jit(solution)/shard_map/reduce_scatter | solution.py:167
  1833.4 169.4 %reduce-scatter.26.cloned.1.call-done = f32[2048,256]{1,0:T(8,128)} async-done(((f32[2048,2048]{1,0:T(8,128)}), f32[2048,256]{1,0:T(8,128)}) %reduce-scatter.26.cloned.1.call-update) | async-done | bytes 2097168 | tf_op jit(solution)/shard_map/reduce_scatter | solution.py:171
  2002.8 51.1 %reduce-scatter.20.cloned.1.call-done = f32[512,256]{1,0:T(8,128)} async-done(((f32[512,2048]{1,0:T(8,128)}), f32[512,256]{1,0:T(8,128)}) %reduce-scatter.20.cloned.1.call-update) | async-done | bytes 524304 | tf_op jit(solution)/shard_map/reduce_scatter | solution.py:170
  2053.9 130.1 %reduce-scatter.18.cloned.1.call-done = f32[256,3,512]{2,0,1:T(8,128)} async-done(((f32[2048,3,512]{2,0,1:T(8,128)}), f32[256,3,512]{2,0,1:T(8,128)}) %reduce-scatter.18.cloned.1.call-update) | async-done | bytes 1572880 | tf_op jit(solution)/shard_map/reduce_scatter | solution.py:165
  (136 shorter events, 22.4 us)
Async XLA Ops:
  7.2 69.9 %all-gather.12.cloned.1.call-start = ((), (), s32[]{:S(2)}) async-start(), calls=%async_computation.10 | async-start | bytes 7077888 | tf_op jit(solution)/shard_map/all_gather | solution.py:71
  7.9 157.2 %all-gather.10.cloned.1.call-start = ((), (), s32[]{:S(2)}) async-start(), calls=%async_computation.9 | async-start | bytes 10485760 | tf_op jit(solution)/shard_map/all_gather | solution.py:39
  8.7 188.9 %all-gather.14.cloned.1.call-start = ((), (), s32[]{:S(2)}) async-start(), calls=%async_computation.11 | async-start | bytes 2359296 | tf_op jit(solution)/shard_map/all_gather | solution.py:76
  9.4 352.8 %reduce-scatter.10.cloned.1.call-start = ((), (), s32[]{:S(2)}) async-start(), calls=%async_computation.12 | async-start | bytes 20971520 | tf_op jit(solution)/shard_map/reduce_scatter | solution.py:43
  10.3 177.4 %copy-start.14 = (f32[2048]{0:T(1024)}, f32[2048]{0:T(1024)S(1)}, u32[]{:S(2)}) copy-start(f32[2048]{0:T(1024)S(1)} %get-tuple-element.39) | copy-start | bytes 24580
  10.3 177.4 %copy-start.16 = (f32[2048]{0:T(1024)}, f32[2048]{0:T(1024)S(1)}, u32[]{:S(2)}) copy-start(f32[2048]{0:T(1024)S(1)} %get-tuple-element.40) | copy-start | bytes 24580
  11.2 176.5 %copy-start.25 = (f32[1,512]{1,0:T(1,128)}, f32[1,512]{1,0:T(1,128)S(1)}, u32[]{:S(2)}) copy-start(f32[1,512]{1,0:T(1,128)S(1)} %get-tuple-element.36) | copy-start | bytes 6148
  11.2 176.5 %copy-start.27 = (f32[1,512]{1,0:T(1,128)}, f32[1,512]{1,0:T(1,128)S(1)}, u32[]{:S(2)}) copy-start(f32[1,512]{1,0:T(1,128)S(1)} %get-tuple-element.37) | copy-start | bytes 6148
  11.3 176.5 %copy-start.29 = (f32[1,512]{1,0:T(1,128)}, f32[1,512]{1,0:T(1,128)S(1)}, u32[]{:S(2)}) copy-start(f32[1,512]{1,0:T(1,128)S(1)} %get-tuple-element.38) | copy-start | bytes 6148
  86.0 84.9 %copy-start.35 = (f32[2048]{0:T(1024)S(1)}, f32[2048]{0:T(1024)}, u32[]{:S(2)}) copy-start(f32[2048]{0:T(1024)} %param.13) | copy-start | bytes 24580
  165.1 5.9 copy-start.7
  186.6 4.5 copy-start.2
  187.7 4.8 copy-start
  197.6 10.5 copy-start.10
  208.1 154.1 %copy-start.3 = (bf16[2048,512]{1,0:T(8,128)(2,1)S(1)}, bf16[2048,512]{1,0:T(8,128)(2,1)}, u32[]{:S(2)}) copy-start(bf16[2048,512]{1,0:T(8,128)(2,1)} %param.11) | copy-start | bytes 6291460
  208.1 237.5 %all-gather.18.cloned.1.call-start = ((), (), s32[]{:S(2)}) async-start(), calls=%async_computation.14 | async-start | bytes 9437184 | tf_op jit(solution)/shard_map/all_gather | solution.py:72
  208.7 325.2 %all-gather.16.cloned.1.call-start = ((), (), s32[]{:S(2)}) async-start(), calls=%async_computation.13 | async-start | bytes 10485760 | tf_op jit(solution)/shard_map/all_gather | solution.py:39
  210.0 166.0 %copy-start.22 = (f32[512]{0:T(512)}, f32[512]{0:T(512)S(1)}, u32[]{:S(2)}) copy-start(f32[512]{0:T(512)S(1)} %dynamic_slice.10) | copy-start | bytes 6148
  380.5 237.2 %all-gather.20.cloned.1.call-start = ((), (), s32[]{:S(2)}) async-start(), calls=%async_computation.15 | async-start | bytes 9437184 | tf_op jit(solution)/shard_map/all_gather | solution.py:73
  381.3 324.3 %all-gather.24.cloned.1.call-start = ((), (), s32[]{:S(2)}) async-start(), calls=%async_computation.18 | async-start | bytes 10485760 | tf_op jit(solution)/shard_map/all_gather | solution.py:39
  382.0 407.6 %all-gather.22.cloned.1.call-start = ((), (), s32[]{:S(2)}) async-start(), calls=%async_computation.16 | async-start | bytes 9437184 | tf_op jit(solution)/shard_map/all_gather | solution.py:77
  382.7 646.5 %reduce-scatter.14.cloned.1.call-start = ((), (), s32[]{:S(2)}) async-start(), calls=%async_computation.19 | async-start | bytes 20971520 | tf_op jit(solution)/shard_map/reduce_scatter | solution.py:43
  877.1 152.1 %copy-start.12 = (f32[2048,1]{0,1:T(1,128)S(1)}, f32[2048,1]{0,1:T(1,128)}, u32[]{:S(2)}) copy-start(f32[2048,1]{0,1:T(1,128)} %copy-done.11) | copy-start | bytes 24580
  877.1 152.1 %copy-start.23 = (f32[512]{0:T(512)S(1)}, f32[512]{0:T(512)}, u32[]{:S(2)}) copy-start(f32[512]{0:T(512)} %copy-done.22) | copy-start | bytes 6148
  877.2 166.5 %copy-start.5 = (bf16[2048,512]{1,0:T(8,128)(2,1)S(1)}, bf16[2048,512]{1,0:T(8,128)(2,1)}, u32[]{:S(2)}) copy-start(bf16[2048,512]{1,0:T(8,128)(2,1)} %param.21) | copy-start | bytes 6291460
  877.2 259.1 %all-gather.26.cloned.1.call-start = ((), (), s32[]{:S(2)}) async-start(), calls=%async_computation.20 | async-start | bytes 10485760 | tf_op jit(solution)/shard_map/all_gather | solution.py:39
  1048.7 101.3 %copy-start.15 = (f32[2048]{0:T(1024)S(1)}, f32[2048]{0:T(1024)}, u32[]{:S(2)}) copy-start(f32[2048]{0:T(1024)} %copy-done.14) | copy-start | bytes 24580
  1048.7 101.3 %copy-start.17 = (f32[2048]{0:T(1024)S(1)}, f32[2048]{0:T(1024)}, u32[]{:S(2)}) copy-start(f32[2048]{0:T(1024)} %copy-done.16) | copy-start | bytes 24580
  1048.7 286.9 %reduce-scatter.16.cloned.1.call-start = ((), (), s32[]{:S(2)}) async-start(), calls=%async_computation.21 | async-start | bytes 20971520 | tf_op jit(solution)/shard_map/reduce_scatter | solution.py:43
  1136.2 13.8 copy-start.1
  1150.0 6.7 slice-start
  1150.0 6.7 slice-start.1
  1158.2 2.7 copy-start.6
  1158.2 4.2 copy-start.8
  1158.2 6.2 slice-start.3
  1159.2 5.1 copy-start.9
  1159.2 5.4 slice-start.4
  1181.7 311.3 %reduce-scatter.12.cloned.1.call-start = ((), (), s32[]{:S(2)}) async-start(), calls=%async_computation.17 | async-start | bytes 20971520 | tf_op jit(solution)/shard_map/reduce_scatter | solution.py:43
  1206.1 457.9 %reduce-scatter.22.cloned.1.call-start = ((), (), s32[]{:S(2)}) async-start(), calls=%async_computation.24 | async-start | bytes 18874368 | tf_op jit(solution)/shard_map/reduce_scatter | solution.py:166
  1230.8 602.6 %reduce-scatter.24.cloned.1.call-start = ((), (), s32[]{:S(2)}) async-start(), calls=%async_computation.25 | async-start | bytes 18874368 | tf_op jit(solution)/shard_map/reduce_scatter | solution.py:167
  1255.8 747.0 %reduce-scatter.26.cloned.1.call-start = ((), (), s32[]{:S(2)}) async-start(), calls=%async_computation.26 | async-start | bytes 18874368 | tf_op jit(solution)/shard_map/reduce_scatter | solution.py:171
  1280.7 773.2 %reduce-scatter.20.cloned.1.call-start = ((), (), s32[]{:S(2)}) async-start(), calls=%async_computation.23 | async-start | bytes 4718592 | tf_op jit(solution)/shard_map/reduce_scatter | solution.py:170
  1291.3 892.7 %reduce-scatter.18.cloned.1.call-start = ((), (), s32[]{:S(2)}) async-start(), calls=%async_computation.22 | async-start | bytes 14155776 | tf_op jit(solution)/shard_map/reduce_scatter | solution.py:165
  1313.0 22.6 %copy-start.4 = (bf16[2048,512]{1,0:T(8,128)(2,1)S(1)}, bf16[2048,512]{1,0:T(8,128)(2,1)}, u32[]{:S(2)}) copy-start(bf16[2048,512]{1,0:T(8,128)(2,1)} %param.11) | copy-start | bytes 6291460
  1313.1 25.8 %copy-start.33 = (f32[512]{0:T(512)S(1)}, f32[512]{0:T(512)}, u32[]{:S(2)}) copy-start(f32[512]{0:T(512)} %get-tuple-element.10) | copy-start | bytes 6148
  1313.1 179.9 %copy-start.13 = (f32[2048,1]{0,1:T(1,128)S(1)}, f32[2048,1]{0,1:T(1,128)}, u32[]{:S(2)}) copy-start(f32[2048,1]{0,1:T(1,128)} %copy-done.11) | copy-start | bytes 24580
  1313.1 179.8 %copy-start.21 = (f32[2048,1]{0,1:T(1,128)S(1)}, f32[2048,1]{0,1:T(1,128)}, u32[]{:S(2)}) copy-start(f32[2048,1]{0,1:T(1,128)} %copy-done.20) | copy-start | bytes 24580
  1313.1 179.8 %copy-start.24 = (f32[512]{0:T(512)S(1)}, f32[512]{0:T(512)}, u32[]{:S(2)}) copy-start(f32[512]{0:T(512)} %copy-done.22) | copy-start | bytes 6148
  (12 other events, 11.3 us)
Sparse Core Ops, SparseCore 0:
  9.6 67.4 all-gather.11
  78.9 86.1 all-gather.9
  166.7 30.8 all-gather.13
  208.3 153.8 reduce-scatter.9
  363.6 82.0 all-gather.17
  447.9 85.9 all-gather.15
  535.6 82.0 all-gather.19
  619.5 85.9 all-gather.23
  707.1 82.4 all-gather.21
  877.3 151.9 reduce-scatter.13
  1048.8 87.3 all-gather.25
  1181.8 153.7 reduce-scatter.15
  1338.7 154.2 reduce-scatter.11
  1495.7 168.2 reduce-scatter.21
  1666.8 166.5 reduce-scatter.23
  1836.2 166.5 reduce-scatter.25
  2005.5 48.3 reduce-scatter.19
  2056.7 127.3 reduce-scatter.17
where the time goes:
time: 2200 us; the launch traced here: 2190 us
  waiting for transfers between devices  1720 us (78%)
  matrix products  323 us (15%)
  blocking collectives  56.1 us (3%)
  other arithmetic  52.6 us (2%)
  local copies, waits for them, and re-layouts  24.3 us (1%)
    reduce_scatter x4, waiting for transfers between devices, narrow_sums(): return lax.psum_scatter(terms, 'narrow', scatter_dimension=1, tiled=True)  442 us
    all_gather x4, waiting for transfers between devices, full_rows(): return lax.all_gather(piece_in, 'narrow', axis=1, tiled=True)  318 us
    reduce_scatter x1, waiting for transfers between devices, per_device(): lax.psum_scatter(down_grad, 'wide', scatter_dimension=1, tiled=True)  169 us
    reduce_scatter x1, waiting for transfers between devices, per_device(): lax.psum_scatter(up_grad, 'wide', scatter_dimension=0, tiled=True)  169 us
    reduce_scatter x1, waiting for transfers between devices, per_device(): lax.psum_scatter(gate_grad, 'wide', scatter_dimension=0, tiled=True)  161 us
    reduce_scatter x1, waiting for transfers between devices, per_device(): lax.psum_scatter(in_grad, 'wide', scatter_dimension=0, tiled=True)  130 us
    dot_general x5, matrix products, contract_cols(): lax.dot_general(left, right, (((1,), (1,)), ((), ())), preferred_element_...  118 us
    dot_general x5, matrix products, contract_rows(): lax.dot_general(left, right, (((0,), (0,)), ((), ())), preferred_element_...  106 us
  transfers between devices with their start and end apart: 18, of which 17 were waited for; matrix products, arithmetic and copies ran while one was open for 11% of the time, Pallas kernels for 0%

commit v1 on v0

v1 whole, which is shorter than its diff:
```python
import functools

import jax
import jax.numpy as jnp
from jax import lax
from jax.experimental import pallas as pl
from jax.experimental.pallas import tpu as pltpu
from jax.sharding import PartitionSpec as P

CONV = 3
EPSILON = 1e-05
BF = jnp.bfloat16
F32 = jnp.float32
TILE = 256
BIG = 512


def contract_rows(left, right):
    return lax.dot_general(left, right, (((0,), (0,)), ((), ())), preferred_element_type=F32)


def contract_cols(left, right):
    return lax.dot_general(left, right, (((1,), (1,)), ((), ())), preferred_element_type=F32)


def lagged(values, shift_by):
    head = jnp.zeros((shift_by,) + values.shape[1:], values.dtype)
    return jnp.concatenate([head, values[: values.shape[0] - shift_by]], axis=0)


ALONG_X = [(0, 1), (1, 0), (2, 3), (3, 2)]
ALONG_Y = [(0, 2), (2, 0), (1, 3), (3, 1)]


def to_x(values):
    return lax.ppermute(values, "narrow", ALONG_X)


def to_y(values):
    return lax.ppermute(values, "narrow", ALONG_Y)


def halves(values, axis):
    middle = values.shape[axis] // 2
    return lax.slice_in_dim(values, 0, middle, axis=axis), lax.slice_in_dim(values, middle, None, axis=axis)


def gather_pieces(block, axis, square, beside=(lambda: (), lambda _: ())):
    if not square:
        first = beside[0]()
        return [lax.all_gather(block, "narrow", axis=axis, tiled=True)], first, beside[1](first)
    from_x, from_y, first = lax.optimization_barrier((to_x(block), to_y(block), beside[0]()))
    low, high, second = lax.optimization_barrier(
        (to_x(halves(from_y, axis)[0]), to_y(halves(from_x, axis)[1]), beside[1](first))
    )
    return [block, from_x, from_y, low, high], first, second


def piece_starts(me, width, square):
    if not square:
        return [0]
    return [me * width, (me ^ 1) * width, (me ^ 2) * width, (me ^ 3) * width, (me ^ 3) * width + width // 2]


def whole(shape):
    return pl.BlockSpec(shape, lambda *_: (0,) * len(shape), pipeline_mode=pl.Buffered(1))


def tiles(width, tile=TILE):
    return pl.BlockSpec((tile, width), lambda i, *_: (i, 0))


def run(kernel, grid, scalars, operands, in_specs, outs, out_specs, scratch=(), flops=0, aliases=None, vmem=56):
    moved = sum(o.size * o.dtype.itemsize for o in operands) + sum(o.size * o.dtype.itemsize for o in outs)
    return pl.pallas_call(
        kernel,
        grid_spec=pltpu.PrefetchScalarGridSpec(
            num_scalar_prefetch=1, grid=grid, in_specs=in_specs, out_specs=out_specs, scratch_shapes=list(scratch)
        ),
        out_shape=outs,
        input_output_aliases=aliases or {},
        cost_estimate=pl.CostEstimate(flops=flops, bytes_accessed=moved, transcendentals=0),
        compiler_params=pltpu.CompilerParams(
            dimension_semantics=("arbitrary",) * len(grid), vmem_limit_bytes=vmem << 20
        ),
    )(scalars, *operands)


def shape_of(shape, dtype):
    return jax.ShapeDtypeStruct(shape, dtype)


def project(me, pieces, square, gain, weight, kernel, masks):
    count = len(pieces)
    row_count = pieces[0].shape[0]
    full, part = weight.shape[0], kernel.shape[1]
    share = full // (4 if square else 1)
    packed = pl.BlockSpec((full, 3 * part), lambda *_: (0, 0), pipeline_mode=pl.Buffered(1))

    def body(me_ref, *refs):
        xs, (gain_ref, w_ref, k_ref, m_ref), (n_ref, x_ref, p_ref, v_ref, y_ref, s_ref), (carry,) = (
            refs[:count],
            refs[count : count + 4],
            refs[count + 4 : count + 10],
            refs[count + 10 :],
        )

        @pl.when(pl.program_id(0) == 0)
        def _():
            carry[...] = jnp.zeros_like(carry)

        values = [ref[...].astype(F32) for ref in xs]
        total = functools.reduce(jnp.add, [jnp.sum(v * v, axis=1, keepdims=True) for v in values])
        scale = lax.rsqrt(total / full + EPSILON)
        s_ref[...] = scale
        for ref, v, start in zip(xs, values, piece_starts(me_ref[0], share, square)):
            at = pl.ds(pl.multiple_of(start, 128), v.shape[1])
            n_ref[:, at] = (v * scale * gain_ref[:, at]).astype(BF)
            x_ref[:, at] = ref[...]
        mixed = jnp.dot(n_ref[...], w_ref[...], preferred_element_type=F32)
        p_ref[...] = mixed
        gated = mixed[:, :part] * mixed[:, 2 * part :]
        row = lax.broadcasted_iota(jnp.int32, gated.shape, 0)
        before, last = carry[6:7, :], carry[7:8, :]
        back_one = jnp.where(row == 0, last, pltpu.roll(gated, 1, 0))
        back_two = jnp.where(row == 0, before, jnp.where(row == 1, last, pltpu.roll(gated, 2, 0)))
        carry[...] = gated[-8:, :]
        keep = m_ref[...]
        filtered = (
            k_ref[0:1, :] * gated + k_ref[1:2, :] * keep[:, 0:1] * back_one + k_ref[2:3, :] * keep[:, 1:2] * back_two
        )
        v_ref[...] = filtered
        y_ref[...] = (mixed[:, part : 2 * part] * filtered).astype(BF)

    return run(
        body,
        (row_count // TILE,),
        me,
        [*pieces, gain, weight, kernel, masks],
        [tiles(p.shape[1]) for p in pieces] + [whole(gain.shape), packed, whole(kernel.shape), tiles(2)],
        [
            shape_of((row_count, full), BF),
            shape_of((row_count, full), BF),
            shape_of((row_count, 3 * part), F32),
            shape_of((row_count, part), F32),
            shape_of((row_count, part), BF),
            shape_of((row_count, 1), F32),
        ],
        [tiles(full), tiles(full), tiles(3 * part), tiles(part), tiles(part), tiles(1)],
        [pltpu.VMEM((8, part), F32)],
        flops=2 * row_count * full * 3 * part,
    )


def mix(core, pieces, mats, x_full, gain):
    count, parts = len(pieces), len(mats)
    row_count, full = x_full.shape
    cols = mats[0].shape[1]

    def body(core_ref, *refs):
        ys, ms, (x_ref, gain_ref), (h_ref, n_ref, s_ref), (all_ref,) = (
            refs[:count],
            refs[count : count + parts],
            refs[count + parts : count + parts + 2],
            refs[count + parts + 2 : count + parts + 5],
            refs[count + parts + 5 :],
        )
        at = 0
        for ref in ys:
            all_ref[:, at : at + ref.shape[1]] = ref[...]
            at += ref.shape[1]
        total = 0.0
        for k, ref in enumerate(ms):
            where = pl.ds(pl.multiple_of((core_ref[0] ^ k) * cols, 128), cols) if parts > 1 else slice(None)
            h = x_ref[:, where].astype(F32) + jnp.dot(all_ref[...], ref[...], preferred_element_type=F32)
            h_ref[:, where] = h
            total = total + jnp.sum(h * h, axis=1, keepdims=True)
        scale = lax.rsqrt(total / full + EPSILON)
        s_ref[...] = scale
        n_ref[...] = (h_ref[...] * scale * gain_ref[...]).astype(BF)

    return run(
        body,
        (row_count // BIG,),
        core,
        [*pieces, *mats, x_full, gain],
        [tiles(p.shape[1], BIG) for p in pieces] + [whole(m.shape) for m in mats] + [tiles(full, BIG), whole(gain.shape)],
        [shape_of((row_count, full), F32), shape_of((row_count, full), BF), shape_of((row_count, 1), F32)],
        [tiles(full, BIG), tiles(full, BIG), tiles(1, BIG)],
        [pltpu.VMEM((BIG, full), BF)],
        flops=2 * row_count * full * full,
    )


def lay(me, pieces, square):
    if not square:
        return pieces[0]
    row_count, share = pieces[0].shape
    full = 4 * share

    def body(me_ref, *refs):
        for ref, start in zip(refs[:-1], piece_starts(me_ref[0], share, True)):
            refs[-1][:, pl.ds(pl.multiple_of(start, 128), ref.shape[1])] = ref[...]

    return run(
        body,
        (row_count // BIG,),
        me,
        pieces,
        [tiles(p.shape[1], BIG) for p in pieces],
        [shape_of((row_count, full), BF)],
        [tiles(full, BIG)],
    )[0]


def expand(me, normed, weight):
    row_count, full = normed.shape
    units = weight.shape[1] // 2

    def body(_, n_ref, w_ref, q_ref, a_ref, b_ref):
        step = min(512, units)
        for at in range(0, units, step):
            gate = jnp.dot(n_ref[...], w_ref[:, at : at + step], preferred_element_type=F32)
            up = jnp.dot(n_ref[...], w_ref[:, units + at : units + at + step], preferred_element_type=F32)
            sig = 1.0 / (1.0 + jnp.exp(-gate))
            active = gate * sig
            q_ref[:, at : at + step] = (active * up).astype(BF)
            a_ref[:, at : at + step] = active.astype(BF)
            b_ref[:, at : at + step] = (up * sig * (1.0 + gate * (1.0 - sig))).astype(BF)

    return run(
        body,
        (row_count // BIG,),
        me,
        [normed, weight],
        [tiles(full, BIG), whole(weight.shape)],
        [shape_of((row_count, units), BF)] * 3,
        [tiles(units, BIG)] * 3,
        flops=2 * row_count * full * 2 * units,
    )


def ffn_back(owners, band, grad, slope_up, slope_gate, down, weight):
    row_count, full = grad.shape
    units = down.shape[0]
    step = min(512, units)
    count = units // step

    def body(_, g_ref, a_ref, b_ref, d_ref, wg_ref, wu_ref, low_ref, high_ref, o_ref, total):
        j = pl.program_id(1)
        dq = contract_cols(g_ref[...], d_ref[...])
        d_gate = (dq * b_ref[...].astype(F32)).astype(BF)
        d_up = (dq * a_ref[...].astype(F32)).astype(BF)
        at = pl.multiple_of(j * step, 128)
        o_ref[:, pl.ds(at, step)] = d_gate
        o_ref[:, pl.ds(units + at, step)] = d_up
        term = contract_cols(d_gate, wg_ref[...]) + contract_cols(d_up, wu_ref[...])

        @pl.when(j == 0)
        def _():
            total[...] = term

        @pl.when(j > 0)
        def _():
            total[...] += term

        @pl.when(j == count - 1)
        def _():
            low_ref[...] = total[:, : full // 2].astype(BF)
            high_ref[...] = total[:, full // 2 :].astype(BF)

    return run(
        body,
        (row_count // band, count),
        owners,
        [grad, slope_up, slope_gate, down, weight, weight],
        [
            pl.BlockSpec((band, full), lambda i, j, o: (o[i], 0)),
            pl.BlockSpec((band, step), lambda i, j, o: (o[i], j)),
            pl.BlockSpec((band, step), lambda i, j, o: (o[i], j)),
            pl.BlockSpec((step, full), lambda i, j, o: (j, 0)),
            pl.BlockSpec((full, step), lambda i, j, o: (0, j)),
            pl.BlockSpec((full, step), lambda i, j, o: (0, count + j)),
        ],
        [shape_of((row_count, full // 2), BF)] * 2 + [shape_of((row_count, 2 * units), BF)],
        [
            pl.BlockSpec((band, full // 2), lambda i, j, o: (i, 0)),
            pl.BlockSpec((band, full // 2), lambda i, j, o: (i, 0)),
            pl.BlockSpec((band, 2 * units), lambda i, j, o: (o[i], 0)),
        ],
        [pltpu.VMEM((band, full), F32)],
        flops=6 * row_count * full * units,
    )


def hidden_back(me, terms, hidden, scale_two, grad, gain):
    band = terms[0][0].shape[0]
    full = gain.shape[1]
    tile = min(TILE, band)
    count = 2 * len(terms)

    def body(_, *refs):
        h_ref, s_ref, g_ref, gain_ref, o_ref, n_ref = refs[count:]

        @pl.when(pl.program_id(0) == 0)
        def _():
            n_ref[...] = jnp.zeros_like(n_ref)

        sums = [functools.reduce(jnp.add, [r[...].astype(F32) for r in refs[k:count:2]]) for k in (0, 1)]
        d_normed = jnp.concatenate(sums, axis=1)
        h, scale = h_ref[...], s_ref[...]
        scaled = d_normed * gain_ref[...]
        inner = jnp.sum(scaled * h, axis=1, keepdims=True) / full
        o_ref[...] = (g_ref[...].astype(F32) + scale * (scaled - h * scale * scale * inner)).astype(BF)
        n_ref[...] += jnp.sum(d_normed * h * scale, axis=0, keepdims=True)

    def mine(width):
        return pl.BlockSpec((tile, width), lambda i, o: (o[0] * (band // tile) + i, 0))

    flat = [half for pair in terms for half in pair]
    return run(
        body,
        (band // tile,),
        me,
        [*flat, hidden, scale_two, grad, gain],
        [tiles(f.shape[1], tile) for f in flat] + [mine(full), mine(1), mine(full), whole(gain.shape)],
        [shape_of((band, full), BF), shape_of((1, full), F32)],
        [tiles(full, tile), pl.BlockSpec((1, full), lambda i, *_: (0, 0))],
    )


def mixer_back(owners, pieces, out_rows, mixed, filtered, kernel, masks, weight):
    part, full = out_rows.shape
    row_count = mixed.shape[0]
    count = row_count // TILE
    size = owners.shape[0]
    band = row_count // size
    given = len(pieces)
    packed = pl.BlockSpec((full, 3 * part), lambda *_: (0, 0), pipeline_mode=pl.Buffered(1))

    def body(own_ref, *refs):
        w_ref, p_ref, v_ref, k_ref, m_ref, r_ref = refs[given : given + 6]
        outs = refs[given + 6 : given + 6 + 2 * size]
        o_ref, kg_ref, d_ref, carry, dy_ref = refs[given + 6 + 2 * size :]
        i = pl.program_id(0)

        @pl.when(i == 0)
        def _():
            carry[...] = jnp.zeros_like(carry)
            kg_ref[...] = jnp.zeros_like(kg_ref)

        first = (count - 1 - i) * TILE
        if given == 1:
            d_ref[...] = refs[0][pl.ds(pl.multiple_of(first, TILE), TILE), :]
        else:
            apart = (first // band) ^ own_ref[size - 1]
            within = pl.multiple_of(first % band, TILE)
            for k in range(3):

                @pl.when(apart == k)
                def _(k=k):
                    d_ref[...] = refs[k][pl.ds(within, TILE), :]

            @pl.when((apart == 3) & (within < band // 2))
            def _():
                d_ref[...] = refs[3][pl.ds(within, TILE), :]

            @pl.when((apart == 3) & (within >= band // 2))
            def _():
                d_ref[...] = refs[4][pl.ds(pl.multiple_of(within - band // 2, TILE), TILE), :]

        dy_ref[...] = contract_cols(d_ref[...], w_ref[...])
        dy = dy_ref[...]
        b, c, x = p_ref[:, :part], p_ref[:, part : 2 * part], p_ref[:, 2 * part :]
        dv = dy * c
        keep = m_ref[...]
        one, two = dv * keep[:, 0:1], dv * keep[:, 1:2]
        row = lax.broadcasted_iota(jnp.int32, dv.shape, 0)
        end = TILE - 1
        next_one = jnp.where(row == end, carry[0:1, :], pltpu.roll(one, TILE - 1, 0))
        next_two = jnp.where(
            row == end, carry[2:3, :], jnp.where(row == end - 1, carry[1:2, :], pltpu.roll(two, TILE - 2, 0))
        )
        carry[0:1, :] = one[0:1, :]
        carry[1:3, :] = two[0:2, :]
        u = b * x
        kg_ref[0:1, :] += jnp.sum(dv * u, axis=0, keepdims=True)
        kg_ref[1:2, :] += jnp.sum(next_one * u, axis=0, keepdims=True)
        kg_ref[2:3, :] += jnp.sum(next_two * u, axis=0, keepdims=True)
        du = k_ref[0:1, :] * dv + k_ref[1:2, :] * next_one + k_ref[2:3, :] * next_two
        o_ref[:, :part] = (du * x).astype(BF)
        o_ref[:, part : 2 * part] = (dy * v_ref[...]).astype(BF)
        o_ref[:, 2 * part :] = (du * b).astype(BF)
        for k in range(size):
            rows = pl.ds(pl.multiple_of(own_ref[k] * part, part), part)
            term = contract_cols(o_ref[...], r_ref[rows, :])
            outs[2 * k][...] = term[:, : part // 2].astype(BF)
            outs[2 * k + 1][...] = term[:, part // 2 :].astype(BF)

    def back(width):
        return pl.BlockSpec((TILE, width), lambda i, *_: (count - 1 - i, 0))

    return run(
        body,
        (count,),
        owners,
        [*pieces, out_rows, mixed, filtered, kernel, masks, weight],
        [whole(p.shape) for p in pieces]
        + [whole(out_rows.shape), back(3 * part), back(part), whole(kernel.shape), back(2), packed],
        [shape_of((row_count, part // 2), BF)] * (2 * size)
        + [shape_of((row_count, 3 * part), BF), shape_of((CONV, part), F32), shape_of((row_count, full), BF)],
        [back(part // 2)] * (2 * size)
        + [back(3 * part), pl.BlockSpec((CONV, part), lambda i, *_: (0, 0)), back(full)],
        [pltpu.VMEM((8, part), F32), pltpu.VMEM((TILE, part), F32)],
        flops=2 * row_count * full * part * 4,
    )


def front_terms(owners, left, right):
    row_count, depth = left.shape
    size = owners.shape[0]
    width = right.shape[1] // size

    def body(own_ref, l_ref, r_ref, *outs):
        for k in range(size):
            at = pl.ds(pl.multiple_of(own_ref[k] * width, width), width)
            term = jnp.dot(l_ref[...], r_ref[:, at], preferred_element_type=F32)
            outs[2 * k][...] = term[:, : width // 2].astype(BF)
            outs[2 * k + 1][...] = term[:, width // 2 :].astype(BF)

    return run(
        body,
        (row_count // BIG,),
        owners,
        [left, right],
        [tiles(depth, BIG), whole(right.shape)],
        [shape_of((row_count, width // 2), BF)] * (2 * size),
        [tiles(width // 2, BIG)] * (2 * size),
        flops=2 * row_count * depth * width * size,
    )


def add_low(left, right):
    return (left.astype(F32) + right.astype(F32)).astype(BF)


def scatter_first(terms):
    return lax.optimization_barrier((to_x(terms[0][0]), to_y(terms[0][1])))


def scatter_last(terms, via_x, via_y):
    to_send = terms[1][0], add_low(terms[1][1], via_y), add_low(terms[2][0], via_x), terms[2][1]
    x_low, x_high, y_low, y_high = lax.optimization_barrier(
        (to_x(to_send[0]), to_x(to_send[1]), to_y(to_send[2]), to_y(to_send[3]))
    )
    return [terms[3], (x_low, x_high), (y_low, y_high)]


def scatter_plain(terms, axis):
    joined = jnp.concatenate([jnp.concatenate(pair, axis=1) for pair in terms], axis=axis).astype(F32)
    return lax.psum_scatter(joined, "narrow", scatter_dimension=axis, tiled=True)


def total_of(pairs):
    return jnp.concatenate(
        [functools.reduce(jnp.add, [pair[k].astype(F32) for pair in pairs]) for k in (0, 1)], axis=1
    )


def wide_all(block, axis):
    return lax.all_gather(block, "wide", axis=axis, tiled=True)


def wide_sums(terms, axis):
    return lax.psum_scatter(terms.astype(BF), "wide", scatter_dimension=axis, tiled=True).astype(F32)


def narrow_total(values, square):
    if not square:
        return lax.psum(values, "narrow")
    values = values + to_x(values)
    return values + to_y(values)


def wide_total(values, square):
    if not square:
        return lax.psum(values, "wide")
    for bit in (1, 2, 4):
        values = values + lax.ppermute(values, "wide", [(i, i ^ bit) for i in range(lax.axis_size("wide"))])
    return values


def after(value, *others):
    return lax.optimization_barrier((value, *others))[0]


def per_device(
    square,
    size,
    tokens,
    segment_ids,
    norm1_gain,
    in_weight,
    conv_weight,
    out_weight,
    norm2_gain,
    gate_weight,
    up_weight,
    down_weight,
    cotangent,
):
    full_width = norm1_gain.shape[0]
    part_width = tokens.shape[1]
    units = gate_weight.shape[1]
    row_count = tokens.shape[0]
    band = row_count // size
    me = lax.axis_index("narrow")
    core = lax.axis_index("wide") % 2
    me_s = me.reshape(1).astype(jnp.int32)
    core_s = core.reshape(1).astype(jnp.int32)
    offset = me * part_width
    kernel = lax.dynamic_slice_in_dim(conv_weight, offset, part_width, 1)
    gain_one, gain_two = norm1_gain[None, :], norm2_gain[None, :]

    order = [me ^ 3, me ^ 1, me ^ 2, me] if square else list(range(size))
    owners = jnp.stack([jnp.asarray(o, jnp.int32) for o in order])

    pack = jnp.concatenate([in_weight[:, k] for k in range(3)] + list(halves(out_weight, 0)), axis=1)
    slim = pack.shape[0]
    if square:
        pack_all = wide_all(pack, 0)
        out_rows = pack_all[:, 3 * part_width :].reshape(-1, slim, 2, slim)
        out_rows = out_rows.transpose(2, 1, 0, 3).reshape(part_width, full_width)
    else:
        pack_all = wide_all(jnp.concatenate([in_weight[:, k] for k in range(3)], axis=1), 0)
        out_rows = wide_all(out_weight, 1)
    x_pieces, _, _ = gather_pieces(tokens, 1, square)
    both_all = wide_all(after(jnp.concatenate([gate_weight, up_weight], axis=1), *x_pieces), 0)

    positions = lax.broadcasted_iota(jnp.int32, (row_count,), 0)
    masks = jnp.stack(
        [((positions >= k) & (segment_ids == lagged(segment_ids, k))).astype(F32) for k in (1, 2)], axis=1
    )
    normed_one, x_full, mixed, filtered, mixer_low, scale_one = project(
        me_s, x_pieces, square, gain_one, pack_all, kernel, masks
    )
    down_all = wide_all(after(down_weight, mixer_low), 1)

    if square:
        half_cols = full_width // 2
        pairs = [(i, i ^ 1) for i in range(lax.axis_size("wide"))]
        out_half = lax.dynamic_slice_in_dim(out_rows, core * half_cols, half_cols, 1)
        out_half = after(out_half, x_pieces[3])
        mine = jnp.concatenate(gather_pieces(out_half, 0, True)[0], axis=0)
        mats = [mine, lax.ppermute(mine, "wide", pairs)]
    else:
        mats = [lax.all_gather(out_rows, "narrow", axis=0, tiled=True)]
    y_pieces, _, _ = gather_pieces(mixer_low, 1, square)
    g_pieces, (hidden, normed_two, scale_two), (hidden_low, slope_up, slope_gate) = gather_pieces(
        after(cotangent, *y_pieces[1:]),
        1,
        square,
        (
            lambda: tuple(mix(core_s, y_pieces, mats, x_full, gain_two)),
            lambda first: tuple(expand(me_s, first[1], both_all)),
        ),
    )
    grad_full = lay(me_s, g_pieces, square)

    down_terms = contract_rows(hidden_low, grad_full).astype(BF)
    down_grad = wide_sums(down_terms, 1)
    low, high, d_both = ffn_back(owners, band, grad_full, after(slope_up, down_terms), slope_gate, down_all, both_all)
    ffn_terms = [(low[k * band : (k + 1) * band], high[k * band : (k + 1) * band]) for k in range(size)]
    if square:
        via_x, via_y = scatter_first(ffn_terms)
        both_terms = contract_rows(normed_two, d_both).astype(BF)
        via_x, via_y, both_terms = lax.optimization_barrier((via_x, via_y, both_terms))
        sums = scatter_last(ffn_terms, via_x, via_y)
    else:
        both_terms = contract_rows(normed_two, d_both).astype(BF)
        sums = [tuple(halves(scatter_plain(ffn_terms, 0), 1))]
    both_grad = wide_sums(after(both_terms, down_grad), 0)
    d_hidden_rows, gain_two_terms = hidden_back(me_s, sums, hidden, scale_two, grad_full, gain_two)
    dh_pieces, out_parts, _ = gather_pieces(
        d_hidden_rows, 0, square, (lambda: tuple(front_terms(owners, hidden_low, down_all)), lambda _: ())
    )
    *one_parts, d_flat, kernel_grad, d_hidden_low = mixer_back(
        owners, dh_pieces, out_rows, mixed, filtered, kernel, masks, pack_all
    )
    one_parts = list(zip(one_parts[0::2], one_parts[1::2]))
    out_parts = list(zip(out_parts[0::2], out_parts[1::2]))
    if square:
        via_x, via_y = scatter_first(one_parts)
        in_terms = contract_rows(normed_one, d_flat).astype(BF)
        via_x, via_y, in_terms = lax.optimization_barrier((via_x, via_y, in_terms))
        one_sums = scatter_last(one_parts, via_x, via_y)
        out_terms = contract_rows(mixer_low, after(d_hidden_low, in_terms)).astype(BF)
        d_normed_one = total_of(one_sums)
        via_x, via_y = scatter_first([tuple(after(out_parts[0], d_normed_one))] + out_parts[1:])
        ffn_out = total_of(scatter_last(out_parts, via_x, via_y))
        in_grad = wide_sums(after(in_terms, both_grad), 0)
        out_grad = wide_sums(after(out_terms, in_grad, ffn_out), 1)
    else:
        in_terms = contract_rows(normed_one, d_flat).astype(BF)
        out_terms = contract_rows(mixer_low, d_hidden_low).astype(BF)
        d_normed_one = scatter_plain(one_parts, 1)
        ffn_out = scatter_plain(out_parts, 1)
        in_grad, out_grad = wide_sums(in_terms, 0), wide_sums(out_terms, 1)
    gate_grad, up_grad = both_grad[:, :units], both_grad[:, units:]
    in_grad = jnp.stack([in_grad[:, k * part_width : (k + 1) * part_width] for k in range(3)], axis=1)
    block_out = (lax.dynamic_slice_in_dim(hidden, offset, part_width, 1) + ffn_out).astype(BF)

    my_gain = lax.dynamic_slice_in_dim(norm1_gain, offset, part_width)
    x_part = tokens.astype(F32)
    scaled_one = d_normed_one * my_gain
    inner_one = narrow_total(jnp.sum(scaled_one * x_part, axis=1).reshape(-1, 128), square)
    inner_one = inner_one.reshape(row_count, 1) / full_width
    tokens_grad = (
        lax.dynamic_slice_in_dim(d_hidden_low, offset, part_width, 1).astype(F32)
        + scale_one * (scaled_one - x_part * scale_one * scale_one * inner_one)
    ).astype(BF)
    gain_one_grad = jnp.sum(d_normed_one * x_part * scale_one, axis=0)
    gain_two_terms = narrow_total(gain_two_terms.reshape(size, part_width), square)
    gain_two_terms = lax.dynamic_slice_in_dim(gain_two_terms, me, 1, 0)
    small = wide_total(jnp.concatenate([gain_one_grad[None, :], gain_two_terms, kernel_grad], axis=0), square)
    gain_one_grad, gain_two_grad, kernel_grad = small[0], small[1], small[2:]
    return (
        block_out,
        tokens_grad,
        gain_one_grad,
        in_grad,
        kernel_grad,
        out_grad,
        gain_two_grad,
        gate_grad,
        up_grad,
        down_grad,
    )


def solution(mesh):
    size = mesh.shape["narrow"]
    square = size == 4 and mesh.shape["wide"] == 8

    def step(*args):
        return per_device(square, size, *args)

    in_specs = (
        P("wide", "narrow"),
        P("wide"),
        P(),
        P("wide", None, "narrow"),
        P(),
        P("narrow", "wide"),
        P(),
        P("wide", "narrow"),
        P("wide", "narrow"),
        P("narrow", "wide"),
        P("wide", "narrow"),
    )
    out_specs = (
        P("wide", "narrow"),
        P("wide", "narrow"),
        P("narrow"),
        P("wide", None, "narrow"),
        P(None, "narrow"),
        P("narrow", "wide"),
        P("narrow"),
        P("wide", "narrow"),
        P("wide", "narrow"),
        P("narrow", "wide"),
    )
    return jax.shard_map(step, mesh=mesh, in_specs=in_specs, out_specs=out_specs, check_vma=False)
```

time: 2200 us -> 842 us (0.38)
  waiting for transfers between devices: 1720 us -> 351 us
  Pallas kernels: 0 us -> 255 us
  matrix products: 323 us -> 91.7 us
  blocking collectives: 56.1 us -> 0 us
  starting transfers between devices: 1.19 us -> 46.5 us
    reduce_scatter x9 -> x4, waiting for transfers between devices: 1120 us -> 2.53 us  [wide_sums(): lax.psum_scatter(terms.astype(BF), 'wide', scatter_dimension=axis, tiled=...]
    all_gather x9 -> x3, waiting for transfers between devices: 591 us -> 6.75 us  [wide_all(): return lax.all_gather(block, 'wide', axis=axis, tiled=True)]
    ppermute x0 -> x46, waiting for transfers between devices: none -> 342 us  [the longest x21 198 us: to_y(): return lax.ppermute(values, 'narrow', ALONG_Y)]
    pallas_call x0 -> x8, Pallas kernels: none -> 255 us  [run(): pl.pallas_call(kernel, grid_spec=pltpu.PrefetchScalarGridSpec(num_scalar_...]
    dot_general x10 -> x0, matrix products: 217 us -> none  [the longest x5 118 us: contract_cols(): lax.dot_general(left, right, (((1,), (1,)), ((), ())), preferred_element_...]
    psum x4 -> x0, blocking collectives: 56.1 us -> none  [the longest x1 28.5 us: per_device(): lax.psum((gain_one_grad, gain_two_grad, kernel_grad), 'wide')]
    ppermute x0 -> x46, starting transfers between devices: none -> 46.2 us  [the longest x21 23.5 us: to_y(): return lax.ppermute(values, 'narrow', ALONG_Y)]
    dot_general x5 -> x4, matrix products: 106 us -> 91.7 us  [contract_rows(): lax.dot_general(left, right, (((0,), (0,)), ((), ())), preferred_element_...]
  transfers between devices with their start and end apart: 18 -> 53, of which waited for: 17 -> 31; matrix products, arithmetic and copies ran while one was open for 11% -> 18% of each run, Pallas kernels for 0% -> 30%
where the time goes in v1:
time: 842 us; the launch traced here: 836 us
  waiting for transfers between devices  351 us (42%)
  Pallas kernels  255 us (30%)
  matrix products  91.7 us (11%)
  starting transfers between devices  46.5 us (6%)
  other arithmetic  40.3 us (5%)
  local copies, waits for them, and re-layouts  36.4 us (4%)
  between operations  15 us (2%)
    pallas_call x8, Pallas kernels, run(): pl.pallas_call(kernel, grid_spec=pltpu.PrefetchScalarGridSpec(num_scalar_...  255 us
    ppermute x21, waiting for transfers between devices, to_y(): return lax.ppermute(values, 'narrow', ALONG_Y)  198 us
    ppermute x21, waiting for transfers between devices, to_x(): return lax.ppermute(values, 'narrow', ALONG_X)  142 us
    dot_general x4, matrix products, contract_rows(): lax.dot_general(left, right, (((0,), (0,)), ((), ())), preferred_element_...  91.7 us
    ppermute x21, starting transfers between devices, to_y(): return lax.ppermute(values, 'narrow', ALONG_Y)  23.5 us
    ppermute x21, starting transfers between devices, to_x(): return lax.ppermute(values, 'narrow', ALONG_X)  21.4 us
  transfers between devices with their start and end apart: 53, of which 31 were waited for; matrix products, arithmetic and copies ran while one was open for 18% of the time, Pallas kernels for 30%

profile of v1, /device:TPU:0, one launch (start us, length us, event | category | flops | bytes accessed | tf_op | source)
XLA Modules:
  0.0 835.7 jit_solution(3747671296888601719)
XLA Ops:
  13.2 3.0 collective-permute-start.1
  17.7 44.4 %collective-permute-done.1.refs_2_ = bf16[2048,512]{1,0:T(8,128)(2,1)S(1)} collective-permute-done((bf16[2048,512]{1,0:T(8,128)(2,1)}, bf16[2048,512]{1,0:T(8,128)(2,1)S(1)}, u32[]{:S(2)}, u32[]{:S(2)}) %collective-permute-start.1) | collective-permute-done | bytes 2097184 | tf_op jit(solution)/shard_map/ppermute | solution.py:40
  67.3 20.4 %collective-permute-done.2.refs_3_ = bf16[2048,256]{1,0:T(8,128)(2,1)} collective-permute-done((bf16[2048,256]{1,0:T(8,128)(2,1)S(1)}, bf16[2048,256]{1,0:T(8,128)(2,1)}, u32[]{:S(2)}, u32[]{:S(2)}) %collective-permute-start.2) | collective-permute-done | bytes 1048608 | tf_op jit(solution)/shard_map/ppermute | solution.py:36
  91.3 6.8 all-gather.4.cloned.1.call-done.refs_6_.refs_10_
  98.0 3.0 slice.136
  101.1 2.5 reshape.51
  105.5 27.8 %shard_map.186 = (bf16[2048,2048]{1,0:T(8,128)(2,1)}, bf16[2048,2048]{1,0:T(8,128)(2,1)}, f32[2048,1536]{1,0:T(8,128)}, f32[2048,512]{1,0:T(8,128)}, bf16[2048,512]{1,0:T(8,128)(2,1)}, /*index=5*/f32[2048,1]{1,0:T(8,128)}) custom-call(s32[1]{0:T(128)} %bitcast.me_ref._, bf16[2048,512]{1,0:T(8,128)(2,1)} %refs_0_.1, bf16[2048,512]{1,0:T(8,128)(2,1)} %copy-done.29, ...), custom_call_target="tpu_custom_call" | custom-call | flops 12884901888 | bytes 52467712 | tf_op jit(solution)/shard_map/pallas_call | solution.py:75
  136.6 22.2 %collective-permute-done.11 = bf16[512,1024]{1,0:T(8,128)(2,1)S(1)} collective-permute-done((bf16[512,1024]{1,0:T(8,128)(2,1)S(1)}, bf16[512,1024]{1,0:T(8,128)(2,1)S(1)}, u32[]{:S(2)}, u32[]{:S(2)}) %collective-permute-start.11) | collective-permute-done | bytes 1048608 | tf_op jit(solution)/shard_map/ppermute | solution.py:40
  162.6 10.8 %collective-permute-done.12 = bf16[256,1024]{1,0:T(8,128)(2,1)S(1)} collective-permute-done((bf16[256,1024]{1,0:T(8,128)(2,1)S(1)}, bf16[256,1024]{1,0:T(8,128)(2,1)S(1)}, u32[]{:S(2)}, u32[]{:S(2)}) %collective-permute-start.12) | collective-permute-done | bytes 524320 | tf_op jit(solution)/shard_map/ppermute | solution.py:36
  176.0 46.8 %collective-permute-done.5.refs_2_ = bf16[2048,512]{1,0:T(8,128)(2,1)S(1)} collective-permute-done((bf16[2048,512]{1,0:T(8,128)(2,1)S(1)}, bf16[2048,512]{1,0:T(8,128)(2,1)S(1)}, u32[]{:S(2)}, u32[]{:S(2)}) %collective-permute-start.5) | collective-permute-done | bytes 2097184 | tf_op jit(solution)/shard_map/ppermute | solution.py:40
  225.3 22.5 %collective-permute-done.6.refs_3_ = bf16[2048,256]{1,0:T(8,128)(2,1)S(1)} collective-permute-done((bf16[2048,256]{1,0:T(8,128)(2,1)S(1)}, bf16[2048,256]{1,0:T(8,128)(2,1)S(1)}, u32[]{:S(2)}, u32[]{:S(2)}) %collective-permute-start.6) | collective-permute-done | bytes 1048608 | tf_op jit(solution)/shard_map/ppermute | solution.py:36
  251.1 1.9 copy-done.39
  253.1 28.9 %shard_map.187 = (f32[2048,2048]{1,0:T(8,128)}, bf16[2048,2048]{1,0:T(8,128)(2,1)}, f32[2048,1]{1,0:T(8,128)}) custom-call(s32[1]{0:T(128)} %bitcast.5.core_ref, bf16[2048,512]{1,0:T(8,128)(2,1)} %get-tuple-element.119.refs_0_, bf16[2048,512]{1,0:T(8,128)(2,1)} %copy-done.33, bf16[2048,512]{1,0:T(8,128)(2,1)} %copy-done.32, bf16[2048,256]{1,0:T(8,128)(2,1)} %copy-done.43, ...), custom_call_target="tpu_custom_call" | custom-call | flops 17179869184 | bytes 50348032 | tf_op jit(solution)/shard_map/pallas_call | solution.py:75
  282.0 12.1 %collective-permute-done.9.refs_2_ = bf16[2048,512]{1,0:T(8,128)(2,1)S(1)} collective-permute-done((bf16[2048,512]{1,0:T(8,128)(2,1)S(1)}, bf16[2048,512]{1,0:T(8,128)(2,1)S(1)}, u32[]{:S(2)}, u32[]{:S(2)}) %collective-permute-start.9) | collective-permute-done | bytes 2097184 | tf_op jit(solution)/shard_map/ppermute | solution.py:40
  300.8 46.9 %shard_map.188 = (bf16[2048,2048]{1,0:T(8,128)(2,1)}, bf16[2048,2048]{1,0:T(8,128)(2,1)}, bf16[2048,2048]{1,0:T(8,128)(2,1)}) custom-call(s32[1]{0:T(128)} %bitcast.me_ref._, bf16[2048,2048]{1,0:T(8,128)(2,1)} %get-tuple-element.137.n_ref, bf16[2048,4096]{1,0:T(8,128)(2,1)} %all-gather.6.cloned.1.call-done.w_ref.wg_ref.wu_ref), custom_call_target="tpu_custom_call" | custom-call | flops 34359738368 | bytes 50331648 | tf_op jit(solution)/shard_map/pallas_call | solution.py:75
  348.7 7.0 shard_map.189.g_ref.refs_8_
  355.7 23.9 %convolution_convert_fusion.1 = bf16[2048,2048]{1,0:T(8,128)(2,1)} fusion(bf16[2048,2048]{1,0:T(8,128)(2,1)} %get-tuple-element.145.l_ref, bf16[2048,2048]{1,0:T(8,128)(2,1)} %shard_map.189.g_ref.refs_8_), kind=kOutput, calls=%fused_computation.1 | convolution fusion | flops 17184063488 | bytes 25165824 | tf_op jit(solution)/shard_map/dot_general | solution.py:19
  380.4 78.1 %shard_map.190 = (bf16[2048,1024]{1,0:T(8,128)(2,1)}, bf16[2048,1024]{1,0:T(8,128)(2,1)}, bf16[2048,4096]{1,0:T(8,128)(2,1)}) custom-call(s32[4]{0:T(128)} %pad_add_fusion.1._.own_ref, bf16[2048,2048]{1,0:T(8,128)(2,1)} %shard_map.189.g_ref.refs_8_, bf16[2048,2048]{1,0:T(8,128)(2,1)} %get-tuple-element.146.a_ref, ...), custom_call_target="tpu_custom_call" | custom-call | flops 51539607552 | bytes 92274688 | tf_op jit(solution)/shard_map/pallas_call | solution.py:75
  458.5 3.7 fusion.13
  465.3 42.2 %convolution_convert_fusion = bf16[2048,4096]{1,0:T(8,128)(2,1)} fusion(bf16[2048,2048]{1,0:T(8,128)(2,1)} %get-tuple-element.137.n_ref, bf16[2048,4096]{1,0:T(8,128)(2,1)} %get-tuple-element.153), kind=kOutput, calls=%fused_computation | convolution fusion | flops 34368126976 | bytes 41943040 | tf_op jit(solution)/shard_map/dot_general | solution.py:19
  507.6 2.7 convert_element_type.165
  510.3 1.9 collective-permute-start.17
  517.9 18.6 %collective-permute-done.17.refs_2_ = bf16[512,1024]{1,0:T(8,128)(2,1)S(1)} collective-permute-done((bf16[512,1024]{1,0:T(8,128)(2,1)S(1)}, bf16[512,1024]{1,0:T(8,128)(2,1)S(1)}, u32[]{:S(2)}, u32[]{:S(2)}) %collective-permute-start.17) | collective-permute-done | bytes 1048608 | tf_op jit(solution)/shard_map/ppermute | solution.py:36
  536.5 2.0 collective-permute-done.22.refs_5_
  538.6 15.4 %collective-permute-done.20.refs_3_ = bf16[512,1024]{1,0:T(8,128)(2,1)S(1)} collective-permute-done((bf16[512,1024]{1,0:T(8,128)(2,1)S(1)}, bf16[512,1024]{1,0:T(8,128)(2,1)S(1)}, u32[]{:S(2)}, u32[]{:S(2)}) %collective-permute-start.20) | collective-permute-done | bytes 1048608 | tf_op jit(solution)/shard_map/ppermute | solution.py:36
  556.2 8.3 shard_map.191
  565.9 24.1 %shard_map.192 = (bf16[2048,256]{1,0:T(8,128)(2,1)}, bf16[2048,256]{1,0:T(8,128)(2,1)}, bf16[2048,256]{1,0:T(8,128)(2,1)}, bf16[2048,256]{1,0:T(8,128)(2,1)}, bf...) custom-call(s32[4]{0:T(128)} %pad_add_fusion.1._.own_ref, ...), custom_call_target="tpu_custom_call" | custom-call | flops 17179869184 | bytes 25165824 | tf_op jit(solution)/shard_map/pallas_call | solution.py:75
  590.1 18.6 %collective-permute-done.24.refs_2_ = bf16[512,2048]{1,0:T(8,128)(2,1)S(1)} collective-permute-done((bf16[512,2048]{1,0:T(8,128)(2,1)}, bf16[512,2048]{1,0:T(8,128)(2,1)S(1)}, u32[]{:S(2)}, u32[]{:S(2)}) %collective-permute-start.24) | collective-permute-done | bytes 2097184 | tf_op jit(solution)/shard_map/ppermute | solution.py:40
  608.7 2.1 collective-permute-done.23.refs_1_
  611.3 1.9 collective-permute-start.27
  613.2 16.2 %collective-permute-done.26.refs_3_ = bf16[256,2048]{1,0:T(8,128)(2,1)S(1)} collective-permute-done((bf16[256,2048]{1,0:T(8,128)(2,1)S(1)}, bf16[256,2048]{1,0:T(8,128)(2,1)S(1)}, u32[]{:S(2)}, u32[]{:S(2)}) %collective-permute-start.26) | collective-permute-done | bytes 1048608 | tf_op jit(solution)/shard_map/ppermute | solution.py:36
  630.7 33.6 %shard_map.193 = (bf16[2048,256]{1,0:T(8,128)(2,1)}, bf16[2048,256]{1,0:T(8,128)(2,1)}, bf16[2048,256]{1,0:T(8,128)(2,1)}, bf16[2048,256]{1,0:T(8,128)(2,1)}, bf...) custom-call(s32[4]{0:T(128)} %pad_add_fusion.1._.own_ref, ...), custom_call_target="tpu_custom_call" | custom-call | flops 17179869184 | bytes 58748928 | tf_op jit(solution)/shard_map/pallas_call | solution.py:75
  667.0 19.7 %convolution_convert_fusion.2 = bf16[2048,1536]{1,0:T(8,128)(2,1)} fusion(bf16[2048,2048]{1,0:T(8,128)(2,1)} %get-tuple-element.188, bf16[2048,1536]{1,0:T(8,128)(2,1)} %get-tuple-element.189), kind=kOutput, calls=%fused_computation.2 | convolution fusion | flops 12888047616 | bytes 20971520 | tf_op jit(solution)/shard_map/dot_general | solution.py:19
  691.5 16.2 %collective-permute-done.41 = f32[4,512]{1,0:T(4,128)S(1)} collective-permute-done((f32[4,512]{1,0:T(4,128)S(1)}, f32[4,512]{1,0:T(4,128)S(1)}, u32[]{:S(2)}, u32[]{:S(2)}) %collective-permute-start.41) | collective-permute-done | bytes 8224 | tf_op jit(solution)/shard_map/ppermute | solution.py:36
  718.0 2.7 add_convert_fusion.2
  720.7 2.5 add_convert_fusion.4
  724.5 13.5 %collective-permute-done.25 = bf16[2048,256]{1,0:T(8,128)(2,1)} collective-permute-done((bf16[2048,256]{1,0:T(8,128)(2,1)}, bf16[2048,256]{1,0:T(8,128)(2,1)}, u32[]{:S(2)}, u32[]{:S(2)}) %collective-permute-start.25) | collective-permute-done | bytes 1048608 | tf_op jit(solution)/shard_map/ppermute | solution.py:36
  739.7 43.4 %collective-permute-done.37 = bf16[2048,256]{1,0:T(8,128)(2,1)S(1)} collective-permute-done((bf16[2048,256]{1,0:T(8,128)(2,1)S(1)}, bf16[2048,256]{1,0:T(8,128)(2,1)S(1)}, u32[]{:S(2)}, u32[]{:S(2)}) %collective-permute-start.37) | collective-permute-done | bytes 1048608 | tf_op jit(solution)/shard_map/ppermute | solution.py:40
  784.9 5.9 convolution_convert_fusion.3
  793.1 3.2 convert_add_fusion
  796.3 4.3 add_convert_fusion
  800.6 3.0 convert_add_fusion.2
  803.7 1.9 fusion.8
  806.8 2.5 collective-permute-done.39
  810.1 2.8 collective-permute-done.40
  815.2 3.7 fusion.5
  820.4 2.6 fusion.14
  824.4 2.5 reduce-scatter.11.cloned.1.call-done
  (235 shorter events, 89.8 us)
Async XLA Ops:
  7.2 90.8 %all-gather.4.cloned.1.call-start = ((), (), s32[]{:S(2)}) async-start(), calls=%async_computation.4 | async-start | bytes 9437184 | tf_op jit(solution)/shard_map/all_gather | solution.py:471
  13.1 287.7 %all-gather.6.cloned.1.call-start = ((), (), s32[]{:S(2)}) async-start(), calls=%async_computation.5 | async-start | bytes 18874368 | tf_op jit(solution)/shard_map/all_gather | solution.py:471
  13.2 48.9 %collective-permute-start.1 = (bf16[2048,512]{1,0:T(8,128)(2,1)}, bf16[2048,512]{1,0:T(8,128)(2,1)S(1)}, u32[]{:S(2)}, u32[]{:S(2)}) collective-permute-start(bf16[2048,512]{1,0:T(8,128)(2,1)} %refs_0_.1), channel_id=1, source_target_pairs={{0,2},{2,0},{1,3},{3,1},{4,6},{6,4},{5,7},{7,5},{8,10},{10,8},{9,1... | collective-permute-start | bytes 6291464 | tf_op jit(solution)/shard_map/ppermute | solution.py:40
  16.2 47.3 %collective-permute-start = (bf16[2048,512]{1,0:T(8,128)(2,1)}, bf16[2048,512]{1,0:T(8,128)(2,1)S(1)}, u32[]{:S(2)}, u32[]{:S(2)}) collective-permute-start(bf16[2048,512]{1,0:T(8,128)(2,1)} %refs_0_.1), channel_id=1, source_target_pairs={{0,1},{1,0},{2,3},{3,2},{4,5},{5,4},{6,7},{7,6},{8,9},{9,8},{10,11... | collective-permute-start | bytes 6291464 | tf_op jit(solution)/shard_map/ppermute | solution.py:36
  63.7 24.0 %collective-permute-start.2 = (bf16[2048,256]{1,0:T(8,128)(2,1)S(1)}, bf16[2048,256]{1,0:T(8,128)(2,1)}, u32[]{:S(2)}, u32[]{:S(2)}) collective-permute-start(bf16[2048,256]{1,0:T(8,128)(2,1)S(1)} %slice.102), channel_id=1, source_target_pairs={{0,1},{1,0},{2,3},{3,2},{4,5},{5,4},{6,7},{7,6},{8,9},{9,8},{10,11... | collective-permute-start | bytes 3145736 | tf_op jit(solution)/shard_map/ppermute | solution.py:36
  65.2 23.6 %collective-permute-start.3 = (bf16[2048,256]{1,0:T(8,128)(2,1)S(1)}, bf16[2048,256]{1,0:T(8,128)(2,1)}, u32[]{:S(2)}, u32[]{:S(2)}) collective-permute-start(bf16[2048,256]{1,0:T(8,128)(2,1)S(1)} %slice.103), channel_id=1, source_target_pairs={{0,2},{2,0},{1,3},{3,1},{4,6},{6,4},{5,7},{7,5},{8,10},{10,8},{9,1... | collective-permute-start | bytes 3145736 | tf_op jit(solution)/shard_map/ppermute | solution.py:40
  88.9 291.4 %all-gather.8.cloned.1.call-start = ((), (), s32[]{:S(2)}) async-start(), calls=%async_computation.6 | async-start | bytes 9437184 | tf_op jit(solution)/shard_map/all_gather | solution.py:471
  133.4 374.2 %reduce-scatter.5.cloned.1.call-start = ((), (), s32[]{:S(2)}) async-start(), calls=%async_computation.7 | async-start | bytes 9437184 | tf_op jit(solution)/shard_map/reduce_scatter | solution.py:475
  133.5 25.3 %collective-permute-start.11 = (bf16[512,1024]{1,0:T(8,128)(2,1)S(1)}, bf16[512,1024]{1,0:T(8,128)(2,1)S(1)}, u32[]{:S(2)}, u32[]{:S(2)}) collective-permute-start(bf16[512,1024]{1,0:T(8,128)(2,1)S(1)} %constant_dynamic-slice_fusion), channel_id=1, source_target_pairs={{0,2},{2,0},{1,3},{3,1},{4,6},{6,4},{5,7},{7,5},{8,10},{10,8},{9,1... | collective-permute-start | bytes 3145736 | tf_op jit(solution)/shard_map/ppermute | solution.py:40
  135.2 25.0 %collective-permute-start.10 = (bf16[512,1024]{1,0:T(8,128)(2,1)S(1)}, bf16[512,1024]{1,0:T(8,128)(2,1)S(1)}, u32[]{:S(2)}, u32[]{:S(2)}) collective-permute-start(bf16[512,1024]{1,0:T(8,128)(2,1)S(1)} %constant_dynamic-slice_fusion), channel_id=1, source_target_pairs={{0,1},{1,0},{2,3},{3,2},{4,5},{5,4},{6,7},{7,6},{8,9},{9,8},{10,11... | collective-permute-start | bytes 3145736 | tf_op jit(solution)/shard_map/ppermute | solution.py:36
  160.3 13.1 %collective-permute-start.12 = (bf16[256,1024]{1,0:T(8,128)(2,1)S(1)}, bf16[256,1024]{1,0:T(8,128)(2,1)S(1)}, u32[]{:S(2)}, u32[]{:S(2)}) collective-permute-start(bf16[256,1024]{1,0:T(8,128)(2,1)S(1)} %slice.114), channel_id=1, source_target_pairs={{0,1},{1,0},{2,3},{3,2},{4,5},{5,4},{6,7},{7,6},{8,9},{9,8},{10,11... | collective-permute-start | bytes 1572872 | tf_op jit(solution)/shard_map/ppermute | solution.py:36
  161.8 12.7 %collective-permute-start.13 = (bf16[256,1024]{1,0:T(8,128)(2,1)S(1)}, bf16[256,1024]{1,0:T(8,128)(2,1)S(1)}, u32[]{:S(2)}, u32[]{:S(2)}) collective-permute-start(bf16[256,1024]{1,0:T(8,128)(2,1)S(1)} %slice.115), channel_id=1, source_target_pairs={{0,2},{2,0},{1,3},{3,1},{4,6},{6,4},{5,7},{7,5},{8,10},{10,8},{9,1... | collective-permute-start | bytes 1572872 | tf_op jit(solution)/shard_map/ppermute | solution.py:40
  174.7 76.5 %collective-permute-start.14 = (bf16[2048,1024]{1,0:T(8,128)(2,1)S(1)}, bf16[2048,1024]{1,0:T(8,128)(2,1)S(1)}, u32[]{:S(2)}, u32[]{:S(2)}) collective-permute-start(bf16[2048,1024]{1,0:T(8,128)(2,1)S(1)} %constant_dynamic-update-slice_fusion.refs_5_), channel_id=1, source_target_pairs={{0,4},{4,0},{8,12},{12,8},{16,20},{20,16},{24,28},{28,24},{1,5},{5... | collective-permute-start | bytes 12582920 | tf_op jit(solution)/shard_map/ppermute | solution.py:555
  174.7 48.0 %collective-permute-start.5 = (bf16[2048,512]{1,0:T(8,128)(2,1)S(1)}, bf16[2048,512]{1,0:T(8,128)(2,1)S(1)}, u32[]{:S(2)}, u32[]{:S(2)}) collective-permute-start(bf16[2048,512]{1,0:T(8,128)(2,1)S(1)} %copy-done.40), channel_id=1, source_target_pairs={{0,2},{2,0},{1,3},{3,1},{4,6},{6,4},{5,7},{7,5},{8,10},{10,8},{9,1... | collective-permute-start | bytes 6291464 | tf_op jit(solution)/shard_map/ppermute | solution.py:40
  175.4 47.7 %collective-permute-start.4 = (bf16[2048,512]{1,0:T(8,128)(2,1)S(1)}, bf16[2048,512]{1,0:T(8,128)(2,1)S(1)}, u32[]{:S(2)}, u32[]{:S(2)}) collective-permute-start(bf16[2048,512]{1,0:T(8,128)(2,1)S(1)} %copy-done.40), channel_id=1, source_target_pairs={{0,1},{1,0},{2,3},{3,2},{4,5},{5,4},{6,7},{7,6},{8,9},{9,8},{10,11... | collective-permute-start | bytes 6291464 | tf_op jit(solution)/shard_map/ppermute | solution.py:36
  223.3 24.6 %collective-permute-start.6 = (bf16[2048,256]{1,0:T(8,128)(2,1)S(1)}, bf16[2048,256]{1,0:T(8,128)(2,1)S(1)}, u32[]{:S(2)}, u32[]{:S(2)}) collective-permute-start(bf16[2048,256]{1,0:T(8,128)(2,1)S(1)} %slice.111), channel_id=1, source_target_pairs={{0,1},{1,0},{2,3},{3,2},{4,5},{5,4},{6,7},{7,6},{8,9},{9,8},{10,11... | collective-permute-start | bytes 3145736 | tf_op jit(solution)/shard_map/ppermute | solution.py:36
  223.9 24.3 %collective-permute-start.7 = (bf16[2048,256]{1,0:T(8,128)(2,1)S(1)}, bf16[2048,256]{1,0:T(8,128)(2,1)}, u32[]{:S(2)}, u32[]{:S(2)}) collective-permute-start(bf16[2048,256]{1,0:T(8,128)(2,1)S(1)} %slice.112), channel_id=1, source_target_pairs={{0,2},{2,0},{1,3},{3,1},{4,6},{6,4},{5,7},{7,5},{8,10},{10,8},{9,1... | collective-permute-start | bytes 3145736 | tf_op jit(solution)/shard_map/ppermute | solution.py:40
  248.2 45.8 %collective-permute-start.9 = (bf16[2048,512]{1,0:T(8,128)(2,1)S(1)}, bf16[2048,512]{1,0:T(8,128)(2,1)S(1)}, u32[]{:S(2)}, u32[]{:S(2)}) collective-permute-start(bf16[2048,512]{1,0:T(8,128)(2,1)S(1)} %copy-done.8), channel_id=1, source_target_pairs={{0,2},{2,0},{1,3},{3,1},{4,6},{6,4},{5,7},{7,5},{8,10},{10,8},{9,1... | collective-permute-start | bytes 6291464 | tf_op jit(solution)/shard_map/ppermute | solution.py:40
  249.7 45.5 %collective-permute-start.8 = (bf16[2048,512]{1,0:T(8,128)(2,1)S(1)}, bf16[2048,512]{1,0:T(8,128)(2,1)S(1)}, u32[]{:S(2)}, u32[]{:S(2)}) collective-permute-start(bf16[2048,512]{1,0:T(8,128)(2,1)S(1)} %copy-done.8), channel_id=1, source_target_pairs={{0,1},{1,0},{2,3},{3,2},{4,5},{5,4},{6,7},{7,6},{8,9},{9,8},{10,11... | collective-permute-start | bytes 6291464 | tf_op jit(solution)/shard_map/ppermute | solution.py:36
  298.6 49.1 %collective-permute-start.15 = (bf16[2048,256]{1,0:T(8,128)(2,1)}, bf16[2048,256]{1,0:T(8,128)(2,1)S(1)}, u32[]{:S(2)}, u32[]{:S(2)}) collective-permute-start(bf16[2048,256]{1,0:T(8,128)(2,1)} %slice.116), channel_id=1, source_target_pairs={{0,1},{1,0},{2,3},{3,2},{4,5},{5,4},{6,7},{7,6},{8,9},{9,8},{10,11... | collective-permute-start | bytes 3145736 | tf_op jit(solution)/shard_map/ppermute | solution.py:36
  300.0 47.8 %collective-permute-start.16 = (bf16[2048,256]{1,0:T(8,128)(2,1)}, bf16[2048,256]{1,0:T(8,128)(2,1)}, u32[]{:S(2)}, u32[]{:S(2)}) collective-permute-start(bf16[2048,256]{1,0:T(8,128)(2,1)} %slice.117), channel_id=1, source_target_pairs={{0,2},{2,0},{1,3},{3,1},{4,6},{6,4},{5,7},{7,5},{8,10},{10,8},{9,1... | collective-permute-start | bytes 3145736 | tf_op jit(solution)/shard_map/ppermute | solution.py:40
  379.7 307.1 %reduce-scatter.7.cloned.1.call-start = ((), (), s32[]{:S(2)}) async-start(), calls=%async_computation.8 | async-start | bytes 18874368 | tf_op jit(solution)/shard_map/reduce_scatter | solution.py:475
  462.2 45.4 %collective-permute-start.18 = (bf16[512,1024]{1,0:T(8,128)(2,1)}, bf16[512,1024]{1,0:T(8,128)(2,1)S(1)}, u32[]{:S(2)}, u32[]{:S(2)}) collective-permute-start(bf16[512,1024]{1,0:T(8,128)(2,1)} %get-tuple-element.225), channel_id=1, source_target_pairs={{0,1},{1,0},{2,3},{3,2},{4,5},{5,4},{6,7},{7,6},{8,9},{9,8},{10,11... | collective-permute-start | bytes 3145736 | tf_op jit(solution)/shard_map/ppermute | solution.py:36
  464.3 43.2 %collective-permute-start.19 = (bf16[512,1024]{1,0:T(8,128)(2,1)}, bf16[512,1024]{1,0:T(8,128)(2,1)S(1)}, u32[]{:S(2)}, u32[]{:S(2)}) collective-permute-start(bf16[512,1024]{1,0:T(8,128)(2,1)} %get-tuple-element.223), channel_id=1, source_target_pairs={{0,2},{2,0},{1,3},{3,1},{4,6},{6,4},{5,7},{7,5},{8,10},{10,8},{9,1... | collective-permute-start | bytes 3145736 | tf_op jit(solution)/shard_map/ppermute | solution.py:40
  510.3 281.5 %reduce-scatter.9.cloned.1.call-start = ((), (), s32[]{:S(2)}) async-start(), calls=%async_computation.9 | async-start | bytes 7077888 | tf_op jit(solution)/shard_map/reduce_scatter | solution.py:475
  510.3 26.2 %collective-permute-start.17 = (bf16[512,1024]{1,0:T(8,128)(2,1)S(1)}, bf16[512,1024]{1,0:T(8,128)(2,1)S(1)}, u32[]{:S(2)}, u32[]{:S(2)}) collective-permute-start(bf16[512,1024]{1,0:T(8,128)(2,1)S(1)} %get-tuple-element.226), channel_id=1, source_target_pairs={{0,1},{1,0},{2,3},{3,2},{4,5},{5,4},{6,7},{7,6},{8,9},{9,8},{10,11... | collective-permute-start | bytes 3145736 | tf_op jit(solution)/shard_map/ppermute | solution.py:36
  512.3 26.3 %collective-permute-start.22 = (bf16[512,1024]{1,0:T(8,128)(2,1)}, bf16[512,1024]{1,0:T(8,128)(2,1)S(1)}, u32[]{:S(2)}, u32[]{:S(2)}) collective-permute-start(bf16[512,1024]{1,0:T(8,128)(2,1)} %get-tuple-element.222), channel_id=1, source_target_pairs={{0,2},{2,0},{1,3},{3,1},{4,6},{6,4},{5,7},{7,5},{8,10},{10,8},{9,1... | collective-permute-start | bytes 3145736 | tf_op jit(solution)/shard_map/ppermute | solution.py:40
  516.5 37.4 %collective-permute-start.20 = (bf16[512,1024]{1,0:T(8,128)(2,1)S(1)}, bf16[512,1024]{1,0:T(8,128)(2,1)S(1)}, u32[]{:S(2)}, u32[]{:S(2)}) collective-permute-start(bf16[512,1024]{1,0:T(8,128)(2,1)S(1)} %add_convert_fusion.6), channel_id=1, source_target_pairs={{0,1},{1,0},{2,3},{3,2},{4,5},{5,4},{6,7},{7,6},{8,9},{9,8},{10,11... | collective-permute-start | bytes 3145736 | tf_op jit(solution)/shard_map/ppermute | solution.py:36
  517.1 38.1 %collective-permute-start.21 = (bf16[512,1024]{1,0:T(8,128)(2,1)S(1)}, bf16[512,1024]{1,0:T(8,128)(2,1)S(1)}, u32[]{:S(2)}, u32[]{:S(2)}) collective-permute-start(bf16[512,1024]{1,0:T(8,128)(2,1)S(1)} %add_convert_fusion.5), channel_id=1, source_target_pairs={{0,2},{2,0},{1,3},{3,1},{4,6},{6,4},{5,7},{7,5},{8,10},{10,8},{9,1... | collective-permute-start | bytes 3145736 | tf_op jit(solution)/shard_map/ppermute | solution.py:40
  564.5 44.2 %collective-permute-start.24 = (bf16[512,2048]{1,0:T(8,128)(2,1)}, bf16[512,2048]{1,0:T(8,128)(2,1)S(1)}, u32[]{:S(2)}, u32[]{:S(2)}) collective-permute-start(bf16[512,2048]{1,0:T(8,128)(2,1)} %get-tuple-element.161.refs_0_), channel_id=1, source_target_pairs={{0,2},{2,0},{1,3},{3,1},{4,6},{6,4},{5,7},{7,5},{8,10},{10,8},{9,1... | collective-permute-start | bytes 6291464 | tf_op jit(solution)/shard_map/ppermute | solution.py:40
  565.3 45.5 %collective-permute-start.23 = (bf16[512,2048]{1,0:T(8,128)(2,1)}, bf16[512,2048]{1,0:T(8,128)(2,1)S(1)}, u32[]{:S(2)}, u32[]{:S(2)}) collective-permute-start(bf16[512,2048]{1,0:T(8,128)(2,1)} %get-tuple-element.161.refs_0_), channel_id=1, source_target_pairs={{0,1},{1,0},{2,3},{3,2},{4,5},{5,4},{6,7},{7,6},{8,9},{9,8},{10,11... | collective-permute-start | bytes 6291464 | tf_op jit(solution)/shard_map/ppermute | solution.py:36
  610.9 18.5 %collective-permute-start.26 = (bf16[256,2048]{1,0:T(8,128)(2,1)S(1)}, bf16[256,2048]{1,0:T(8,128)(2,1)S(1)}, u32[]{:S(2)}, u32[]{:S(2)}) collective-permute-start(bf16[256,2048]{1,0:T(8,128)(2,1)S(1)} %slice.126), channel_id=1, source_target_pairs={{0,1},{1,0},{2,3},{3,2},{4,5},{5,4},{6,7},{7,6},{8,9},{9,8},{10,11... | collective-permute-start | bytes 3145736 | tf_op jit(solution)/shard_map/ppermute | solution.py:36
  611.3 18.1 %collective-permute-start.27 = (bf16[256,2048]{1,0:T(8,128)(2,1)S(1)}, bf16[256,2048]{1,0:T(8,128)(2,1)S(1)}, u32[]{:S(2)}, u32[]{:S(2)}) collective-permute-start(bf16[256,2048]{1,0:T(8,128)(2,1)S(1)} %slice.127), channel_id=1, source_target_pairs={{0,2},{2,0},{1,3},{3,1},{4,6},{6,4},{5,7},{7,5},{8,10},{10,8},{9,1... | collective-permute-start | bytes 3145736 | tf_op jit(solution)/shard_map/ppermute | solution.py:40
  664.2 22.5 %collective-permute-start.29 = (bf16[2048,256]{1,0:T(8,128)(2,1)}, bf16[2048,256]{1,0:T(8,128)(2,1)S(1)}, u32[]{:S(2)}, u32[]{:S(2)}) collective-permute-start(bf16[2048,256]{1,0:T(8,128)(2,1)} %get-tuple-element.184), channel_id=1, source_target_pairs={{0,1},{1,0},{2,3},{3,2},{4,5},{5,4},{6,7},{7,6},{8,9},{9,8},{10,11... | collective-permute-start | bytes 3145736 | tf_op jit(solution)/shard_map/ppermute | solution.py:36
  665.3 21.4 %collective-permute-start.30 = (bf16[2048,256]{1,0:T(8,128)(2,1)}, bf16[2048,256]{1,0:T(8,128)(2,1)}, u32[]{:S(2)}, u32[]{:S(2)}) collective-permute-start(bf16[2048,256]{1,0:T(8,128)(2,1)} %get-tuple-element.185), channel_id=1, source_target_pairs={{0,2},{2,0},{1,3},{3,1},{4,6},{6,4},{5,7},{7,5},{8,10},{10,8},{9,1... | collective-permute-start | bytes 3145736 | tf_op jit(solution)/shard_map/ppermute | solution.py:40
  687.8 139.1 %reduce-scatter.11.cloned.1.call-start = ((), (), s32[]{:S(2)}) async-start(), calls=%async_computation.10 | async-start | bytes 2359296 | tf_op jit(solution)/shard_map/reduce_scatter | solution.py:475
  687.8 26.4 %collective-permute-start.34 = (bf16[2048,256]{1,0:T(8,128)(2,1)}, bf16[2048,256]{1,0:T(8,128)(2,1)}, u32[]{:S(2)}, u32[]{:S(2)}) collective-permute-start(bf16[2048,256]{1,0:T(8,128)(2,1)} %get-tuple-element.199), channel_id=1, source_target_pairs={{0,1},{1,0},{2,3},{3,2},{4,5},{5,4},{6,7},{7,6},{8,9},{9,8},{10,11... | collective-permute-start | bytes 3145736 | tf_op jit(solution)/shard_map/ppermute | solution.py:36
  688.6 27.1 %collective-permute-start.35 = (bf16[2048,256]{1,0:T(8,128)(2,1)}, bf16[2048,256]{1,0:T(8,128)(2,1)}, u32[]{:S(2)}, u32[]{:S(2)}) collective-permute-start(bf16[2048,256]{1,0:T(8,128)(2,1)} %get-tuple-element.200), channel_id=1, source_target_pairs={{0,2},{2,0},{1,3},{3,1},{4,6},{6,4},{5,7},{7,5},{8,10},{10,8},{9,1... | collective-permute-start | bytes 3145736 | tf_op jit(solution)/shard_map/ppermute | solution.py:40
  690.4 17.3 %collective-permute-start.41 = (f32[4,512]{1,0:T(4,128)S(1)}, f32[4,512]{1,0:T(4,128)S(1)}, u32[]{:S(2)}, u32[]{:S(2)}) collective-permute-start(f32[4,512]{1,0:T(4,128)S(1)} %reshape.54), channel_id=1, source_target_pairs={{0,1},{1,0},{2,3},{3,2},{4,5},{5,4},{6,7},{7,6},{8,9},{9,8},{10,11... | collective-permute-start | bytes 24584 | tf_op jit(solution)/shard_map/ppermute | solution.py:36
  711.5 26.5 %collective-permute-start.25 = (bf16[2048,256]{1,0:T(8,128)(2,1)}, bf16[2048,256]{1,0:T(8,128)(2,1)}, u32[]{:S(2)}, u32[]{:S(2)}) collective-permute-start(bf16[2048,256]{1,0:T(8,128)(2,1)} %get-tuple-element.171), channel_id=1, source_target_pairs={{0,1},{1,0},{2,3},{3,2},{4,5},{5,4},{6,7},{7,6},{8,9},{9,8},{10,11... | collective-permute-start | bytes 3145736 | tf_op jit(solution)/shard_map/ppermute | solution.py:36
  711.9 26.4 %collective-permute-start.38 = (bf16[2048,256]{1,0:T(8,128)(2,1)}, bf16[2048,256]{1,0:T(8,128)(2,1)}, u32[]{:S(2)}, u32[]{:S(2)}) collective-permute-start(bf16[2048,256]{1,0:T(8,128)(2,1)} %get-tuple-element.204), channel_id=1, source_target_pairs={{0,2},{2,0},{1,3},{3,1},{4,6},{6,4},{5,7},{7,5},{8,10},{10,8},{9,1... | collective-permute-start | bytes 3145736 | tf_op jit(solution)/shard_map/ppermute | solution.py:40
  713.3 87.3 %collective-permute-start.28 = (bf16[2048,256]{1,0:T(8,128)(2,1)}, bf16[2048,256]{1,0:T(8,128)(2,1)}, u32[]{:S(2)}, u32[]{:S(2)}) collective-permute-start(bf16[2048,256]{1,0:T(8,128)(2,1)} %get-tuple-element.182), channel_id=1, source_target_pairs={{0,1},{1,0},{2,3},{3,2},{4,5},{5,4},{6,7},{7,6},{8,9},{9,8},{10,11... | collective-permute-start | bytes 3145736 | tf_op jit(solution)/shard_map/ppermute | solution.py:36
  714.2 86.4 %collective-permute-start.33 = (bf16[2048,256]{1,0:T(8,128)(2,1)}, bf16[2048,256]{1,0:T(8,128)(2,1)}, u32[]{:S(2)}, u32[]{:S(2)}) collective-permute-start(bf16[2048,256]{1,0:T(8,128)(2,1)} %get-tuple-element.193), channel_id=1, source_target_pairs={{0,2},{2,0},{1,3},{3,1},{4,6},{6,4},{5,7},{7,5},{8,10},{10,8},{9,1... | collective-permute-start | bytes 3145736 | tf_op jit(solution)/shard_map/ppermute | solution.py:40
  717.3 65.8 %collective-permute-start.37 = (bf16[2048,256]{1,0:T(8,128)(2,1)S(1)}, bf16[2048,256]{1,0:T(8,128)(2,1)S(1)}, u32[]{:S(2)}, u32[]{:S(2)}) collective-permute-start(bf16[2048,256]{1,0:T(8,128)(2,1)S(1)} %add_convert_fusion.1), channel_id=1, source_target_pairs={{0,2},{2,0},{1,3},{3,1},{4,6},{6,4},{5,7},{7,5},{8,10},{10,8},{9,1... | collective-permute-start | bytes 3145736 | tf_op jit(solution)/shard_map/ppermute | solution.py:40
  738.0 52.8 %collective-permute-start.36 = (bf16[2048,256]{1,0:T(8,128)(2,1)}, bf16[2048,256]{1,0:T(8,128)(2,1)S(1)}, u32[]{:S(2)}, u32[]{:S(2)}) collective-permute-start(bf16[2048,256]{1,0:T(8,128)(2,1)} %add_convert_fusion.2), channel_id=1, source_target_pairs={{0,1},{1,0},{2,3},{3,2},{4,5},{5,4},{6,7},{7,6},{8,9},{9,8},{10,11... | collective-permute-start | bytes 3145736 | tf_op jit(solution)/shard_map/ppermute | solution.py:36
  738.3 62.3 %collective-permute-start.32 = (bf16[2048,256]{1,0:T(8,128)(2,1)}, bf16[2048,256]{1,0:T(8,128)(2,1)}, u32[]{:S(2)}, u32[]{:S(2)}) collective-permute-start(bf16[2048,256]{1,0:T(8,128)(2,1)} %add_convert_fusion.3), channel_id=1, source_target_pairs={{0,2},{2,0},{1,3},{3,1},{4,6},{6,4},{5,7},{7,5},{8,10},{10,8},{9,1... | collective-permute-start | bytes 3145736 | tf_op jit(solution)/shard_map/ppermute | solution.py:40
  783.1 17.5 %collective-permute-start.31 = (bf16[2048,256]{1,0:T(8,128)(2,1)}, bf16[2048,256]{1,0:T(8,128)(2,1)}, u32[]{:S(2)}, u32[]{:S(2)}) collective-permute-start(bf16[2048,256]{1,0:T(8,128)(2,1)} %add_convert_fusion.4), channel_id=1, source_target_pairs={{0,1},{1,0},{2,3},{3,2},{4,5},{5,4},{6,7},{7,6},{8,9},{9,8},{10,11... | collective-permute-start | bytes 3145736 | tf_op jit(solution)/shard_map/ppermute | solution.py:36
  814.2 5.1 collective-permute-start.45
  (50 other events, 938.1 us)
Sparse Core Ops, SparseCore 0:
  13.2 84.7 all-gather.3
  100.2 149.6 all-gather.5
  251.5 80.7 all-gather.7
  379.8 86.9 reduce-scatter.4
  510.4 166.1 reduce-scatter.6
  687.9 67.1 reduce-scatter.8
  793.2 33.6 reduce-scatter.10

commit v2 on v1

--- a/solution.py
+++ b/solution.py
@@ -11,7 +11,7 @@
 EPSILON = 1e-05
 BF = jnp.bfloat16
 F32 = jnp.float32
-TILE = 256
+TILE = 512
 BIG = 512
 
 
@@ -30,6 +30,7 @@
 
 ALONG_X = [(0, 1), (1, 0), (2, 3), (3, 2)]
 ALONG_Y = [(0, 2), (2, 0), (1, 3), (3, 1)]
+ACROSS = [(0, 3), (3, 0), (1, 2), (2, 1)]
 
 
 def to_x(values):
@@ -38,6 +39,10 @@
 
 def to_y(values):
     return lax.ppermute(values, "narrow", ALONG_Y)
+
+
+def to_far(values):
+    return lax.ppermute(values, "narrow", ACROSS)
 
 
 def halves(values, axis):
@@ -152,32 +157,50 @@
     )
 
 
-def mix(core, pieces, mats, x_full, gain):
-    count, parts = len(pieces), len(mats)
+def mix(core, pieces, mine, other, x_full, gain):
+    count = len(pieces)
     row_count, full = x_full.shape
-    cols = mats[0].shape[1]
+    packed = bool(other)
+    mats = [*mine, *other]
+    parts = len(mats)
+    slab = pieces[0].shape[1] // 2
 
     def body(core_ref, *refs):
-        ys, ms, (x_ref, gain_ref), (h_ref, n_ref, s_ref), (all_ref,) = (
+        ys, ms, (x_ref, gain_ref), (h_ref, n_ref, s_ref), (all_ref, *weight) = (
             refs[:count],
             refs[count : count + parts],
             refs[count + parts : count + parts + 2],
             refs[count + parts + 2 : count + parts + 5],
             refs[count + parts + 5 :],
         )
+        weight_ref = weight[0] if packed else ms[0]
+
+        if packed:
+
+            @pl.when(pl.program_id(0) == 0)
+            def _():
+                for side in range(2):
+                    start = (core_ref[0] ^ side) * (full // 2)
+                    for k in range(5):
+                        ref = ms[5 * side + k]
+                        for n in range(ref.shape[0] // slab):
+                            column = start + (n + (k == 4) * (full // 4 // slab)) * slab
+                            at = pl.ds(pl.multiple_of(column, 128), slab)
+                            for half in range(2):
+                                row = (2 * min(k, 3) + half) * slab
+                                weight_ref[row : row + slab, at] = ref[
+                                    n * slab : (n + 1) * slab, half * slab : (half + 1) * slab
+                                ]
+
         at = 0
         for ref in ys:
             all_ref[:, at : at + ref.shape[1]] = ref[...]
             at += ref.shape[1]
-        total = 0.0
-        for k, ref in enumerate(ms):
-            where = pl.ds(pl.multiple_of((core_ref[0] ^ k) * cols, 128), cols) if parts > 1 else slice(None)
-            h = x_ref[:, where].astype(F32) + jnp.dot(all_ref[...], ref[...], preferred_element_type=F32)
-            h_ref[:, where] = h
-            total = total + jnp.sum(h * h, axis=1, keepdims=True)
-        scale = lax.rsqrt(total / full + EPSILON)
+        h = x_ref[...].astype(F32) + jnp.dot(all_ref[...], weight_ref[...], preferred_element_type=F32)
+        h_ref[...] = h
+        scale = lax.rsqrt(jnp.sum(h * h, axis=1, keepdims=True) / full + EPSILON)
         s_ref[...] = scale
-        n_ref[...] = (h_ref[...] * scale * gain_ref[...]).astype(BF)
+        n_ref[...] = (h * scale * gain_ref[...]).astype(BF)
 
     return run(
         body,
@@ -187,7 +210,7 @@
         [tiles(p.shape[1], BIG) for p in pieces] + [whole(m.shape) for m in mats] + [tiles(full, BIG), whole(gain.shape)],
         [shape_of((row_count, full), F32), shape_of((row_count, full), BF), shape_of((row_count, 1), F32)],
         [tiles(full, BIG), tiles(full, BIG), tiles(1, BIG)],
-        [pltpu.VMEM((BIG, full), BF)],
+        [pltpu.VMEM((BIG, full), BF)] + ([pltpu.VMEM((full, full), BF)] if packed else []),
         flops=2 * row_count * full * full,
     )
 
@@ -199,7 +222,9 @@
     full = 4 * share
 
     def body(me_ref, *refs):
-        for ref, start in zip(refs[:-1], piece_starts(me_ref[0], share, True)):
+        starts = piece_starts(me_ref[0], share, True)
+        starts[4] = starts[3] + pieces[3].shape[1]
+        for ref, start in zip(refs[:-1], starts):
             refs[-1][:, pl.ds(pl.multiple_of(start, 128), ref.shape[1])] = ref[...]
 
     return run(
@@ -240,13 +265,15 @@
     )
 
 
-def ffn_back(owners, band, grad, slope_up, slope_gate, down, weight):
+def ffn_back(owners, band, grad, slope_up, slope_gate, down, weight, d_both=None):
+    bands = owners.shape[0]
     row_count, full = grad.shape
     units = down.shape[0]
     step = min(512, units)
     count = units // step
 
-    def body(_, g_ref, a_ref, b_ref, d_ref, wg_ref, wu_ref, low_ref, high_ref, o_ref, total):
+    def body(_, g_ref, a_ref, b_ref, d_ref, wg_ref, wu_ref, *refs):
+        *halves_of, o_ref, total = refs[-2 * bands - 2 :]
         j = pl.program_id(1)
         dq = contract_cols(g_ref[...], d_ref[...])
         d_gate = (dq * b_ref[...].astype(F32)).astype(BF)
@@ -264,16 +291,18 @@
         def _():
             total[...] += term
 
-        @pl.when(j == count - 1)
-        def _():
-            low_ref[...] = total[:, : full // 2].astype(BF)
-            high_ref[...] = total[:, full // 2 :].astype(BF)
+        for k in range(bands):
+
+            @pl.when((pl.program_id(0) == k) & (j == count - 1))
+            def _(k=k):
+                halves_of[2 * k][...] = total[:, : full // 2].astype(BF)
+                halves_of[2 * k + 1][...] = total[:, full // 2 :].astype(BF)
 
     return run(
         body,
-        (row_count // band, count),
+        (bands, count),
         owners,
-        [grad, slope_up, slope_gate, down, weight, weight],
+        [grad, slope_up, slope_gate, down, weight, weight] + ([] if d_both is None else [d_both]),
         [
             pl.BlockSpec((band, full), lambda i, j, o: (o[i], 0)),
             pl.BlockSpec((band, step), lambda i, j, o: (o[i], j)),
@@ -281,22 +310,21 @@
             pl.BlockSpec((step, full), lambda i, j, o: (j, 0)),
             pl.BlockSpec((full, step), lambda i, j, o: (0, j)),
             pl.BlockSpec((full, step), lambda i, j, o: (0, count + j)),
-        ],
-        [shape_of((row_count, full // 2), BF)] * 2 + [shape_of((row_count, 2 * units), BF)],
-        [
-            pl.BlockSpec((band, full // 2), lambda i, j, o: (i, 0)),
-            pl.BlockSpec((band, full // 2), lambda i, j, o: (i, 0)),
-            pl.BlockSpec((band, 2 * units), lambda i, j, o: (o[i], 0)),
-        ],
+        ]
+        + ([] if d_both is None else [pl.BlockSpec(memory_space=pl.ANY)]),
+        [shape_of((band, full // 2), BF)] * (2 * bands) + [shape_of((row_count, 2 * units), BF)],
+        [pl.BlockSpec((band, full // 2), lambda i, j, o: (0, 0))] * (2 * bands)
+        + [pl.BlockSpec((band, 2 * units), lambda i, j, o: (o[i], 0))],
         [pltpu.VMEM((band, full), F32)],
-        flops=6 * row_count * full * units,
+        flops=6 * bands * band * full * units,
+        aliases=None if d_both is None else {7: 2 * bands},
     )
 
 
 def hidden_back(me, terms, hidden, scale_two, grad, gain):
     band = terms[0][0].shape[0]
     full = gain.shape[1]
-    tile = min(TILE, band)
+    tile = min(128, band)
     count = 2 * len(terms)
 
     def body(_, *refs):
@@ -334,8 +362,8 @@
     row_count = mixed.shape[0]
     count = row_count // TILE
     size = owners.shape[0]
-    band = row_count // size
     given = len(pieces)
+    assert given == 1 or row_count == size * TILE
     packed = pl.BlockSpec((full, 3 * part), lambda *_: (0, 0), pipeline_mode=pl.Buffered(1))
 
     def body(own_ref, *refs):
@@ -353,21 +381,17 @@
         if given == 1:
             d_ref[...] = refs[0][pl.ds(pl.multiple_of(first, TILE), TILE), :]
         else:
-            apart = (first // band) ^ own_ref[size - 1]
-            within = pl.multiple_of(first % band, TILE)
+            apart = (count - 1 - i) ^ own_ref[size - 1]
             for k in range(3):
 
                 @pl.when(apart == k)
                 def _(k=k):
-                    d_ref[...] = refs[k][pl.ds(within, TILE), :]
-
-            @pl.when((apart == 3) & (within < band // 2))
+                    d_ref[...] = refs[k][...]
+
+            @pl.when(apart == 3)
             def _():
-                d_ref[...] = refs[3][pl.ds(within, TILE), :]
-
-            @pl.when((apart == 3) & (within >= band // 2))
-            def _():
-                d_ref[...] = refs[4][pl.ds(pl.multiple_of(within - band // 2, TILE), TILE), :]
+                d_ref[: TILE // 2, :] = refs[3][...]
+                d_ref[TILE // 2 :, :] = refs[4][...]
 
         dy_ref[...] = contract_cols(d_ref[...], w_ref[...])
         dy = dy_ref[...]
@@ -444,18 +468,6 @@
     return (left.astype(F32) + right.astype(F32)).astype(BF)
 
 
-def scatter_first(terms):
-    return lax.optimization_barrier((to_x(terms[0][0]), to_y(terms[0][1])))
-
-
-def scatter_last(terms, via_x, via_y):
-    to_send = terms[1][0], add_low(terms[1][1], via_y), add_low(terms[2][0], via_x), terms[2][1]
-    x_low, x_high, y_low, y_high = lax.optimization_barrier(
-        (to_x(to_send[0]), to_x(to_send[1]), to_y(to_send[2]), to_y(to_send[3]))
-    )
-    return [terms[3], (x_low, x_high), (y_low, y_high)]
-
-
 def scatter_plain(terms, axis):
     joined = jnp.concatenate([jnp.concatenate(pair, axis=1) for pair in terms], axis=axis).astype(F32)
     return lax.psum_scatter(joined, "narrow", scatter_dimension=axis, tiled=True)
@@ -472,7 +484,7 @@
 
 
 def wide_sums(terms, axis):
-    return lax.psum_scatter(terms.astype(BF), "wide", scatter_dimension=axis, tiled=True).astype(F32)
+    return lax.psum_scatter(terms.astype(BF), "wide", scatter_dimension=axis, tiled=True)
 
 
 def narrow_total(values, square):
@@ -488,6 +500,38 @@
     for bit in (1, 2, 4):
         values = values + lax.ppermute(values, "wide", [(i, i ^ bit) for i in range(lax.axis_size("wide"))])
     return values
+
+
+def to_core(values):
+    return lax.ppermute(values, "wide", [(i, i ^ 1) for i in range(lax.axis_size("wide"))])
+
+
+def line_step(state, step):
+    sums, right, left = state
+    z = lax.axis_index("wide") // 2
+
+    def with_own(come, chip):
+        own = lax.dynamic_index_in_dim(sums, jnp.clip(chip, 0, 3), 0, keepdims=False)
+        return own if come is None else add_low(own, come)
+
+    return (
+        sums,
+        lax.ppermute(with_own(right, z + 4 - step), "wide", [(w, w + 2) for w in range(2 * step)]),
+        lax.ppermute(with_own(left, z - 4 + step), "wide", [(w, w - 2) for w in range(8 - 2 * step, 8)]),
+    )
+
+
+def line_start(terms, core):
+    blocks = terms.reshape(4, 2, terms.shape[0] // 8, terms.shape[1])
+    other = to_core(lax.dynamic_index_in_dim(blocks, 1 - core, 1, keepdims=False))
+    sums = add_low(lax.dynamic_index_in_dim(blocks, core, 1, keepdims=False), other)
+    return line_step((sums, None, None), 1)
+
+
+def line_end(state):
+    sums, right, left = line_step(state, 3)
+    own = lax.dynamic_index_in_dim(sums, lax.axis_index("wide") // 2, 0, keepdims=False)
+    return own.astype(F32) + right.astype(F32) + left.astype(F32)
 
 
 def after(value, *others):
@@ -525,102 +569,186 @@
     order = [me ^ 3, me ^ 1, me ^ 2, me] if square else list(range(size))
     owners = jnp.stack([jnp.asarray(o, jnp.int32) for o in order])
 
-    pack = jnp.concatenate([in_weight[:, k] for k in range(3)] + list(halves(out_weight, 0)), axis=1)
-    slim = pack.shape[0]
-    if square:
-        pack_all = wide_all(pack, 0)
-        out_rows = pack_all[:, 3 * part_width :].reshape(-1, slim, 2, slim)
-        out_rows = out_rows.transpose(2, 1, 0, 3).reshape(part_width, full_width)
-    else:
-        pack_all = wide_all(jnp.concatenate([in_weight[:, k] for k in range(3)], axis=1), 0)
-        out_rows = wide_all(out_weight, 1)
-    x_pieces, _, _ = gather_pieces(tokens, 1, square)
-    both_all = wide_all(after(jnp.concatenate([gate_weight, up_weight], axis=1), *x_pieces), 0)
-
     positions = lax.broadcasted_iota(jnp.int32, (row_count,), 0)
     masks = jnp.stack(
         [((positions >= k) & (segment_ids == lagged(segment_ids, k))).astype(F32) for k in (1, 2)], axis=1
     )
-    normed_one, x_full, mixed, filtered, mixer_low, scale_one = project(
-        me_s, x_pieces, square, gain_one, pack_all, kernel, masks
-    )
-    down_all = wide_all(after(down_weight, mixer_low), 1)
+    barrier = lax.optimization_barrier
+    in_cols = 3 * part_width
+    pack = [in_weight[:, k] for k in range(3)]
+    both = jnp.concatenate([gate_weight, up_weight], axis=1)
+
+    def project_rows(x_pieces, in_all):
+        return tuple(project(me_s, x_pieces, square, gain_one, in_all, kernel, masks))
+
+    def unpacked(in_all):
+        rows = in_all[:, in_cols:].reshape(-1, pack[0].shape[0], 2, part_width // 2)
+        return rows.transpose(2, 1, 0, 3).reshape(part_width, full_width)
 
     if square:
+        in_all = wide_all(jnp.concatenate(pack + list(halves(out_weight, 0)), axis=1), 0)
+        x_pieces = gather_pieces(tokens, 1, True)[0]
+        both_all = wide_all(after(both, *x_pieces), 0)
+
         half_cols = full_width // 2
-        pairs = [(i, i ^ 1) for i in range(lax.axis_size("wide"))]
-        out_half = lax.dynamic_slice_in_dim(out_rows, core * half_cols, half_cols, 1)
-        out_half = after(out_half, x_pieces[3])
-        mine = jnp.concatenate(gather_pieces(out_half, 0, True)[0], axis=0)
-        mats = [mine, lax.ppermute(mine, "wide", pairs)]
+        own_out = lax.dynamic_slice(in_all, (core * half_cols, jnp.int32(in_cols)), (half_cols, part_width))
+        low_grad, high_grad = cotangent[:, : part_width // 4], cotangent[:, part_width // 4 :]
+        x_out, y_out, low_far, projected = barrier(
+            (to_x(own_out), to_y(own_out), to_far(after(low_grad, *x_pieces)), project_rows(x_pieces, in_all))
+        )
+        normed_one, x_full, mixed, filtered, mixer_low, scale_one = projected
+        down_all = wide_all(after(down_weight, mixer_low), 1)
+        x_mix, y_mix = barrier((to_x(mixer_low), to_y(mixer_low)))
+        low_out, high_out = to_x(halves(y_out, 0)[0]), to_y(halves(x_out, 0)[1])
+        low_mix, high_mix, low_out, high_out, *near = barrier(
+            (
+                to_x(halves(y_mix, 1)[0]),
+                to_y(halves(x_mix, 1)[1]),
+                low_out,
+                high_out,
+                to_core(own_out),
+                to_core(x_out),
+                to_core(y_out),
+            )
+        )
+        far = [to_core(low_out), to_core(high_out)]
+        y_pieces = [mixer_low, x_mix, y_mix, low_mix, high_mix]
+        mine, other = [own_out, x_out, y_out, low_out, high_out], [*near, *far]
+        grad_now, high_now, _ = barrier((cotangent, high_grad, low_mix))
+        hidden, normed_two, scale_two = mix(core_s, y_pieces, mine, other, x_full, gain_two)
+        x_grad, y_grad, high_far, (hidden_low, slope_up, slope_gate) = barrier(
+            (to_x(grad_now), to_y(grad_now), to_far(high_now), expand(me_s, normed_two, both_all))
+        )
+        g_pieces = [cotangent, x_grad, y_grad, low_far, high_far]
     else:
-        mats = [lax.all_gather(out_rows, "narrow", axis=0, tiled=True)]
-    y_pieces, _, _ = gather_pieces(mixer_low, 1, square)
-    g_pieces, (hidden, normed_two, scale_two), (hidden_low, slope_up, slope_gate) = gather_pieces(
-        after(cotangent, *y_pieces[1:]),
-        1,
-        square,
-        (
-            lambda: tuple(mix(core_s, y_pieces, mats, x_full, gain_two)),
-            lambda first: tuple(expand(me_s, first[1], both_all)),
-        ),
-    )
+        in_all = wide_all(jnp.concatenate(pack, axis=1), 0)
+        out_rows = wide_all(out_weight, 1)
+        x_pieces = gather_pieces(tokens, 1, False)[0]
+        both_all = wide_all(both, 0)
+        down_all = wide_all(down_weight, 1)
+        normed_one, x_full, mixed, filtered, mixer_low, scale_one = project_rows(x_pieces, in_all)
+        y_pieces = gather_pieces(mixer_low, 1, False)[0]
+        mine, other = [lax.all_gather(out_rows, "narrow", axis=0, tiled=True)], []
+        hidden, normed_two, scale_two = mix(core_s, y_pieces, mine, other, x_full, gain_two)
+        hidden_low, slope_up, slope_gate = expand(me_s, normed_two, both_all)
+        g_pieces = gather_pieces(cotangent, 1, False)[0]
     grad_full = lay(me_s, g_pieces, square)
-
     down_terms = contract_rows(hidden_low, grad_full).astype(BF)
     down_grad = wide_sums(down_terms, 1)
-    low, high, d_both = ffn_back(owners, band, grad_full, after(slope_up, down_terms), slope_gate, down_all, both_all)
-    ffn_terms = [(low[k * band : (k + 1) * band], high[k * band : (k + 1) * band]) for k in range(size)]
+    slope_up = after(slope_up, down_terms)
+
+    def ffn(which, d_both):
+        *parts, d_both = ffn_back(which, band, grad_full, slope_up, slope_gate, down_all, both_all, d_both)
+        return list(zip(parts[0::2], parts[1::2])), d_both
+
+    def mixer(dh_pieces, out_rows):
+        *parts, d_flat, kernel_grad, d_hidden_low = mixer_back(
+            owners, dh_pieces, out_rows, mixed, filtered, kernel, masks, in_all
+        )
+        return list(zip(parts[0::2], parts[1::2])), d_flat, kernel_grad, d_hidden_low
+
+    def dh_of(sums):
+        return hidden_back(me_s, sums, hidden, scale_two, grad_full, gain_two)
+
+    def out_terms_of(hidden_low):
+        parts = front_terms(owners, hidden_low, down_all)
+        return list(zip(parts[0::2], parts[1::2]))
+
     if square:
-        via_x, via_y = scatter_first(ffn_terms)
-        both_terms = contract_rows(normed_two, d_both).astype(BF)
-        via_x, via_y, both_terms = lax.optimization_barrier((via_x, via_y, both_terms))
-        sums = scatter_last(ffn_terms, via_x, via_y)
+        (across, for_x), d_both = ffn(owners[:2], None)
+        via_x, via_y, ((for_y,), d_both) = barrier((to_x(across[0]), to_y(across[1]), ffn(owners[2:3], d_both)))
+        x_low, y_high, x_high, y_low, ((own,), d_both) = barrier(
+            (
+                to_x(after(for_x[0], via_x)),
+                to_y(for_y[1]),
+                add_low(for_x[1], via_y),
+                add_low(for_y[0], via_x),
+                ffn(owners[3:], d_both),
+            )
+        )
+        x_high, y_low, gate_terms = barrier(
+            (to_x(x_high), to_y(y_low), contract_rows(normed_two, d_both[:, :units]).astype(BF))
+        )
+        gate_grad = wide_sums(gate_terms, 0)
+        y_high = after(y_high, down_grad)
+        d_hidden_rows, gain_two_terms = dh_of([own, (x_low, x_high), (y_low, y_high)])
+
+        def beside_dh():
+            up_terms = contract_rows(after(normed_two, d_hidden_rows), d_both[:, units:]).astype(BF)
+            return up_terms, out_terms_of(after(hidden_low, up_terms)), unpacked(after(in_all, d_hidden_rows))
+
+        dh_pieces, (up_terms, out_parts, out_rows), _ = gather_pieces(
+            d_hidden_rows, 0, True, (beside_dh, lambda _: ())
+        )
+        up_grad = wide_sums(up_terms, 0)
+        out_parts, gate_grad = barrier((out_parts, gate_grad))
+        out_first = [tuple(after(half, *dh_pieces[3:]) for half in part) for part in out_parts]
+        out_via_x, out_via_y, out_x_low, out_y_high, (one_parts, d_flat, kernel_grad, d_hidden_low) = barrier(
+            (
+                to_x(out_first[0][0]),
+                to_y(out_first[0][1]),
+                to_x(out_first[1][0]),
+                to_y(out_first[2][1]),
+                mixer(dh_pieces, out_rows),
+            )
+        )
+        via_x, via_y, in_terms = barrier(
+            (to_x(one_parts[0][0]), to_y(one_parts[0][1]), contract_rows(normed_one, d_flat).astype(BF))
+        )
+        x_low, y_high, x_high, y_low, out_x_high, out_y_low, out_terms, in_terms, up_grad = barrier(
+            (
+                to_x(after(one_parts[1][0], via_x)),
+                to_y(after(one_parts[2][1], via_y)),
+                add_low(one_parts[1][1], via_y),
+                add_low(one_parts[2][0], via_x),
+                add_low(out_parts[1][1], out_via_y),
+                add_low(out_parts[2][0], out_via_x),
+                contract_rows(after(d_hidden_low, in_terms), mixer_low).astype(BF),
+                in_terms,
+                up_grad,
+            )
+        )
+        in_grad = wide_sums(in_terms, 0)
+        x_high, y_low, line = barrier((to_x(x_high), to_y(y_low), line_start(out_terms, core)))
+        d_normed_one = total_of([one_parts[3], (x_low, x_high), (y_low, y_high)])
+        my_gain = lax.dynamic_slice_in_dim(norm1_gain, offset, part_width)
+        inner_one = jnp.sum(d_normed_one * my_gain * tokens.astype(F32), axis=1).reshape(-1, 128)
+        out_x_high, out_y_low, inner_one, line = barrier(
+            (
+                to_x(after(out_x_high, x_low, x_high)),
+                to_y(after(out_y_low, y_low, y_high)),
+                inner_one + to_x(inner_one),
+                line_step(line, 2),
+            )
+        )
+        inner_one = inner_one + to_y(inner_one)
+        out_grad = line_end(line).T
+        ffn_out = total_of([out_parts[3], (out_x_low, out_x_high), (out_y_low, out_y_high)])
     else:
-        both_terms = contract_rows(normed_two, d_both).astype(BF)
-        sums = [tuple(halves(scatter_plain(ffn_terms, 0), 1))]
-    both_grad = wide_sums(after(both_terms, down_grad), 0)
-    d_hidden_rows, gain_two_terms = hidden_back(me_s, sums, hidden, scale_two, grad_full, gain_two)
-    dh_pieces, out_parts, _ = gather_pieces(
-        d_hidden_rows, 0, square, (lambda: tuple(front_terms(owners, hidden_low, down_all)), lambda _: ())
-    )
-    *one_parts, d_flat, kernel_grad, d_hidden_low = mixer_back(
-        owners, dh_pieces, out_rows, mixed, filtered, kernel, masks, pack_all
-    )
-    one_parts = list(zip(one_parts[0::2], one_parts[1::2]))
-    out_parts = list(zip(out_parts[0::2], out_parts[1::2]))
-    if square:
-        via_x, via_y = scatter_first(one_parts)
-        in_terms = contract_rows(normed_one, d_flat).astype(BF)
-        via_x, via_y, in_terms = lax.optimization_barrier((via_x, via_y, in_terms))
-        one_sums = scatter_last(one_parts, via_x, via_y)
-        out_terms = contract_rows(mixer_low, after(d_hidden_low, in_terms)).astype(BF)
-        d_normed_one = total_of(one_sums)
-        via_x, via_y = scatter_first([tuple(after(out_parts[0], d_normed_one))] + out_parts[1:])
-        ffn_out = total_of(scatter_last(out_parts, via_x, via_y))
-        in_grad = wide_sums(after(in_terms, both_grad), 0)
-        out_grad = wide_sums(after(out_terms, in_grad, ffn_out), 1)
-    else:
-        in_terms = contract_rows(normed_one, d_flat).astype(BF)
-        out_terms = contract_rows(mixer_low, d_hidden_low).astype(BF)
+        ffn_terms, d_both = ffn(owners, None)
+        both_grad = wide_sums(contract_rows(normed_two, d_both), 0)
+        gate_grad, up_grad = both_grad[:, :units], both_grad[:, units:]
+        d_hidden_rows, gain_two_terms = dh_of([tuple(halves(scatter_plain(ffn_terms, 0), 1))])
+        one_parts, d_flat, kernel_grad, d_hidden_low = mixer(gather_pieces(d_hidden_rows, 0, False)[0], out_rows)
         d_normed_one = scatter_plain(one_parts, 1)
-        ffn_out = scatter_plain(out_parts, 1)
-        in_grad, out_grad = wide_sums(in_terms, 0), wide_sums(out_terms, 1)
-    gate_grad, up_grad = both_grad[:, :units], both_grad[:, units:]
+        ffn_out = scatter_plain(out_terms_of(hidden_low), 1)
+        in_grad = wide_sums(contract_rows(normed_one, d_flat), 0)
+        out_grad = wide_sums(contract_rows(mixer_low, d_hidden_low), 1)
     in_grad = jnp.stack([in_grad[:, k * part_width : (k + 1) * part_width] for k in range(3)], axis=1)
     block_out = (lax.dynamic_slice_in_dim(hidden, offset, part_width, 1) + ffn_out).astype(BF)
 
     my_gain = lax.dynamic_slice_in_dim(norm1_gain, offset, part_width)
     x_part = tokens.astype(F32)
     scaled_one = d_normed_one * my_gain
-    inner_one = narrow_total(jnp.sum(scaled_one * x_part, axis=1).reshape(-1, 128), square)
+    if not square:
+        inner_one = lax.psum(jnp.sum(scaled_one * x_part, axis=1), "narrow")
     inner_one = inner_one.reshape(row_count, 1) / full_width
     tokens_grad = (
         lax.dynamic_slice_in_dim(d_hidden_low, offset, part_width, 1).astype(F32)
         + scale_one * (scaled_one - x_part * scale_one * scale_one * inner_one)
     ).astype(BF)
     gain_one_grad = jnp.sum(d_normed_one * x_part * scale_one, axis=0)
-    gain_two_terms = narrow_total(gain_two_terms.reshape(size, part_width), square)
+    gain_two_terms = narrow_total(after(gain_two_terms, ffn_out).reshape(size, part_width), square)
     gain_two_terms = lax.dynamic_slice_in_dim(gain_two_terms, me, 1, 0)
     small = wide_total(jnp.concatenate([gain_one_grad[None, :], gain_two_terms, kernel_grad], axis=0), square)
     gain_one_grad, gain_two_grad, kernel_grad = small[0], small[1], small[2:]
@@ -628,13 +756,13 @@
         block_out,
         tokens_grad,
         gain_one_grad,
-        in_grad,
+        in_grad.astype(F32),
         kernel_grad,
-        out_grad,
+        out_grad.astype(F32),
         gain_two_grad,
-        gate_grad,
-        up_grad,
-        down_grad,
+        gate_grad.astype(F32),
+        up_grad.astype(F32),
+        down_grad.astype(F32),
     )
 
 

time: 842 us -> 749 us (0.89)
  waiting for transfers between devices: 351 us -> 215 us
  Pallas kernels: 255 us -> 267 us
  starting transfers between devices: 46.5 us -> 57.2 us
  matrix products: 91.7 us -> 101 us
    ppermute x21 -> x20, waiting for transfers between devices: 198 us -> 107 us  [to_y(): return lax.ppermute(values, 'narrow', ALONG_Y)]
    ppermute x21 -> x20, waiting for transfers between devices: 142 us -> 74.3 us  [to_x(): return lax.ppermute(values, 'narrow', ALONG_X)]
    ppermute x1 -> x14, starting transfers between devices: 0.07 us -> 14.7 us  [the longest x3 6.94 us: line_step(): lax.ppermute(with_own(right, z + 4 - step), 'wide', [(w, w + 2) for w in...]
    reduce_scatter x4, waiting for transfers between devices: 2.53 us -> 15.2 us  [wide_sums(): lax.psum_scatter(terms.astype(BF), 'wide', scatter_dimension=axis, tiled=...]
    ppermute x3, waiting for transfers between devices: 1.51 us -> 13.4 us  [wide_total(): lax.ppermute(values, 'wide', [(i, i ^ bit) for i in range(lax.axis_size('...]
    pallas_call x8 -> x10, Pallas kernels: 255 us -> 267 us  [run(): pl.pallas_call(kernel, grid_spec=pltpu.PrefetchScalarGridSpec(num_scalar_...]
    dot_general x4 -> x5, matrix products: 91.7 us -> 101 us  [contract_rows(): lax.dot_general(left, right, (((0,), (0,)), ((), ())), preferred_element_...]
    ppermute x21 -> x20, starting transfers between devices: 23.5 us -> 19.7 us  [to_y(): return lax.ppermute(values, 'narrow', ALONG_Y)]
  transfers between devices with their start and end apart: 53 -> 64, of which waited for: 31 -> 21; matrix products, arithmetic and copies ran while one was open for 18% -> 23% of each run, Pallas kernels for 30% -> 36%
where the time goes in v2:
time: 749 us; the launch traced here: 742 us
  Pallas kernels  267 us (36%)
  waiting for transfers between devices  215 us (29%)
  matrix products  101 us (13%)
  starting transfers between devices  57.2 us (8%)
  other arithmetic  48.4 us (6%)
  local copies, waits for them, and re-layouts  38.8 us (5%)
  between operations  15.5 us (2%)
    pallas_call x10, Pallas kernels, run(): pl.pallas_call(kernel, grid_spec=pltpu.PrefetchScalarGridSpec(num_scalar_...  267 us
    ppermute x20, waiting for transfers between devices, to_y(): return lax.ppermute(values, 'narrow', ALONG_Y)  107 us
    dot_general x5, matrix products, contract_rows(): lax.dot_general(left, right, (((0,), (0,)), ((), ())), preferred_element_...  101 us
    ppermute x20, waiting for transfers between devices, to_x(): return lax.ppermute(values, 'narrow', ALONG_X)  74.3 us
    ppermute x20, starting transfers between devices, to_x(): return lax.ppermute(values, 'narrow', ALONG_X)  20.7 us
    ppermute x20, starting transfers between devices, to_y(): return lax.ppermute(values, 'narrow', ALONG_Y)  19.7 us
    unnamed x104, local copies, waits for them, and re-layouts  15.6 us
    reduce_scatter x4, waiting for transfers between devices, wide_sums(): lax.psum_scatter(terms.astype(BF), 'wide', scatter_dimension=axis, tiled=...  15.2 us
  transfers between devices with their start and end apart: 64, of which 21 were waited for; matrix products, arithmetic and copies ran while one was open for 23% of the time, Pallas kernels for 36%

profile of v2, /device:TPU:0, one launch (start us, length us, event | category | flops | bytes accessed | tf_op | source)
XLA Modules:
  0.0 742.2 jit_solution(1552771375913200132)
XLA Ops:
  13.1 3.0 collective-permute-start.3
  17.6 44.4 %collective-permute-done.3.refs_2_ = bf16[2048,512]{1,0:T(8,128)(2,1)S(1)} collective-permute-done((bf16[2048,512]{1,0:T(8,128)(2,1)}, bf16[2048,512]{1,0:T(8,128)(2,1)S(1)}, u32[]{:S(2)}, u32[]{:S(2)}) %collective-permute-start.3) | collective-permute-done | bytes 2097184 | tf_op jit(solution)/shard_map/ppermute | solution.py:41
  68.4 20.3 %collective-permute-done.4.refs_3_ = bf16[2048,256]{1,0:T(8,128)(2,1)} collective-permute-done((bf16[2048,256]{1,0:T(8,128)(2,1)}, bf16[2048,256]{1,0:T(8,128)(2,1)}, u32[]{:S(2)}, u32[]{:S(2)}) %collective-permute-start.4) | collective-permute-done | bytes 1048608 | tf_op jit(solution)/shard_map/ppermute | solution.py:37
  94.7 3.3 all-gather.4.cloned.1.call-done.refs_6_.refs_10_
  102.3 27.6 %shard_map.186 = (bf16[2048,2048]{1,0:T(8,128)(2,1)}, bf16[2048,2048]{1,0:T(8,128)(2,1)}, f32[2048,1536]{1,0:T(8,128)}, f32[2048,512]{1,0:T(8,128)}, bf16[2048,512]{1,0:T(8,128)(2,1)}, /*index=5*/f32[2048,1]{1,0:T(8,128)}) custom-call(s32[1]{0:T(128)} %bitcast.4.me_ref._, bf16[2048,512]{1,0:T(8,128)(2,1)} %refs_0_.2, bf16[2048,512]{1,0:T(8,128)(2,1)} %copy-done.24, ...), custom_call_target="tpu_custom_call" | custom-call | flops 12884901888 | bytes 52467712 | tf_op jit(solution)/shard_map/pallas_call | solution.py:80
  135.9 44.9 %collective-permute-done.8.refs_2_ = bf16[2048,512]{1,0:T(8,128)(2,1)S(1)} collective-permute-done((bf16[2048,512]{1,0:T(8,128)(2,1)}, bf16[2048,512]{1,0:T(8,128)(2,1)S(1)}, u32[]{:S(2)}, u32[]{:S(2)}) %collective-permute-start.8) | collective-permute-done | bytes 2097184 | tf_op jit(solution)/shard_map/ppermute | solution.py:41
  182.0 10.1 %collective-permute-done.12.refs_9_ = bf16[512,512]{1,0:T(8,128)(2,1)S(1)} collective-permute-done((bf16[512,512]{1,0:T(8,128)(2,1)S(1)}, bf16[512,512]{1,0:T(8,128)(2,1)S(1)}, u32[]{:S(2)}, u32[]{:S(2)}) %collective-permute-start.12) | collective-permute-done | bytes 524320 | tf_op jit(solution)/shard_map/ppermute | solution.py:41
  192.3 25.6 %collective-permute-done.11.refs_8_ = bf16[512,512]{1,0:T(8,128)(2,1)S(1)} collective-permute-done((bf16[512,512]{1,0:T(8,128)(2,1)S(1)}, bf16[512,512]{1,0:T(8,128)(2,1)S(1)}, u32[]{:S(2)}, u32[]{:S(2)}) %collective-permute-start.11) | collective-permute-done | bytes 524320 | tf_op jit(solution)/shard_map/ppermute | solution.py:37
  221.4 2.6 collective-permute-start.20
  225.7 28.6 %shard_map.187 = (f32[2048,2048]{1,0:T(8,128)}, bf16[2048,2048]{1,0:T(8,128)(2,1)}, f32[2048,1]{1,0:T(8,128)}) custom-call(s32[1]{0:T(128)} %bitcast.core_ref, bf16[2048,512]{1,0:T(8,128)(2,1)} %get-tuple-element.190.refs_0_, bf16[2048,512]{1,0:T(8,128)(2,1)} %copy-done.26, bf16[2048,512]{1,0:T(8,128)(2,1)} %copy-done.25, bf16[2048,256]{1,0:T(8,128)(2,1)} %copy-done.41, ...), custom_call_target="tpu_custom_call" | custom-call | flops 17179869184 | bytes 50348032 | tf_op jit(solution)/shard_map/pallas_call | solution.py:80
  254.3 48.0 %shard_map.188 = (bf16[2048,2048]{1,0:T(8,128)(2,1)}, bf16[2048,2048]{1,0:T(8,128)(2,1)}, bf16[2048,2048]{1,0:T(8,128)(2,1)}) custom-call(s32[1]{0:T(128)} %bitcast.4.me_ref._, bf16[2048,2048]{1,0:T(8,128)(2,1)} %get-tuple-element.249.n_ref, bf16[2048,4096]{1,0:T(8,128)(2,1)} %all-gather.6.cloned.1.call-done.w_ref.wg_ref.wu_ref), custom_call_target="tpu_custom_call" | custom-call | flops 34359738368 | bytes 50331648 | tf_op jit(solution)/shard_map/pallas_call | solution.py:80
  303.6 7.1 shard_map.189.g_ref.refs_8_
  310.7 24.1 %convolution_convert_fusion = bf16[2048,2048]{1,0:T(8,128)(2,1)} fusion(bf16[2048,2048]{1,0:T(8,128)(2,1)} %get-tuple-element.250.l_ref, bf16[2048,2048]{1,0:T(8,128)(2,1)} %shard_map.189.g_ref.refs_8_), kind=kOutput, calls=%fused_computation.6 | convolution fusion | flops 17184063488 | bytes 25165824 | tf_op jit(solution)/shard_map/dot_general | solution.py:19
  335.4 41.5 %shard_map.190 = (bf16[512,1024]{1,0:T(8,128)(2,1)}, bf16[512,1024]{1,0:T(8,128)(2,1)}, bf16[512,1024]{1,0:T(8,128)(2,1)}, bf16[512,1024]{1,0:T(8,128)(2,1)}, bf16[2048,4096]{1,0:T(8,128)(2,1)}) custom-call(s32[2]{0:T(128)} %pad_add_fusion.1._, bf16[2048,2048]{1,0:T(8,128)(2,1)} %shard_map.189.g_ref.refs_8_, bf16[2048,2048]{1,0:T(8,128)(2,1)} %get-tuple-element.217.a_ref, ...), custom_call_target="tpu_custom_call" | custom-call | flops 25769803776 | bytes 88080384 | tf_op jit(solution)/shard_map/pallas_call | solution.py:80
  377.7 23.9 %shard_map.191 = (bf16[512,1024]{1,0:T(8,128)(2,1)}, bf16[512,1024]{1,0:T(8,128)(2,1)}, bf16[2048,4096]{1,0:T(8,128)(2,1)}) custom-call(s32[1]{0:T(128)} %bitcast.9._, bf16[2048,2048]{1,0:T(8,128)(2,1)} %shard_map.189.g_ref.refs_8_, bf16[2048,2048]{1,0:T(8,128)(2,1)} %get-tuple-element.217.a_ref, ...), custom_call_target="tpu_custom_call", output_to_operand_aliasing={{2}: (7, {})} | custom-call | flops 12884901888 | bytes 102760448 | tf_op jit(solution)/shard_map/pallas_call | solution.py:80
  404.8 3.5 add_convert_fusion.5
  408.4 23.9 %shard_map.192 = (bf16[512,1024]{1,0:T(8,128)(2,1)}, bf16[512,1024]{1,0:T(8,128)(2,1)}, bf16[2048,4096]{1,0:T(8,128)(2,1)}) custom-call(s32[1]{0:T(128)} %bitcast.4.me_ref._, bf16[2048,2048]{1,0:T(8,128)(2,1)} %shard_map.189.g_ref.refs_8_, bf16[2048,2048]{1,0:T(8,128)(2,1)} %get-tuple-element.217.a_ref, ...), custom_call_target="tpu_custom_call", output_to_operand_aliasing={{2}: (7, {})} | custom-call | flops 12884901888 | bytes 102760448 | tf_op jit(solution)/shard_map/pallas_call | solution.py:80
  433.3 23.8 %fusion.4 = bf16[2048,2048]{1,0:T(8,128)(2,1)} fusion(bf16[2048,2048]{1,0:T(8,128)(2,1)} %get-tuple-element.249.n_ref, bf16[2048,4096]{1,0:T(8,128)(2,1)} %get-tuple-element.242), kind=kOutput, calls=%fused_computation.4 | convolution fusion | flops 17184063488 | bytes 25165824 | tf_op jit(solution)/shard_map/dot_general | solution.py:19
  458.7 8.5 %shard_map.193 = (bf16[512,2048]{1,0:T(8,128)(2,1)}, f32[1,2048]{1,0:T(1,128)}) custom-call(s32[1]{0:T(128)} %bitcast.4.me_ref._, bf16[512,1024]{1,0:T(8,128)(2,1)} %get-tuple-element.237.refs_0_, bf16[512,1024]{1,0:T(8,128)(2,1)} %get-tuple-element.238.refs_1_, bf16[512,1024]{1,0:T(8,128)(2,1)} %copy-done.15, bf16[512,1024]{1,0:T(8,128)(2,1)} %copy-done.18, ...), custom_call_target="tpu_custom_call" | custom-call | bytes 33579008 | tf_op jit(solution)/shard_map/pallas_call | solution.py:80
  470.5 23.9 %fusion.7 = bf16[2048,2048]{1,0:T(8,128)(2,1)} fusion(bf16[2048,2048]{1,0:T(8,128)(2,1)} %get-tuple-element.249.n_ref, bf16[2048,4096]{1,0:T(8,128)(2,1)} %get-tuple-element.242), kind=kOutput, calls=%fused_computation.5 | convolution fusion | flops 17184063488 | bytes 25165824 | tf_op jit(solution)/shard_map/dot_general | solution.py:19
  494.4 3.1 slice.97
  497.4 2.6 reshape.66
  501.2 2.0 copy.36
  503.2 24.1 %shard_map.194 = (bf16[2048,256]{1,0:T(8,128)(2,1)}, bf16[2048,256]{1,0:T(8,128)(2,1)}, bf16[2048,256]{1,0:T(8,128)(2,1)}, bf16[2048,256]{1,0:T(8,128)(2,1)}, bf...) custom-call(s32[4]{0:T(128)} %pad_add_fusion.2.own_ref, ...), custom_call_target="tpu_custom_call" | custom-call | flops 17179869184 | bytes 25165824 | tf_op jit(solution)/shard_map/pallas_call | solution.py:80
  531.0 15.2 %reduce-scatter.7.cloned.1.call-done = bf16[256,2048]{1,0:T(8,128)(2,1)} async-done(((bf16[2048,2048]{1,0:T(8,128)(2,1)}), bf16[256,2048]{1,0:T(8,128)(2,1)}) %reduce-scatter.7.cloned.1.call-update) | async-done | bytes 1048592 | tf_op jit(solution)/shard_map/reduce_scatter | solution.py:487
  546.2 5.7 collective-permute-done.30.refs_4_
  555.2 2.0 collective-permute-start.33
  557.3 33.3 %shard_map.195 = (bf16[2048,256]{1,0:T(8,128)(2,1)}, bf16[2048,256]{1,0:T(8,128)(2,1)}, bf16[2048,256]{1,0:T(8,128)(2,1)}, bf16[2048,256]{1,0:T(8,128)(2,1)}, bf...) custom-call(s32[4]{0:T(128)} %pad_add_fusion.2.own_ref, ...), custom_call_target="tpu_custom_call" | custom-call | flops 17179869184 | bytes 58748928 | tf_op jit(solution)/shard_map/pallas_call | solution.py:80
  590.6 8.1 %collective-permute-done.33 = bf16[2048,256]{1,0:T(8,128)(2,1)} collective-permute-done((bf16[2048,256]{1,0:T(8,128)(2,1)}, bf16[2048,256]{1,0:T(8,128)(2,1)}, u32[]{:S(2)}, u32[]{:S(2)}) %collective-permute-start.33) | collective-permute-done | bytes 1048608 | tf_op jit(solution)/shard_map/ppermute | solution.py:37
  601.1 19.3 %convolution_convert_fusion.1 = bf16[2048,1536]{1,0:T(8,128)(2,1)} fusion(bf16[2048,2048]{1,0:T(8,128)(2,1)} %get-tuple-element.300, bf16[2048,1536]{1,0:T(8,128)(2,1)} %get-tuple-element.301), kind=kOutput, calls=%fused_computation.7 | convolution fusion | flops 12888047616 | bytes 20971520 | tf_op jit(solution)/shard_map/dot_general | solution.py:19
  621.6 2.9 add_convert_fusion.2
  626.7 9.8 %convolution_convert_fusion.2 = bf16[2048,512]{1,0:T(8,128)(2,1)} fusion(bf16[2048,2048]{1,0:T(8,128)(2,1)} %get-tuple-element.315, bf16[2048,512]{1,0:T(8,128)(2,1)S(1)} %copy-done.35), kind=kOutput, calls=%fused_computation.23 | convolution fusion | flops 4296015872 | bytes 12582912 | tf_op jit(solution)/shard_map/dot_general | solution.py:19
  636.5 2.5 add_convert_fusion.3
  639.0 2.5 add_convert_fusion.4
  650.7 1.8 collective-permute-start.42
  654.9 16.6 %collective-permute-done.50 = f32[4,512]{1,0:T(4,128)S(1)} collective-permute-done((f32[4,512]{1,0:T(4,128)S(1)}, f32[4,512]{1,0:T(4,128)S(1)}, u32[]{:S(2)}, u32[]{:S(2)}) %collective-permute-start.50) | collective-permute-done | bytes 8224 | tf_op jit(solution)/shard_map/ppermute | solution.py:37
  677.5 2.2 convert_add_fusion.3
  679.7 2.2 convert_add_fusion.4
  685.2 2.8 convert_element_type.270
  688.0 2.9 convert_element_type.268
  694.3 3.3 collective-permute-done.53
  697.6 1.9 collective-permute-start.47
  702.3 10.1 %collective-permute-done.54 = f32[5,512]{1,0:T(8,128)S(1)} collective-permute-done((f32[5,512]{1,0:T(8,128)S(1)}, f32[5,512]{1,0:T(8,128)S(1)}, u32[]{:S(2)}, u32[]{:S(2)}) %collective-permute-start.54) | collective-permute-done | bytes 10272 | tf_op jit(solution)/shard_map/ppermute | solution.py:501
  715.0 3.2 collective-permute-start.55
  719.5 1.9 convert_add_fusion.2
  721.5 1.9 convert_add_fusion.1
  723.4 4.3 add_convert_fusion
  727.8 3.8 fusion.16
  (270 shorter events, 96.1 us)
Async XLA Ops:
  7.2 90.8 %all-gather.4.cloned.1.call-start = ((), (), s32[]{:S(2)}) async-start(), calls=%async_computation.4 | async-start | bytes 9437184 | tf_op jit(solution)/shard_map/all_gather | solution.py:483
  13.0 241.2 %all-gather.6.cloned.1.call-start = ((), (), s32[]{:S(2)}) async-start(), calls=%async_computation.5 | async-start | bytes 18874368 | tf_op jit(solution)/shard_map/all_gather | solution.py:483
  13.1 48.9 %collective-permute-start.3 = (bf16[2048,512]{1,0:T(8,128)(2,1)}, bf16[2048,512]{1,0:T(8,128)(2,1)S(1)}, u32[]{:S(2)}, u32[]{:S(2)}) collective-permute-start(bf16[2048,512]{1,0:T(8,128)(2,1)} %refs_0_.2), channel_id=1, source_target_pairs={{0,2},{2,0},{1,3},{3,1},{4,6},{6,4},{5,7},{7,5},{8,10},{10,8},{9,1... | collective-permute-start | bytes 6291464 | tf_op jit(solution)/shard_map/ppermute | solution.py:41
  16.1 47.3 %collective-permute-start.2 = (bf16[2048,512]{1,0:T(8,128)(2,1)}, bf16[2048,512]{1,0:T(8,128)(2,1)S(1)}, u32[]{:S(2)}, u32[]{:S(2)}) collective-permute-start(bf16[2048,512]{1,0:T(8,128)(2,1)} %refs_0_.2), channel_id=1, source_target_pairs={{0,1},{1,0},{2,3},{3,2},{4,5},{5,4},{6,7},{7,6},{8,9},{9,8},{10,11... | collective-permute-start | bytes 6291464 | tf_op jit(solution)/shard_map/ppermute | solution.py:37
  64.6 24.1 %collective-permute-start.4 = (bf16[2048,256]{1,0:T(8,128)(2,1)}, bf16[2048,256]{1,0:T(8,128)(2,1)}, u32[]{:S(2)}, u32[]{:S(2)}) collective-permute-start(bf16[2048,256]{1,0:T(8,128)(2,1)} %slice.86), channel_id=1, source_target_pairs={{0,1},{1,0},{2,3},{3,2},{4,5},{5,4},{6,7},{7,6},{8,9},{9,8},{10,11... | collective-permute-start | bytes 3145736 | tf_op jit(solution)/shard_map/ppermute | solution.py:37
  66.1 23.6 %collective-permute-start.5 = (bf16[2048,256]{1,0:T(8,128)(2,1)S(1)}, bf16[2048,256]{1,0:T(8,128)(2,1)}, u32[]{:S(2)}, u32[]{:S(2)}) collective-permute-start(bf16[2048,256]{1,0:T(8,128)(2,1)S(1)} %slice.87), channel_id=1, source_target_pairs={{0,2},{2,0},{1,3},{3,1},{4,6},{6,4},{5,7},{7,5},{8,10},{10,8},{9,1... | collective-permute-start | bytes 3145736 | tf_op jit(solution)/shard_map/ppermute | solution.py:41
  89.7 245.7 %all-gather.8.cloned.1.call-start = ((), (), s32[]{:S(2)}) async-start(), calls=%async_computation.6 | async-start | bytes 9437184 | tf_op jit(solution)/shard_map/all_gather | solution.py:483
  93.0 36.9 %collective-permute-start.6 = (bf16[2048,128]{1,0:T(8,128)(2,1)}, bf16[2048,128]{1,0:T(8,128)(2,1)}, u32[]{:S(2)}, u32[]{:S(2)}) collective-permute-start(bf16[2048,128]{1,0:T(8,128)(2,1)} %slice.85), channel_id=1, source_target_pairs={{0,3},{3,0},{1,2},{2,1},{4,7},{7,4},{5,6},{6,5},{8,11},{11,8},{9,1... | collective-permute-start | bytes 1572872 | tf_op jit(solution)/shard_map/ppermute | solution.py:45
  99.3 30.6 %collective-permute-start.1 = (bf16[1024,512]{1,0:T(8,128)(2,1)S(1)}, bf16[1024,512]{1,0:T(8,128)(2,1)S(1)}, u32[]{:S(2)}, u32[]{:S(2)}) collective-permute-start(bf16[1024,512]{1,0:T(8,128)(2,1)S(1)} %constant_dynamic-slice_fusion.5.refs_5_), channel_id=1, source_target_pairs={{0,2},{2,0},{1,3},{3,1},{4,6},{6,4},{5,7},{7,5},{8,10},{10,8},{9,1... | collective-permute-start | bytes 3145736 | tf_op jit(solution)/shard_map/ppermute | solution.py:41
  100.8 29.1 %collective-permute-start = (bf16[1024,512]{1,0:T(8,128)(2,1)S(1)}, bf16[1024,512]{1,0:T(8,128)(2,1)S(1)}, u32[]{:S(2)}, u32[]{:S(2)}) collective-permute-start(bf16[1024,512]{1,0:T(8,128)(2,1)S(1)} %constant_dynamic-slice_fusion.5.refs_5_), channel_id=1, source_target_pairs={{0,1},{1,0},{2,3},{3,2},{4,5},{5,4},{6,7},{7,6},{8,9},{9,8},{10,11... | collective-permute-start | bytes 3145736 | tf_op jit(solution)/shard_map/ppermute | solution.py:37
  131.9 326.8 %reduce-scatter.5.cloned.1.call-start = ((), (), s32[]{:S(2)}) async-start(), calls=%async_computation.7 | async-start | bytes 9437184 | tf_op jit(solution)/shard_map/reduce_scatter | solution.py:487
  132.0 48.8 %collective-permute-start.8 = (bf16[2048,512]{1,0:T(8,128)(2,1)}, bf16[2048,512]{1,0:T(8,128)(2,1)S(1)}, u32[]{:S(2)}, u32[]{:S(2)}) collective-permute-start(bf16[2048,512]{1,0:T(8,128)(2,1)} %get-tuple-element.190.refs_0_), channel_id=1, source_target_pairs={{0,2},{2,0},{1,3},{3,1},{4,6},{6,4},{5,7},{7,5},{8,10},{10,8},{9,1... | collective-permute-start | bytes 6291464 | tf_op jit(solution)/shard_map/ppermute | solution.py:41
  132.3 48.6 %collective-permute-start.7 = (bf16[2048,512]{1,0:T(8,128)(2,1)}, bf16[2048,512]{1,0:T(8,128)(2,1)S(1)}, u32[]{:S(2)}, u32[]{:S(2)}) collective-permute-start(bf16[2048,512]{1,0:T(8,128)(2,1)} %get-tuple-element.190.refs_0_), channel_id=1, source_target_pairs={{0,1},{1,0},{2,3},{3,2},{4,5},{5,4},{6,7},{7,6},{8,9},{9,8},{10,11... | collective-permute-start | bytes 6291464 | tf_op jit(solution)/shard_map/ppermute | solution.py:37
  133.0 48.3 %collective-permute-start.13 = (bf16[1024,512]{1,0:T(8,128)(2,1)S(1)}, bf16[1024,512]{1,0:T(8,128)(2,1)S(1)}, u32[]{:S(2)}, u32[]{:S(2)}) collective-permute-start(bf16[1024,512]{1,0:T(8,128)(2,1)S(1)} %constant_dynamic-slice_fusion.5.refs_5_), channel_id=1, source_target_pairs={{0,4},{4,0},{8,12},{12,8},{16,20},{20,16},{24,28},{28,24},{1,5},{5... | collective-permute-start | bytes 3145736 | tf_op jit(solution)/shard_map/ppermute | solution.py:506
  134.1 83.8 %collective-permute-start.14 = (bf16[1024,512]{1,0:T(8,128)(2,1)}, bf16[1024,512]{1,0:T(8,128)(2,1)S(1)}, u32[]{:S(2)}, u32[]{:S(2)}) collective-permute-start(bf16[1024,512]{1,0:T(8,128)(2,1)} %copy-done.29), channel_id=1, source_target_pairs={{0,4},{4,0},{8,12},{12,8},{16,20},{20,16},{24,28},{28,24},{1,5},{5... | collective-permute-start | bytes 3145736 | tf_op jit(solution)/shard_map/ppermute | solution.py:506
  134.6 57.4 %collective-permute-start.12 = (bf16[512,512]{1,0:T(8,128)(2,1)S(1)}, bf16[512,512]{1,0:T(8,128)(2,1)S(1)}, u32[]{:S(2)}, u32[]{:S(2)}) collective-permute-start(bf16[512,512]{1,0:T(8,128)(2,1)S(1)} %slice.93), channel_id=1, source_target_pairs={{0,2},{2,0},{1,3},{3,1},{4,6},{6,4},{5,7},{7,5},{8,10},{10,8},{9,1... | collective-permute-start | bytes 1572872 | tf_op jit(solution)/shard_map/ppermute | solution.py:41
  180.8 37.0 %collective-permute-start.15 = (bf16[1024,512]{1,0:T(8,128)(2,1)}, bf16[1024,512]{1,0:T(8,128)(2,1)S(1)}, u32[]{:S(2)}, u32[]{:S(2)}) collective-permute-start(bf16[1024,512]{1,0:T(8,128)(2,1)} %copy-done.27), channel_id=1, source_target_pairs={{0,4},{4,0},{8,12},{12,8},{16,20},{20,16},{24,28},{28,24},{1,5},{5... | collective-permute-start | bytes 3145736 | tf_op jit(solution)/shard_map/ppermute | solution.py:506
  181.0 36.9 %collective-permute-start.9 = (bf16[2048,256]{1,0:T(8,128)(2,1)S(1)}, bf16[2048,256]{1,0:T(8,128)(2,1)S(1)}, u32[]{:S(2)}, u32[]{:S(2)}) collective-permute-start(bf16[2048,256]{1,0:T(8,128)(2,1)S(1)} %slice.90), channel_id=1, source_target_pairs={{0,1},{1,0},{2,3},{3,2},{4,5},{5,4},{6,7},{7,6},{8,9},{9,8},{10,11... | collective-permute-start | bytes 3145736 | tf_op jit(solution)/shard_map/ppermute | solution.py:37
  181.3 36.6 %collective-permute-start.10 = (bf16[2048,256]{1,0:T(8,128)(2,1)S(1)}, bf16[2048,256]{1,0:T(8,128)(2,1)S(1)}, u32[]{:S(2)}, u32[]{:S(2)}) collective-permute-start(bf16[2048,256]{1,0:T(8,128)(2,1)S(1)} %slice.91), channel_id=1, source_target_pairs={{0,2},{2,0},{1,3},{3,1},{4,6},{6,4},{5,7},{7,5},{8,10},{10,8},{9,1... | collective-permute-start | bytes 3145736 | tf_op jit(solution)/shard_map/ppermute | solution.py:41
  192.1 25.8 %collective-permute-start.11 = (bf16[512,512]{1,0:T(8,128)(2,1)S(1)}, bf16[512,512]{1,0:T(8,128)(2,1)S(1)}, u32[]{:S(2)}, u32[]{:S(2)}) collective-permute-start(bf16[512,512]{1,0:T(8,128)(2,1)S(1)} %slice.92), channel_id=1, source_target_pairs={{0,1},{1,0},{2,3},{3,2},{4,5},{5,4},{6,7},{7,6},{8,9},{9,8},{10,11... | collective-permute-start | bytes 1572872 | tf_op jit(solution)/shard_map/ppermute | solution.py:37
  220.6 83.0 %collective-permute-start.19 = (bf16[2048,512]{1,0:T(8,128)(2,1)S(1)}, bf16[2048,512]{1,0:T(8,128)(2,1)}, u32[]{:S(2)}, u32[]{:S(2)}) collective-permute-start(bf16[2048,512]{1,0:T(8,128)(2,1)S(1)} %copy-done.4), channel_id=1, source_target_pairs={{0,2},{2,0},{1,3},{3,1},{4,6},{6,4},{5,7},{7,5},{8,10},{10,8},{9,1... | collective-permute-start | bytes 6291464 | tf_op jit(solution)/shard_map/ppermute | solution.py:41
  220.8 82.8 %collective-permute-start.18 = (bf16[2048,512]{1,0:T(8,128)(2,1)S(1)}, bf16[2048,512]{1,0:T(8,128)(2,1)}, u32[]{:S(2)}, u32[]{:S(2)}) collective-permute-start(bf16[2048,512]{1,0:T(8,128)(2,1)S(1)} %copy-done.4), channel_id=1, source_target_pairs={{0,1},{1,0},{2,3},{3,2},{4,5},{5,4},{6,7},{7,6},{8,9},{9,8},{10,11... | collective-permute-start | bytes 6291464 | tf_op jit(solution)/shard_map/ppermute | solution.py:37
  221.4 82.2 %collective-permute-start.20 = (bf16[2048,384]{1,0:T(8,128)(2,1)}, bf16[2048,384]{1,0:T(8,128)(2,1)}, u32[]{:S(2)}, u32[]{:S(2)}) collective-permute-start(bf16[2048,384]{1,0:T(8,128)(2,1)} %slice.94), channel_id=1, source_target_pairs={{0,3},{3,0},{1,2},{2,1},{4,7},{7,4},{5,6},{6,5},{8,11},{11,8},{9,1... | collective-permute-start | bytes 4718600 | tf_op jit(solution)/shard_map/ppermute | solution.py:45
  334.8 211.5 %reduce-scatter.7.cloned.1.call-start = ((), (), s32[]{:S(2)}) async-start(), calls=%async_computation.8 | async-start | bytes 9437184 | tf_op jit(solution)/shard_map/reduce_scatter | solution.py:487
  376.9 24.7 %collective-permute-start.21 = (bf16[512,1024]{1,0:T(8,128)(2,1)}, bf16[512,1024]{1,0:T(8,128)(2,1)S(1)}, u32[]{:S(2)}, u32[]{:S(2)}) collective-permute-start(bf16[512,1024]{1,0:T(8,128)(2,1)} %get-tuple-element.221), channel_id=1, source_target_pairs={{0,1},{1,0},{2,3},{3,2},{4,5},{5,4},{6,7},{7,6},{8,9},{9,8},{10,11... | collective-permute-start | bytes 3145736 | tf_op jit(solution)/shard_map/ppermute | solution.py:37
  377.1 24.6 %collective-permute-start.22 = (bf16[512,1024]{1,0:T(8,128)(2,1)}, bf16[512,1024]{1,0:T(8,128)(2,1)S(1)}, u32[]{:S(2)}, u32[]{:S(2)}) collective-permute-start(bf16[512,1024]{1,0:T(8,128)(2,1)} %get-tuple-element.222), channel_id=1, source_target_pairs={{0,2},{2,0},{1,3},{3,1},{4,6},{6,4},{5,7},{7,5},{8,10},{10,8},{9,1... | collective-permute-start | bytes 3145736 | tf_op jit(solution)/shard_map/ppermute | solution.py:41
  401.7 30.6 %collective-permute-start.23 = (bf16[512,1024]{1,0:T(8,128)(2,1)S(1)}, bf16[512,1024]{1,0:T(8,128)(2,1)S(1)}, u32[]{:S(2)}, u32[]{:S(2)}) collective-permute-start(bf16[512,1024]{1,0:T(8,128)(2,1)S(1)} %copy-done.44), channel_id=1, source_target_pairs={{0,1},{1,0},{2,3},{3,2},{4,5},{5,4},{6,7},{7,6},{8,9},{9,8},{10,11... | collective-permute-start | bytes 3145736 | tf_op jit(solution)/shard_map/ppermute | solution.py:37
  403.3 29.0 %collective-permute-start.24 = (bf16[512,1024]{1,0:T(8,128)(2,1)}, bf16[512,1024]{1,0:T(8,128)(2,1)S(1)}, u32[]{:S(2)}, u32[]{:S(2)}) collective-permute-start(bf16[512,1024]{1,0:T(8,128)(2,1)} %get-tuple-element.229), channel_id=1, source_target_pairs={{0,2},{2,0},{1,3},{3,1},{4,6},{6,4},{5,7},{7,5},{8,10},{10,8},{9,1... | collective-permute-start | bytes 3145736 | tf_op jit(solution)/shard_map/ppermute | solution.py:41
  432.3 24.8 %collective-permute-start.25 = (bf16[512,1024]{1,0:T(8,128)(2,1)}, bf16[512,1024]{1,0:T(8,128)(2,1)S(1)}, u32[]{:S(2)}, u32[]{:S(2)}) collective-permute-start(bf16[512,1024]{1,0:T(8,128)(2,1)} %get-tuple-element.240), channel_id=1, source_target_pairs={{0,1},{1,0},{2,3},{3,2},{4,5},{5,4},{6,7},{7,6},{8,9},{9,8},{10,11... | collective-permute-start | bytes 3145736 | tf_op jit(solution)/shard_map/ppermute | solution.py:37
  432.7 24.4 %collective-permute-start.26 = (bf16[512,1024]{1,0:T(8,128)(2,1)}, bf16[512,1024]{1,0:T(8,128)(2,1)}, u32[]{:S(2)}, u32[]{:S(2)}) collective-permute-start(bf16[512,1024]{1,0:T(8,128)(2,1)} %get-tuple-element.241), channel_id=1, source_target_pairs={{0,2},{2,0},{1,3},{3,1},{4,6},{6,4},{5,7},{7,5},{8,10},{10,8},{9,1... | collective-permute-start | bytes 3145736 | tf_op jit(solution)/shard_map/ppermute | solution.py:41
  458.1 185.0 %reduce-scatter.9.cloned.1.call-start = ((), (), s32[]{:S(2)}) async-start(), calls=%async_computation.9 | async-start | bytes 9437184 | tf_op jit(solution)/shard_map/reduce_scatter | solution.py:487
  467.2 60.1 %collective-permute-start.28 = (bf16[512,2048]{1,0:T(8,128)(2,1)}, bf16[512,2048]{1,0:T(8,128)(2,1)}, u32[]{:S(2)}, u32[]{:S(2)}) collective-permute-start(bf16[512,2048]{1,0:T(8,128)(2,1)} %get-tuple-element.248.refs_0_), channel_id=1, source_target_pairs={{0,2},{2,0},{1,3},{3,1},{4,6},{6,4},{5,7},{7,5},{8,10},{10,8},{9,1... | collective-permute-start | bytes 6291464 | tf_op jit(solution)/shard_map/ppermute | solution.py:41
  468.8 58.6 %collective-permute-start.27 = (bf16[512,2048]{1,0:T(8,128)(2,1)}, bf16[512,2048]{1,0:T(8,128)(2,1)}, u32[]{:S(2)}, u32[]{:S(2)}) collective-permute-start(bf16[512,2048]{1,0:T(8,128)(2,1)} %get-tuple-element.248.refs_0_), channel_id=1, source_target_pairs={{0,1},{1,0},{2,3},{3,2},{4,5},{5,4},{6,7},{7,6},{8,9},{9,8},{10,11... | collective-permute-start | bytes 6291464 | tf_op jit(solution)/shard_map/ppermute | solution.py:37
  527.4 205.1 %reduce-scatter.11.cloned.1.call-start = ((), (), s32[]{:S(2)}) async-start(), calls=%async_computation.10 | async-start | bytes 7077888 | tf_op jit(solution)/shard_map/reduce_scatter | solution.py:487
  530.0 21.9 %collective-permute-start.30 = (bf16[256,2048]{1,0:T(8,128)(2,1)S(1)}, bf16[256,2048]{1,0:T(8,128)(2,1)S(1)}, u32[]{:S(2)}, u32[]{:S(2)}) collective-permute-start(bf16[256,2048]{1,0:T(8,128)(2,1)S(1)} %slice.99), channel_id=1, source_target_pairs={{0,2},{2,0},{1,3},{3,1},{4,6},{6,4},{5,7},{7,5},{8,10},{10,8},{9,1... | collective-permute-start | bytes 3145736 | tf_op jit(solution)/shard_map/ppermute | solution.py:41
  530.8 22.1 %collective-permute-start.29 = (bf16[256,2048]{1,0:T(8,128)(2,1)S(1)}, bf16[256,2048]{1,0:T(8,128)(2,1)}, u32[]{:S(2)}, u32[]{:S(2)}) collective-permute-start(bf16[256,2048]{1,0:T(8,128)(2,1)S(1)} %slice.98), channel_id=1, source_target_pairs={{0,1},{1,0},{2,3},{3,2},{4,5},{5,4},{6,7},{7,6},{8,9},{9,8},{10,11... | collective-permute-start | bytes 3145736 | tf_op jit(solution)/shard_map/ppermute | solution.py:37
  552.9 37.6 %collective-permute-start.31 = (bf16[2048,256]{1,0:T(8,128)(2,1)}, bf16[2048,256]{1,0:T(8,128)(2,1)S(1)}, u32[]{:S(2)}, u32[]{:S(2)}) collective-permute-start(bf16[2048,256]{1,0:T(8,128)(2,1)} %get-tuple-element.275), channel_id=1, source_target_pairs={{0,1},{1,0},{2,3},{3,2},{4,5},{5,4},{6,7},{7,6},{8,9},{9,8},{10,11... | collective-permute-start | bytes 3145736 | tf_op jit(solution)/shard_map/ppermute | solution.py:37
  553.9 36.6 %collective-permute-start.32 = (bf16[2048,256]{1,0:T(8,128)(2,1)}, bf16[2048,256]{1,0:T(8,128)(2,1)S(1)}, u32[]{:S(2)}, u32[]{:S(2)}) collective-permute-start(bf16[2048,256]{1,0:T(8,128)(2,1)} %get-tuple-element.277), channel_id=1, source_target_pairs={{0,2},{2,0},{1,3},{3,1},{4,6},{6,4},{5,7},{7,5},{8,10},{10,8},{9,1... | collective-permute-start | bytes 3145736 | tf_op jit(solution)/shard_map/ppermute | solution.py:41
  555.2 43.4 %collective-permute-start.33 = (bf16[2048,256]{1,0:T(8,128)(2,1)}, bf16[2048,256]{1,0:T(8,128)(2,1)}, u32[]{:S(2)}, u32[]{:S(2)}) collective-permute-start(bf16[2048,256]{1,0:T(8,128)(2,1)} %get-tuple-element.279), channel_id=1, source_target_pairs={{0,1},{1,0},{2,3},{3,2},{4,5},{5,4},{6,7},{7,6},{8,9},{9,8},{10,11... | collective-permute-start | bytes 3145736 | tf_op jit(solution)/shard_map/ppermute | solution.py:37
  557.3 41.4 %collective-permute-start.34 = (bf16[2048,256]{1,0:T(8,128)(2,1)}, bf16[2048,256]{1,0:T(8,128)(2,1)}, u32[]{:S(2)}, u32[]{:S(2)}) collective-permute-start(bf16[2048,256]{1,0:T(8,128)(2,1)} %get-tuple-element.281), channel_id=1, source_target_pairs={{0,2},{2,0},{1,3},{3,1},{4,6},{6,4},{5,7},{7,5},{8,10},{10,8},{9,1... | collective-permute-start | bytes 3145736 | tf_op jit(solution)/shard_map/ppermute | solution.py:41
  598.7 25.9 %collective-permute-start.35 = (bf16[2048,256]{1,0:T(8,128)(2,1)}, bf16[2048,256]{1,0:T(8,128)(2,1)}, u32[]{:S(2)}, u32[]{:S(2)}) collective-permute-start(bf16[2048,256]{1,0:T(8,128)(2,1)} %get-tuple-element.298), channel_id=1, source_target_pairs={{0,1},{1,0},{2,3},{3,2},{4,5},{5,4},{6,7},{7,6},{8,9},{9,8},{10,11... | collective-permute-start | bytes 3145736 | tf_op jit(solution)/shard_map/ppermute | solution.py:37
  599.7 24.8 %collective-permute-start.36 = (bf16[2048,256]{1,0:T(8,128)(2,1)}, bf16[2048,256]{1,0:T(8,128)(2,1)}, u32[]{:S(2)}, u32[]{:S(2)}) collective-permute-start(bf16[2048,256]{1,0:T(8,128)(2,1)} %get-tuple-element.299), channel_id=1, source_target_pairs={{0,2},{2,0},{1,3},{3,1},{4,6},{6,4},{5,7},{7,5},{8,10},{10,8},{9,1... | collective-permute-start | bytes 3145736 | tf_op jit(solution)/shard_map/ppermute | solution.py:41
  645.6 29.7 %collective-permute-start.39 = (bf16[2048,256]{1,0:T(8,128)(2,1)}, bf16[2048,256]{1,0:T(8,128)(2,1)}, u32[]{:S(2)}, u32[]{:S(2)}) collective-permute-start(bf16[2048,256]{1,0:T(8,128)(2,1)} %add_convert_fusion.4), channel_id=1, source_target_pairs={{0,1},{1,0},{2,3},{3,2},{4,5},{5,4},{6,7},{7,6},{8,9},{9,8},{10,11... | collective-permute-start | bytes 3145736 | tf_op jit(solution)/shard_map/ppermute | solution.py:37
  647.0 28.2 %collective-permute-start.40 = (bf16[2048,256]{1,0:T(8,128)(2,1)}, bf16[2048,256]{1,0:T(8,128)(2,1)}, u32[]{:S(2)}, u32[]{:S(2)}) collective-permute-start(bf16[2048,256]{1,0:T(8,128)(2,1)} %add_convert_fusion.3), channel_id=1, source_target_pairs={{0,2},{2,0},{1,3},{3,1},{4,6},{6,4},{5,7},{7,5},{8,10},{10,8},{9,1... | collective-permute-start | bytes 3145736 | tf_op jit(solution)/shard_map/ppermute | solution.py:41
  650.0 25.3 %collective-permute-start.43 = (bf16[256,512]{0,1:T(8,128)(2,1)S(1)}, bf16[256,512]{0,1:T(8,128)(2,1)S(1)}, u32[]{:S(2)}, u32[]{:S(2)}) collective-permute-start(bf16[256,512]{0,1:T(8,128)(2,1)S(1)} %get-tuple-element.356), channel_id=1, source_target_pairs={{24,16},{28,20},{25,17},{29,21},{26,18},{30,22},{27,19},{31,23}} | collective-permute-start | bytes 786440 | tf_op jit(solution)/shard_map/ppermute | solution.py:520
  650.7 24.6 %collective-permute-start.42 = (bf16[256,512]{0,1:T(8,128)(2,1)S(1)}, bf16[256,512]{0,1:T(8,128)(2,1)S(1)}, u32[]{:S(2)}, u32[]{:S(2)}) collective-permute-start(bf16[256,512]{0,1:T(8,128)(2,1)S(1)} %get-tuple-element.357), channel_id=1, source_target_pairs={{0,8},{4,12},{1,9},{5,13},{2,10},{6,14},{3,11},{7,15}} | collective-permute-start | bytes 786440 | tf_op jit(solution)/shard_map/ppermute | solution.py:519
  675.3 38.3 %collective-permute-start.45 = (bf16[2048,256]{1,0:T(8,128)(2,1)}, bf16[2048,256]{1,0:T(8,128)(2,1)}, u32[]{:S(2)}, u32[]{:S(2)}) collective-permute-start(bf16[2048,256]{1,0:T(8,128)(2,1)} %add_convert_fusion.1), channel_id=1, source_target_pairs={{0,2},{2,0},{1,3},{3,1},{4,6},{6,4},{5,7},{7,5},{8,10},{10,8},{9,1... | collective-permute-start | bytes 3145736 | tf_op jit(solution)/shard_map/ppermute | solution.py:41
  676.1 37.4 %collective-permute-start.44 = (bf16[2048,256]{1,0:T(8,128)(2,1)}, bf16[2048,256]{1,0:T(8,128)(2,1)}, u32[]{:S(2)}, u32[]{:S(2)}) collective-permute-start(bf16[2048,256]{1,0:T(8,128)(2,1)} %add_convert_fusion.2), channel_id=1, source_target_pairs={{0,1},{1,0},{2,3},{3,2},{4,5},{5,4},{6,7},{7,6},{8,9},{9,8},{10,11... | collective-permute-start | bytes 3145736 | tf_op jit(solution)/shard_map/ppermute | solution.py:37
  (65 other events, 1003.9 us)
Sparse Core Ops, SparseCore 0:
  13.2 84.7 all-gather.3
  100.1 149.6 all-gather.5
  251.4 80.7 all-gather.7
  334.9 88.5 reduce-scatter.4
  457.3 88.9 reduce-scatter.6
  548.4 87.9 reduce-scatter.8
  643.3 81.1 reduce-scatter.10

commit v3 on v2

--- a/solution.py
+++ b/solution.py
@@ -93,6 +93,28 @@
 
 def shape_of(shape, dtype):
     return jax.ShapeDtypeStruct(shape, dtype)
+
+
+def packed_block(in_parts, out_block):
+    slim, part = in_parts.shape[1:]
+
+    def body(_, in_ref, out_ref, o_ref):
+        for k in range(3):
+            o_ref[:, k * part : (k + 1) * part] = in_ref[k]
+        for k in range(2):
+            at = 3 * part + k * (part // 2)
+            o_ref[:, at : at + part // 2] = out_ref[k * slim : (k + 1) * slim, :]
+
+    return run(
+        body,
+        (1,),
+        jnp.zeros((1,), jnp.int32),
+        [in_parts, out_block],
+        [whole(in_parts.shape), whole(out_block.shape)],
+        [shape_of((slim, 4 * part), BF)],
+        [whole((slim, 4 * part))],
+        vmem=16,
+    )[0]
 
 
 def project(me, pieces, square, gain, weight, kernel, masks):
@@ -273,14 +295,13 @@
     count = units // step
 
     def body(_, g_ref, a_ref, b_ref, d_ref, wg_ref, wu_ref, *refs):
-        *halves_of, o_ref, total = refs[-2 * bands - 2 :]
+        *halves_of, dg_ref, du_ref, total = refs[-2 * bands - 3 :]
         j = pl.program_id(1)
         dq = contract_cols(g_ref[...], d_ref[...])
         d_gate = (dq * b_ref[...].astype(F32)).astype(BF)
         d_up = (dq * a_ref[...].astype(F32)).astype(BF)
-        at = pl.multiple_of(j * step, 128)
-        o_ref[:, pl.ds(at, step)] = d_gate
-        o_ref[:, pl.ds(units + at, step)] = d_up
+        dg_ref[...] = d_gate
+        du_ref[...] = d_up
         term = contract_cols(d_gate, wg_ref[...]) + contract_cols(d_up, wu_ref[...])
 
         @pl.when(j == 0)
@@ -302,7 +323,7 @@
         body,
         (bands, count),
         owners,
-        [grad, slope_up, slope_gate, down, weight, weight] + ([] if d_both is None else [d_both]),
+        [grad, slope_up, slope_gate, down, weight, weight] + list(d_both or []),
         [
             pl.BlockSpec((band, full), lambda i, j, o: (o[i], 0)),
             pl.BlockSpec((band, step), lambda i, j, o: (o[i], j)),
@@ -311,13 +332,13 @@
             pl.BlockSpec((full, step), lambda i, j, o: (0, j)),
             pl.BlockSpec((full, step), lambda i, j, o: (0, count + j)),
         ]
-        + ([] if d_both is None else [pl.BlockSpec(memory_space=pl.ANY)]),
-        [shape_of((band, full // 2), BF)] * (2 * bands) + [shape_of((row_count, 2 * units), BF)],
+        + [pl.BlockSpec(memory_space=pl.ANY)] * len(d_both or []),
+        [shape_of((band, full // 2), BF)] * (2 * bands) + [shape_of((row_count, units), BF)] * 2,
         [pl.BlockSpec((band, full // 2), lambda i, j, o: (0, 0))] * (2 * bands)
-        + [pl.BlockSpec((band, 2 * units), lambda i, j, o: (o[i], 0))],
+        + [pl.BlockSpec((band, step), lambda i, j, o: (o[i], j))] * 2,
         [pltpu.VMEM((band, full), F32)],
         flops=6 * bands * band * full * units,
-        aliases=None if d_both is None else {7: 2 * bands},
+        aliases={7: 2 * bands, 8: 2 * bands + 1} if d_both else None,
     )
 
 
@@ -357,7 +378,7 @@
     )
 
 
-def mixer_back(owners, pieces, out_rows, mixed, filtered, kernel, masks, weight):
+def mixer_back(owners, pieces, out_rows, mixed, filtered, kernel, masks, weight, x_full, scale_one, gain):
     part, full = out_rows.shape
     row_count = mixed.shape[0]
     count = row_count // TILE
@@ -367,15 +388,16 @@
     packed = pl.BlockSpec((full, 3 * part), lambda *_: (0, 0), pipeline_mode=pl.Buffered(1))
 
     def body(own_ref, *refs):
-        w_ref, p_ref, v_ref, k_ref, m_ref, r_ref = refs[given : given + 6]
-        outs = refs[given + 6 : given + 6 + 2 * size]
-        o_ref, kg_ref, d_ref, carry, dy_ref = refs[given + 6 + 2 * size :]
+        w_ref, p_ref, v_ref, k_ref, m_ref, r_ref, x_ref, s_ref, gain_ref = refs[given : given + 9]
+        outs = refs[given + 9 : given + 9 + 2 * size]
+        o_ref, kg_ref, d_ref, row_ref, g_ref, carry, dy_ref = refs[given + 9 + 2 * size :]
         i = pl.program_id(0)
 
         @pl.when(i == 0)
         def _():
             carry[...] = jnp.zeros_like(carry)
             kg_ref[...] = jnp.zeros_like(kg_ref)
+            g_ref[...] = jnp.zeros_like(g_ref)
 
         first = (count - 1 - i) * TILE
         if given == 1:
@@ -415,11 +437,16 @@
         o_ref[:, :part] = (du * x).astype(BF)
         o_ref[:, part : 2 * part] = (dy * v_ref[...]).astype(BF)
         o_ref[:, 2 * part :] = (du * b).astype(BF)
+        total = 0.0
         for k in range(size):
             rows = pl.ds(pl.multiple_of(own_ref[k] * part, part), part)
             term = contract_cols(o_ref[...], r_ref[rows, :])
+            by_x = term * x_ref[:, rows].astype(F32)
+            total = total + jnp.sum(by_x * gain_ref[:, rows], axis=1, keepdims=True)
+            g_ref[:, rows] += jnp.sum(by_x * s_ref[...], axis=0, keepdims=True)
             outs[2 * k][...] = term[:, : part // 2].astype(BF)
             outs[2 * k + 1][...] = term[:, part // 2 :].astype(BF)
+        row_ref[...] = total
 
     def back(width):
         return pl.BlockSpec((TILE, width), lambda i, *_: (count - 1 - i, 0))
@@ -428,13 +455,16 @@
         body,
         (count,),
         owners,
-        [*pieces, out_rows, mixed, filtered, kernel, masks, weight],
+        [*pieces, out_rows, mixed, filtered, kernel, masks, weight, x_full, scale_one, gain],
         [whole(p.shape) for p in pieces]
-        + [whole(out_rows.shape), back(3 * part), back(part), whole(kernel.shape), back(2), packed],
+        + [whole(out_rows.shape), back(3 * part), back(part), whole(kernel.shape), back(2), packed]
+        + [back(full), back(1), whole(gain.shape)],
         [shape_of((row_count, part // 2), BF)] * (2 * size)
-        + [shape_of((row_count, 3 * part), BF), shape_of((CONV, part), F32), shape_of((row_count, full), BF)],
+        + [shape_of((row_count, 3 * part), BF), shape_of((CONV, part), F32), shape_of((row_count, full), BF)]
+        + [shape_of((row_count, 1), F32), shape_of((1, full), F32)],
         [back(part // 2)] * (2 * size)
-        + [back(3 * part), pl.BlockSpec((CONV, part), lambda i, *_: (0, 0)), back(full)],
+        + [back(3 * part), pl.BlockSpec((CONV, part), lambda i, *_: (0, 0)), back(full)]
+        + [back(1), pl.BlockSpec((1, full), lambda i, *_: (0, 0))],
         [pltpu.VMEM((8, part), F32), pltpu.VMEM((TILE, part), F32)],
         flops=2 * row_count * full * part * 4,
     )
@@ -487,19 +517,18 @@
     return lax.psum_scatter(terms.astype(BF), "wide", scatter_dimension=axis, tiled=True)
 
 
-def narrow_total(values, square):
-    if not square:
-        return lax.psum(values, "narrow")
-    values = values + to_x(values)
-    return values + to_y(values)
-
-
-def wide_total(values, square):
-    if not square:
-        return lax.psum(values, "wide")
-    for bit in (1, 2, 4):
-        values = values + lax.ppermute(values, "wide", [(i, i ^ bit) for i in range(lax.axis_size("wide"))])
-    return values
+def narrow_total(values):
+    return lax.psum(values, "narrow")
+
+
+def to_core_sum(values):
+    return values + to_core(values)
+
+
+def line_total(values, beside):
+    others = [lax.ppermute(values, "wide", [(i, i ^ bit) for i in range(8)]) for bit in (2, 4, 6)]
+    others, done = lax.optimization_barrier((others, beside()))
+    return functools.reduce(jnp.add, others, values), done
 
 
 def to_core(values):
@@ -521,11 +550,10 @@
     )
 
 
-def line_start(terms, core):
+def line_sums(terms, core):
     blocks = terms.reshape(4, 2, terms.shape[0] // 8, terms.shape[1])
     other = to_core(lax.dynamic_index_in_dim(blocks, 1 - core, 1, keepdims=False))
-    sums = add_low(lax.dynamic_index_in_dim(blocks, core, 1, keepdims=False), other)
-    return line_step((sums, None, None), 1)
+    return add_low(lax.dynamic_index_in_dim(blocks, core, 1, keepdims=False), other)
 
 
 def line_end(state):
@@ -586,7 +614,7 @@
         return rows.transpose(2, 1, 0, 3).reshape(part_width, full_width)
 
     if square:
-        in_all = wide_all(jnp.concatenate(pack + list(halves(out_weight, 0)), axis=1), 0)
+        in_all = wide_all(packed_block(in_weight.transpose(1, 0, 2), out_weight), 0)
         x_pieces = gather_pieces(tokens, 1, True)[0]
         both_all = wide_all(after(both, *x_pieces), 0)
 
@@ -638,17 +666,29 @@
     slope_up = after(slope_up, down_terms)
 
     def ffn(which, d_both):
-        *parts, d_both = ffn_back(which, band, grad_full, slope_up, slope_gate, down_all, both_all, d_both)
-        return list(zip(parts[0::2], parts[1::2])), d_both
+        *parts, d_gate, d_up = ffn_back(which, band, grad_full, slope_up, slope_gate, down_all, both_all, d_both)
+        return list(zip(parts[0::2], parts[1::2])), (d_gate, d_up)
 
     def mixer(dh_pieces, out_rows):
-        *parts, d_flat, kernel_grad, d_hidden_low = mixer_back(
-            owners, dh_pieces, out_rows, mixed, filtered, kernel, masks, in_all
-        )
-        return list(zip(parts[0::2], parts[1::2])), d_flat, kernel_grad, d_hidden_low
+        *parts, d_flat, kernel_grad, d_hidden_low, inner_one, gain_one_terms = mixer_back(
+            owners, dh_pieces, out_rows, mixed, filtered, kernel, masks, in_all, x_full, scale_one, gain_one
+        )
+        inner_one = inner_one.reshape(-1, 128)
+        return list(zip(parts[0::2], parts[1::2])), d_flat, kernel_grad, d_hidden_low, inner_one, gain_one_terms
 
     def dh_of(sums):
         return hidden_back(me_s, sums, hidden, scale_two, grad_full, gain_two)
+
+    def tokens_grad_of(d_normed_one, inner_one, d_hidden_low):
+        my_gain = lax.dynamic_slice_in_dim(norm1_gain, offset, part_width)
+        inner_one = inner_one.reshape(row_count, 1) / full_width
+        return (
+            lax.dynamic_slice_in_dim(d_hidden_low, offset, part_width, 1).astype(F32)
+            + scale_one * (d_normed_one * my_gain - tokens.astype(F32) * scale_one * scale_one * inner_one)
+        ).astype(BF)
+
+    def small_of(gain_terms, kernel_grad):
+        return jnp.concatenate([lax.dynamic_index_in_dim(gain_terms, me, 1, keepdims=False), kernel_grad], axis=0)
 
     def out_terms_of(hidden_low):
         parts = front_terms(owners, hidden_low, down_all)
@@ -667,23 +707,23 @@
             )
         )
         x_high, y_low, gate_terms = barrier(
-            (to_x(x_high), to_y(y_low), contract_rows(normed_two, d_both[:, :units]).astype(BF))
+            (to_x(x_high), to_y(y_low), contract_rows(normed_two, d_both[0]).astype(BF))
         )
         gate_grad = wide_sums(gate_terms, 0)
         y_high = after(y_high, down_grad)
         d_hidden_rows, gain_two_terms = dh_of([own, (x_low, x_high), (y_low, y_high)])
 
         def beside_dh():
-            up_terms = contract_rows(after(normed_two, d_hidden_rows), d_both[:, units:]).astype(BF)
-            return up_terms, out_terms_of(after(hidden_low, up_terms)), unpacked(after(in_all, d_hidden_rows))
-
-        dh_pieces, (up_terms, out_parts, out_rows), _ = gather_pieces(
-            d_hidden_rows, 0, True, (beside_dh, lambda _: ())
+            up_terms = contract_rows(after(normed_two, d_hidden_rows), d_both[1]).astype(BF)
+            return up_terms, unpacked(after(in_all, d_hidden_rows))
+
+        dh_pieces, (up_terms, out_rows), out_parts = gather_pieces(
+            d_hidden_rows, 0, True, (beside_dh, lambda first: out_terms_of(after(hidden_low, first[0])))
         )
         up_grad = wide_sums(up_terms, 0)
         out_parts, gate_grad = barrier((out_parts, gate_grad))
         out_first = [tuple(after(half, *dh_pieces[3:]) for half in part) for part in out_parts]
-        out_via_x, out_via_y, out_x_low, out_y_high, (one_parts, d_flat, kernel_grad, d_hidden_low) = barrier(
+        out_via_x, out_via_y, out_x_low, out_y_high, mixer_outs = barrier(
             (
                 to_x(out_first[0][0]),
                 to_y(out_first[0][1]),
@@ -692,13 +732,24 @@
                 mixer(dh_pieces, out_rows),
             )
         )
-        via_x, via_y, in_terms = barrier(
-            (to_x(one_parts[0][0]), to_y(one_parts[0][1]), contract_rows(normed_one, d_flat).astype(BF))
-        )
-        x_low, y_high, x_high, y_low, out_x_high, out_y_low, out_terms, in_terms, up_grad = barrier(
+        one_parts, d_flat, kernel_grad, d_hidden_low, inner_one, gain_one_terms = mixer_outs
+        gain_terms = jnp.concatenate([gain_one_terms, gain_two_terms], axis=0).reshape(2, size, part_width)
+        via_x, via_y, x_inner, x_gain, in_terms = barrier(
+            (
+                to_x(one_parts[0][0]),
+                to_y(one_parts[0][1]),
+                to_x(inner_one),
+                to_x(gain_terms),
+                contract_rows(normed_one, d_flat).astype(BF),
+            )
+        )
+        inner_one, gain_terms = inner_one + x_inner, gain_terms + x_gain
+        x_low, y_high, y_inner, y_gain, x_high, y_low, out_x_high, out_y_low, out_terms, in_terms, up_grad = barrier(
             (
                 to_x(after(one_parts[1][0], via_x)),
                 to_y(after(one_parts[2][1], via_y)),
+                to_y(inner_one),
+                to_y(gain_terms),
                 add_low(one_parts[1][1], via_y),
                 add_low(one_parts[2][0], via_x),
                 add_low(out_parts[1][1], out_via_y),
@@ -709,48 +760,42 @@
             )
         )
         in_grad = wide_sums(in_terms, 0)
-        x_high, y_low, line = barrier((to_x(x_high), to_y(y_low), line_start(out_terms, core)))
+        inner_one, gain_terms = inner_one + y_inner, gain_terms + y_gain
+        x_high, y_low, line, small = barrier(
+            (
+                to_x(x_high),
+                to_y(y_low),
+                line_step((line_sums(out_terms, core), None, None), 1),
+                to_core_sum(small_of(gain_terms, kernel_grad)),
+            )
+        )
         d_normed_one = total_of([one_parts[3], (x_low, x_high), (y_low, y_high)])
-        my_gain = lax.dynamic_slice_in_dim(norm1_gain, offset, part_width)
-        inner_one = jnp.sum(d_normed_one * my_gain * tokens.astype(F32), axis=1).reshape(-1, 128)
-        out_x_high, out_y_low, inner_one, line = barrier(
-            (
+        tokens_grad = tokens_grad_of(d_normed_one, inner_one, d_hidden_low)
+        small, (out_x_high, out_y_low, line) = line_total(
+            small,
+            lambda: (
                 to_x(after(out_x_high, x_low, x_high)),
                 to_y(after(out_y_low, y_low, y_high)),
-                inner_one + to_x(inner_one),
                 line_step(line, 2),
-            )
-        )
-        inner_one = inner_one + to_y(inner_one)
+            ),
+        )
         out_grad = line_end(line).T
         ffn_out = total_of([out_parts[3], (out_x_low, out_x_high), (out_y_low, out_y_high)])
     else:
         ffn_terms, d_both = ffn(owners, None)
-        both_grad = wide_sums(contract_rows(normed_two, d_both), 0)
-        gate_grad, up_grad = both_grad[:, :units], both_grad[:, units:]
+        gate_grad, up_grad = [wide_sums(contract_rows(normed_two, d), 0) for d in d_both]
         d_hidden_rows, gain_two_terms = dh_of([tuple(halves(scatter_plain(ffn_terms, 0), 1))])
-        one_parts, d_flat, kernel_grad, d_hidden_low = mixer(gather_pieces(d_hidden_rows, 0, False)[0], out_rows)
-        d_normed_one = scatter_plain(one_parts, 1)
+        one_parts, d_flat, kernel_grad, d_hidden_low, inner_one, gain_one_terms = mixer(
+            gather_pieces(d_hidden_rows, 0, False)[0], out_rows
+        )
+        tokens_grad = tokens_grad_of(scatter_plain(one_parts, 1), narrow_total(inner_one), d_hidden_low)
+        gain_terms = jnp.concatenate([gain_one_terms, gain_two_terms], axis=0).reshape(2, size, part_width)
+        small = lax.psum(small_of(narrow_total(gain_terms), kernel_grad), "wide")
         ffn_out = scatter_plain(out_terms_of(hidden_low), 1)
         in_grad = wide_sums(contract_rows(normed_one, d_flat), 0)
         out_grad = wide_sums(contract_rows(mixer_low, d_hidden_low), 1)
     in_grad = jnp.stack([in_grad[:, k * part_width : (k + 1) * part_width] for k in range(3)], axis=1)
     block_out = (lax.dynamic_slice_in_dim(hidden, offset, part_width, 1) + ffn_out).astype(BF)
-
-    my_gain = lax.dynamic_slice_in_dim(norm1_gain, offset, part_width)
-    x_part = tokens.astype(F32)
-    scaled_one = d_normed_one * my_gain
-    if not square:
-        inner_one = lax.psum(jnp.sum(scaled_one * x_part, axis=1), "narrow")
-    inner_one = inner_one.reshape(row_count, 1) / full_width
-    tokens_grad = (
-        lax.dynamic_slice_in_dim(d_hidden_low, offset, part_width, 1).astype(F32)
-        + scale_one * (scaled_one - x_part * scale_one * scale_one * inner_one)
-    ).astype(BF)
-    gain_one_grad = jnp.sum(d_normed_one * x_part * scale_one, axis=0)
-    gain_two_terms = narrow_total(after(gain_two_terms, ffn_out).reshape(size, part_width), square)
-    gain_two_terms = lax.dynamic_slice_in_dim(gain_two_terms, me, 1, 0)
-    small = wide_total(jnp.concatenate([gain_one_grad[None, :], gain_two_terms, kernel_grad], axis=0), square)
     gain_one_grad, gain_two_grad, kernel_grad = small[0], small[1], small[2:]
     return (
         block_out,

time: 749 us -> 751 us (level)
  starting transfers between devices: 57.2 us -> 70.2 us
  Pallas kernels: 267 us -> 277 us
  waiting for transfers between devices: 215 us -> 205 us
    ppermute x3, waiting for transfers between devices: 13.4 us -> 0.01 us  [line_total(): lax.ppermute(values, 'wide', [(i, i ^ bit) for i in range(8)])]
    ppermute x3, waiting for transfers between devices: 0.01 us -> 11.2 us  [line_step(): lax.ppermute(with_own(right, z + 4 - step), 'wide', [(w, w + 2) for w in...]
    pallas_call x10 -> x11, Pallas kernels: 267 us -> 277 us  [run(): pl.pallas_call(kernel, grid_spec=pltpu.PrefetchScalarGridSpec(num_scalar_...]
    ppermute x3, starting transfers between devices: 6.94 us -> 16 us  [line_step(): lax.ppermute(with_own(right, z + 4 - step), 'wide', [(w, w + 2) for w in...]
    ppermute x20, waiting for transfers between devices: 74.3 us -> 65.4 us  [to_x(): return lax.ppermute(values, 'narrow', ALONG_X)]
    ppermute x20, waiting for transfers between devices: 107 us -> 116 us  [to_y(): return lax.ppermute(values, 'narrow', ALONG_Y)]
    unnamed x104 -> x119, local copies, waits for them, and re-layouts: 15.6 us -> 15.1 us
  transfers between devices with their start and end apart: 64 -> 65, of which waited for: 21 -> 25; matrix products, arithmetic and copies ran while one was open for 23% -> 22% of each run, Pallas kernels for 36% -> 37%
where the time goes in v3:
time: 751 us; the launch traced here: 748 us
  Pallas kernels  277 us (37%)
  waiting for transfers between devices  205 us (27%)
  matrix products  101 us (13%)
  starting transfers between devices  70.2 us (9%)
  other arithmetic  42.4 us (6%)
  local copies, waits for them, and re-layouts  37.9 us (5%)
  between operations  15.2 us (2%)
    pallas_call x11, Pallas kernels, run(): pl.pallas_call(kernel, grid_spec=pltpu.PrefetchScalarGridSpec(num_scalar_...  277 us
    ppermute x20, waiting for transfers between devices, to_y(): return lax.ppermute(values, 'narrow', ALONG_Y)  116 us
    dot_general x5, matrix products, contract_rows(): lax.dot_general(left, right, (((0,), (0,)), ((), ())), preferred_element_...  101 us
    ppermute x20, waiting for transfers between devices, to_x(): return lax.ppermute(values, 'narrow', ALONG_X)  65.4 us
    ppermute x20, starting transfers between devices, to_x(): return lax.ppermute(values, 'narrow', ALONG_X)  20.3 us
    ppermute x20, starting transfers between devices, to_y(): return lax.ppermute(values, 'narrow', ALONG_Y)  19.1 us
    ppermute x3, starting transfers between devices, line_step(): lax.ppermute(with_own(right, z + 4 - step), 'wide', [(w, w + 2) for w in...  16 us
    unnamed x119, local copies, waits for them, and re-layouts  15.1 us
  transfers between devices with their start and end apart: 65, of which 25 were waited for; matrix products, arithmetic and copies ran while one was open for 22% of the time, Pallas kernels for 37%

profile of v3, /device:TPU:0, one launch (start us, length us, event | category | flops | bytes accessed | tf_op | source)
XLA Modules:
  0.0 748.2 jit_solution(7665595695706477620)
XLA Ops:
  11.3 3.0 collective-permute-start.3
  15.8 44.1 %collective-permute-done.3.refs_2_ = bf16[2048,512]{1,0:T(8,128)(2,1)S(1)} collective-permute-done((bf16[2048,512]{1,0:T(8,128)(2,1)S(1)}, bf16[2048,512]{1,0:T(8,128)(2,1)S(1)}, u32[]{:S(2)}, u32[]{:S(2)}) %collective-permute-start.3) | collective-permute-done | bytes 2097184 | tf_op jit(solution)/shard_map/ppermute | solution.py:41
  66.3 20.5 %collective-permute-done.4.refs_3_ = bf16[2048,256]{1,0:T(8,128)(2,1)} collective-permute-done((bf16[2048,256]{1,0:T(8,128)(2,1)}, bf16[2048,256]{1,0:T(8,128)(2,1)}, u32[]{:S(2)}, u32[]{:S(2)}) %collective-permute-start.4) | collective-permute-done | bytes 1048608 | tf_op jit(solution)/shard_map/ppermute | solution.py:37
  92.4 2.9 all-gather.4.cloned.1.call-done.refs_6_.refs_10_
  99.7 27.6 %shard_map.187 = (bf16[2048,2048]{1,0:T(8,128)(2,1)}, bf16[2048,2048]{1,0:T(8,128)(2,1)}, f32[2048,1536]{1,0:T(8,128)}, f32[2048,512]{1,0:T(8,128)}, bf16[2048,512]{1,0:T(8,128)(2,1)}, /*index=5*/f32[2048,1]{1,0:T(8,128)}) custom-call(s32[1]{0:T(128)} %bitcast.2.me_ref._, bf16[2048,512]{1,0:T(8,128)(2,1)} %refs_0_.2, bf16[2048,512]{1,0:T(8,128)(2,1)} %copy-done.34, ...), custom_call_target="tpu_custom_call" | custom-call | flops 12884901888 | bytes 52467712 | tf_op jit(solution)/shard_map/pallas_call | solution.py:80
  133.4 44.9 %collective-permute-done.8.refs_2_ = bf16[2048,512]{1,0:T(8,128)(2,1)S(1)} collective-permute-done((bf16[2048,512]{1,0:T(8,128)(2,1)}, bf16[2048,512]{1,0:T(8,128)(2,1)S(1)}, u32[]{:S(2)}, u32[]{:S(2)}) %collective-permute-start.8) | collective-permute-done | bytes 2097184 | tf_op jit(solution)/shard_map/ppermute | solution.py:41
  181.4 8.1 %collective-permute-done.12.refs_9_ = bf16[512,512]{1,0:T(8,128)(2,1)S(1)} collective-permute-done((bf16[512,512]{1,0:T(8,128)(2,1)S(1)}, bf16[512,512]{1,0:T(8,128)(2,1)S(1)}, u32[]{:S(2)}, u32[]{:S(2)}) %collective-permute-start.12) | collective-permute-done | bytes 524320 | tf_op jit(solution)/shard_map/ppermute | solution.py:41
  189.7 26.7 %collective-permute-done.11.refs_8_ = bf16[512,512]{1,0:T(8,128)(2,1)S(1)} collective-permute-done((bf16[512,512]{1,0:T(8,128)(2,1)S(1)}, bf16[512,512]{1,0:T(8,128)(2,1)S(1)}, u32[]{:S(2)}, u32[]{:S(2)}) %collective-permute-start.11) | collective-permute-done | bytes 524320 | tf_op jit(solution)/shard_map/ppermute | solution.py:37
  220.2 2.4 collective-permute-start.20
  223.6 39.5 %shard_map.188 = (f32[2048,2048]{1,0:T(8,128)}, bf16[2048,2048]{1,0:T(8,128)(2,1)}, f32[2048,1]{1,0:T(8,128)}) custom-call(s32[1]{0:T(128)} %bitcast.core_ref, bf16[2048,512]{1,0:T(8,128)(2,1)} %get-tuple-element.205.refs_0_, bf16[2048,512]{1,0:T(8,128)(2,1)} %copy-done.36, bf16[2048,512]{1,0:T(8,128)(2,1)} %copy-done.35, bf16[2048,256]{1,0:T(8,128)(2,1)} %copy-done.49, ...), custom_call_target="tpu_custom_call" | custom-call | flops 17179869184 | bytes 50348032 | tf_op jit(solution)/shard_map/pallas_call | solution.py:80
  263.1 46.8 %shard_map.189 = (bf16[2048,2048]{1,0:T(8,128)(2,1)}, bf16[2048,2048]{1,0:T(8,128)(2,1)}, bf16[2048,2048]{1,0:T(8,128)(2,1)}) custom-call(s32[1]{0:T(128)} %bitcast.2.me_ref._, bf16[2048,2048]{1,0:T(8,128)(2,1)} %get-tuple-element.268.n_ref, bf16[2048,4096]{1,0:T(8,128)(2,1)} %all-gather.6.cloned.1.call-done.w_ref.wg_ref.wu_ref), custom_call_target="tpu_custom_call" | custom-call | flops 34359738368 | bytes 50331648 | tf_op jit(solution)/shard_map/pallas_call | solution.py:80
  310.0 7.1 shard_map.190.g_ref.refs_8_
  317.0 23.9 %convolution_convert_fusion.2 = bf16[2048,2048]{1,0:T(8,128)(2,1)} fusion(bf16[2048,2048]{1,0:T(8,128)(2,1)} %get-tuple-element.274.l_ref, bf16[2048,2048]{1,0:T(8,128)(2,1)} %shard_map.190.g_ref.refs_8_), kind=kOutput, calls=%fused_computation.2 | convolution fusion | flops 17184063488 | bytes 25165824 | tf_op jit(solution)/shard_map/dot_general | solution.py:19
  341.6 40.3 %shard_map.191 = (bf16[512,1024]{1,0:T(8,128)(2,1)}, bf16[512,1024]{1,0:T(8,128)(2,1)}, bf16[512,1024]{1,0:T(8,128)(2,1)}, bf16[512,1024]{1,0:T(8,128)(2,1)}, bf...) custom-call(s32[2]{0:T(128)} %pad_add_fusion.1._, bf16[2048,2048]{1,0:T(8,128)(2,1)} %shard_map.190.g_ref.refs_8_, ...), custom_call_target="tpu_custom_call" | custom-call | flops 25769803776 | bytes 88080384 | tf_op jit(solution)/shard_map/pallas_call | solution.py:80
  382.6 22.6 %shard_map.192 = (bf16[512,1024]{1,0:T(8,128)(2,1)}, bf16[512,1024]{1,0:T(8,128)(2,1)}, bf16[2048,2048]{1,0:T(8,128)(2,1)}, bf16[2048,2048]{1,0:T(8,128)(2,1)}) custom-call(s32[1]{0:T(128)} %bitcast.7._, bf16[2048,2048]{1,0:T(8,128)(2,1)} %shard_map.190.g_ref.refs_8_, ...), custom_call_target="tpu_custom_call", output_to_operand_aliasing={{2}: (7, {}), {3}: (8, {})} | custom-call | flops 12884901888 | bytes 102760448 | tf_op jit(solution)/shard_map/pallas_call | solution.py:80
  408.8 3.6 add_convert_fusion.4
  412.4 22.7 %shard_map.193 = (bf16[512,1024]{1,0:T(8,128)(2,1)}, bf16[512,1024]{1,0:T(8,128)(2,1)}, bf16[2048,2048]{1,0:T(8,128)(2,1)}, bf16[2048,2048]{1,0:T(8,128)(2,1)}) custom-call(s32[1]{0:T(128)} %bitcast.2.me_ref._, bf16[2048,2048]{1,0:T(8,128)(2,1)} %shard_map.190.g_ref.refs_8_, ...), custom_call_target="tpu_custom_call", output_to_operand_aliasing={{2}: (7, {}), {3}: (8, {})} | custom-call | flops 12884901888 | bytes 102760448 | tf_op jit(solution)/shard_map/pallas_call | solution.py:80
  436.9 23.8 %convolution_convert_fusion.1 = bf16[2048,2048]{1,0:T(8,128)(2,1)} fusion(bf16[2048,2048]{1,0:T(8,128)(2,1)} %get-tuple-element.268.n_ref, bf16[2048,2048]{1,0:T(8,128)(2,1)} %get-tuple-element.261), kind=kOutput, calls=%fused_computation.1 | convolution fusion | flops 17184063488 | bytes 25165824 | tf_op jit(solution)/shard_map/dot_general | solution.py:19
  461.7 8.4 %shard_map.194 = (bf16[512,2048]{1,0:T(8,128)(2,1)}, f32[1,2048]{1,0:T(1,128)}) custom-call(s32[1]{0:T(128)} %bitcast.2.me_ref._, bf16[512,1024]{1,0:T(8,128)(2,1)} %get-tuple-element.256.refs_0_, bf16[512,1024]{1,0:T(8,128)(2,1)} %get-tuple-element.257.refs_1_, bf16[512,1024]{1,0:T(8,128)(2,1)} %copy-done.26, bf16[512,1024]{1,0:T(8,128)(2,1)} %copy-done.28, ...), custom_call_target="tpu_custom_call" | custom-call | bytes 33579008 | tf_op jit(solution)/shard_map/pallas_call | solution.py:80
  472.4 3.0 slice.69
  475.4 2.6 reshape.66
  479.2 2.0 copy.39
  481.2 23.9 %convolution_convert_fusion = bf16[2048,2048]{1,0:T(8,128)(2,1)} fusion(bf16[2048,2048]{1,0:T(8,128)(2,1)} %get-tuple-element.268.n_ref, bf16[2048,2048]{1,0:T(8,128)(2,1)} %get-tuple-element.269), kind=kOutput, calls=%fused_computation | convolution fusion | flops 17184063488 | bytes 25165824 | tf_op jit(solution)/shard_map/dot_general | solution.py:19
  505.1 9.7 %collective-permute-done.28.refs_2_ = bf16[512,2048]{1,0:T(8,128)(2,1)} collective-permute-done((bf16[512,2048]{1,0:T(8,128)(2,1)}, bf16[512,2048]{1,0:T(8,128)(2,1)}, u32[]{:S(2)}, u32[]{:S(2)}) %collective-permute-start.28) | collective-permute-done | bytes 2097184 | tf_op jit(solution)/shard_map/ppermute | solution.py:41
  521.3 24.4 %shard_map.195 = (bf16[2048,256]{1,0:T(8,128)(2,1)}, bf16[2048,256]{1,0:T(8,128)(2,1)}, bf16[2048,256]{1,0:T(8,128)(2,1)}, bf16[2048,256]{1,0:T(8,128)(2,1)}, bf...) custom-call(s32[4]{0:T(128)} %pad_add_fusion.2.own_ref, ...), custom_call_target="tpu_custom_call" | custom-call | flops 17179869184 | bytes 25165824 | tf_op jit(solution)/shard_map/pallas_call | solution.py:80
  547.1 2.9 reduce-scatter.7.cloned.1.call-done
  554.1 36.2 %shard_map.196 = (bf16[2048,256]{1,0:T(8,128)(2,1)}, bf16[2048,256]{1,0:T(8,128)(2,1)}, bf16[2048,256]{1,0:T(8,128)(2,1)}, bf16[2048,256]{1,0:T(8,128)(2,1)}, bf...) custom-call(s32[4]{0:T(128)} %pad_add_fusion.2.own_ref, ...), custom_call_target="tpu_custom_call" | custom-call | flops 17179869184 | bytes 67170304 | tf_op jit(solution)/shard_map/pallas_call | solution.py:80
  591.9 3.6 collective-permute-done.32
  601.6 19.7 %convolution_convert_fusion.3 = bf16[2048,1536]{1,0:T(8,128)(2,1)} fusion(bf16[2048,2048]{1,0:T(8,128)(2,1)} %get-tuple-element.327, bf16[2048,1536]{1,0:T(8,128)(2,1)} %get-tuple-element.328), kind=kOutput, calls=%fused_computation.3 | convolution fusion | flops 12888047616 | bytes 20971520 | tf_op jit(solution)/shard_map/dot_general | solution.py:19
  621.4 2.9 add_convert_fusion
  629.7 9.5 %convolution_convert_fusion.4 = bf16[2048,512]{1,0:T(8,128)(2,1)} fusion(bf16[2048,2048]{1,0:T(8,128)(2,1)} %get-tuple-element.344, bf16[2048,512]{1,0:T(8,128)(2,1)S(1)} %copy-done.43), kind=kOutput, calls=%fused_computation.11 | convolution fusion | flops 4296015872 | bytes 12582912 | tf_op jit(solution)/shard_map/dot_general | solution.py:19
  639.2 2.6 add_convert_fusion.2
  641.9 2.5 add_convert_fusion.3
  644.4 3.6 collective-permute-done.40
  648.9 1.8 constant_dynamic-slice_fusion.1
  661.9 7.8 %collective-permute-start.46 = (bf16[256,512]{0,1:T(8,128)(2,1)S(1)}, bf16[256,512]{0,1:T(8,128)(2,1)S(1)}, u32[]{:S(2)}, u32[]{:S(2)}) collective-permute-start(bf16[256,512]{0,1:T(8,128)(2,1)S(1)} %get-tuple-element.385), channel_id=1, source_target_pairs={{0,8},{4,12},{1,9},{5,13},{2,10},{6,14},{3,11},{7,15}} | collective-permute-start | bytes 786440 | tf_op jit(solution)/shard_map/ppermute | solution.py:548
  671.3 12.1 %collective-permute-done.43 = bf16[2048,256]{1,0:T(8,128)(2,1)} collective-permute-done((bf16[2048,256]{1,0:T(8,128)(2,1)}, bf16[2048,256]{1,0:T(8,128)(2,1)}, u32[]{:S(2)}, u32[]{:S(2)}) %collective-permute-start.43) | collective-permute-done | bytes 1048608 | tf_op jit(solution)/shard_map/ppermute | solution.py:37
  683.5 5.0 collective-permute-start.51
  688.5 2.3 collective-permute-start.50
  693.0 2.0 convert_add_fusion.1
  695.0 2.2 convert_add_fusion.2
  698.1 4.5 collective-permute-start.54
  702.6 3.9 fusion.4
  706.5 7.6 %collective-permute-done.54 = bf16[256,512]{0,1:T(8,128)(2,1)S(1)} collective-permute-done((bf16[256,512]{0,1:T(8,128)(2,1)S(1)}, bf16[256,512]{0,1:T(8,128)(2,1)S(1)}, u32[]{:S(2)}, u32[]{:S(2)}) %collective-permute-start.54) | collective-permute-done | bytes 262176 | tf_op jit(solution)/shard_map/ppermute | solution.py:548
  716.4 3.7 collective-permute-start.56
  723.9 4.1 fusion
  727.9 3.5 collective-permute-done.56
  733.8 5.0 reduce-scatter.11.cloned.1.call-done
  (285 shorter events, 99.6 us)
Async XLA Ops:
  7.2 88.1 %all-gather.4.cloned.1.call-start = ((), (), s32[]{:S(2)}) async-start(), calls=%async_computation.4 | async-start | bytes 9437184 | tf_op jit(solution)/shard_map/all_gather | solution.py:513
  10.4 252.7 %all-gather.6.cloned.1.call-start = ((), (), s32[]{:S(2)}) async-start(), calls=%async_computation.5 | async-start | bytes 18874368 | tf_op jit(solution)/shard_map/all_gather | solution.py:513
  11.3 48.6 %collective-permute-start.3 = (bf16[2048,512]{1,0:T(8,128)(2,1)S(1)}, bf16[2048,512]{1,0:T(8,128)(2,1)S(1)}, u32[]{:S(2)}, u32[]{:S(2)}) collective-permute-start(bf16[2048,512]{1,0:T(8,128)(2,1)S(1)} %copy-done.5), channel_id=1, source_target_pairs={{0,2},{2,0},{1,3},{3,1},{4,6},{6,4},{5,7},{7,5},{8,10},{10,8},{9,1... | collective-permute-start | bytes 6291464 | tf_op jit(solution)/shard_map/ppermute | solution.py:41
  14.3 47.1 %collective-permute-start.2 = (bf16[2048,512]{1,0:T(8,128)(2,1)S(1)}, bf16[2048,512]{1,0:T(8,128)(2,1)S(1)}, u32[]{:S(2)}, u32[]{:S(2)}) collective-permute-start(bf16[2048,512]{1,0:T(8,128)(2,1)S(1)} %copy-done.5), channel_id=1, source_target_pairs={{0,1},{1,0},{2,3},{3,2},{4,5},{5,4},{6,7},{7,6},{8,9},{9,8},{10,11... | collective-permute-start | bytes 6291464 | tf_op jit(solution)/shard_map/ppermute | solution.py:37
  62.7 24.1 %collective-permute-start.4 = (bf16[2048,256]{1,0:T(8,128)(2,1)}, bf16[2048,256]{1,0:T(8,128)(2,1)}, u32[]{:S(2)}, u32[]{:S(2)}) collective-permute-start(bf16[2048,256]{1,0:T(8,128)(2,1)} %slice.60), channel_id=1, source_target_pairs={{0,1},{1,0},{2,3},{3,2},{4,5},{5,4},{6,7},{7,6},{8,9},{9,8},{10,11... | collective-permute-start | bytes 3145736 | tf_op jit(solution)/shard_map/ppermute | solution.py:37
  64.1 23.6 %collective-permute-start.5 = (bf16[2048,256]{1,0:T(8,128)(2,1)S(1)}, bf16[2048,256]{1,0:T(8,128)(2,1)}, u32[]{:S(2)}, u32[]{:S(2)}) collective-permute-start(bf16[2048,256]{1,0:T(8,128)(2,1)S(1)} %slice.61), channel_id=1, source_target_pairs={{0,2},{2,0},{1,3},{3,1},{4,6},{6,4},{5,7},{7,5},{8,10},{10,8},{9,1... | collective-permute-start | bytes 3145736 | tf_op jit(solution)/shard_map/ppermute | solution.py:41
  87.8 253.8 %all-gather.8.cloned.1.call-start = ((), (), s32[]{:S(2)}) async-start(), calls=%async_computation.6 | async-start | bytes 9437184 | tf_op jit(solution)/shard_map/all_gather | solution.py:513
  91.0 36.2 %collective-permute-start.6 = (bf16[2048,128]{1,0:T(8,128)(2,1)}, bf16[2048,128]{1,0:T(8,128)(2,1)}, u32[]{:S(2)}, u32[]{:S(2)}) collective-permute-start(bf16[2048,128]{1,0:T(8,128)(2,1)} %slice.59), channel_id=1, source_target_pairs={{0,3},{3,0},{1,2},{2,1},{4,7},{7,4},{5,6},{6,5},{8,11},{11,8},{9,1... | collective-permute-start | bytes 1572872 | tf_op jit(solution)/shard_map/ppermute | solution.py:45
  96.6 30.7 %collective-permute-start.1 = (bf16[1024,512]{1,0:T(8,128)(2,1)S(1)}, bf16[1024,512]{1,0:T(8,128)(2,1)S(1)}, u32[]{:S(2)}, u32[]{:S(2)}) collective-permute-start(bf16[1024,512]{1,0:T(8,128)(2,1)S(1)} %constant_dynamic-slice_fusion.3.refs_5_), channel_id=1, source_target_pairs={{0,2},{2,0},{1,3},{3,1},{4,6},{6,4},{5,7},{7,5},{8,10},{10,8},{9,1... | collective-permute-start | bytes 3145736 | tf_op jit(solution)/shard_map/ppermute | solution.py:41
  98.2 29.1 %collective-permute-start = (bf16[1024,512]{1,0:T(8,128)(2,1)S(1)}, bf16[1024,512]{1,0:T(8,128)(2,1)S(1)}, u32[]{:S(2)}, u32[]{:S(2)}) collective-permute-start(bf16[1024,512]{1,0:T(8,128)(2,1)S(1)} %constant_dynamic-slice_fusion.3.refs_5_), channel_id=1, source_target_pairs={{0,1},{1,0},{2,3},{3,2},{4,5},{5,4},{6,7},{7,6},{8,9},{9,8},{10,11... | collective-permute-start | bytes 3145736 | tf_op jit(solution)/shard_map/ppermute | solution.py:37
  129.3 332.4 %reduce-scatter.5.cloned.1.call-start = ((), (), s32[]{:S(2)}) async-start(), calls=%async_computation.7 | async-start | bytes 9437184 | tf_op jit(solution)/shard_map/reduce_scatter | solution.py:517
  129.4 48.8 %collective-permute-start.8 = (bf16[2048,512]{1,0:T(8,128)(2,1)}, bf16[2048,512]{1,0:T(8,128)(2,1)S(1)}, u32[]{:S(2)}, u32[]{:S(2)}) collective-permute-start(bf16[2048,512]{1,0:T(8,128)(2,1)} %get-tuple-element.205.refs_0_), channel_id=1, source_target_pairs={{0,2},{2,0},{1,3},{3,1},{4,6},{6,4},{5,7},{7,5},{8,10},{10,8},{9,1... | collective-permute-start | bytes 6291464 | tf_op jit(solution)/shard_map/ppermute | solution.py:41
  129.7 48.6 %collective-permute-start.7 = (bf16[2048,512]{1,0:T(8,128)(2,1)}, bf16[2048,512]{1,0:T(8,128)(2,1)S(1)}, u32[]{:S(2)}, u32[]{:S(2)}) collective-permute-start(bf16[2048,512]{1,0:T(8,128)(2,1)} %get-tuple-element.205.refs_0_), channel_id=1, source_target_pairs={{0,1},{1,0},{2,3},{3,2},{4,5},{5,4},{6,7},{7,6},{8,9},{9,8},{10,11... | collective-permute-start | bytes 6291464 | tf_op jit(solution)/shard_map/ppermute | solution.py:37
  130.7 49.8 %collective-permute-start.13 = (bf16[1024,512]{1,0:T(8,128)(2,1)S(1)}, bf16[1024,512]{1,0:T(8,128)(2,1)S(1)}, u32[]{:S(2)}, u32[]{:S(2)}) collective-permute-start(bf16[1024,512]{1,0:T(8,128)(2,1)S(1)} %constant_dynamic-slice_fusion.3.refs_5_), channel_id=1, source_target_pairs={{0,4},{4,0},{8,12},{12,8},{16,20},{20,16},{24,28},{28,24},{1,5},{5... | collective-permute-start | bytes 3145736 | tf_op jit(solution)/shard_map/ppermute | solution.py:535
  131.8 84.6 %collective-permute-start.14 = (bf16[1024,512]{1,0:T(8,128)(2,1)}, bf16[1024,512]{1,0:T(8,128)(2,1)S(1)}, u32[]{:S(2)}, u32[]{:S(2)}) collective-permute-start(bf16[1024,512]{1,0:T(8,128)(2,1)} %copy-done.39), channel_id=1, source_target_pairs={{0,4},{4,0},{8,12},{12,8},{16,20},{20,16},{24,28},{28,24},{1,5},{5... | collective-permute-start | bytes 3145736 | tf_op jit(solution)/shard_map/ppermute | solution.py:535
  132.3 57.1 %collective-permute-start.12 = (bf16[512,512]{1,0:T(8,128)(2,1)S(1)}, bf16[512,512]{1,0:T(8,128)(2,1)S(1)}, u32[]{:S(2)}, u32[]{:S(2)}) collective-permute-start(bf16[512,512]{1,0:T(8,128)(2,1)S(1)} %slice.67), channel_id=1, source_target_pairs={{0,2},{2,0},{1,3},{3,1},{4,6},{6,4},{5,7},{7,5},{8,10},{10,8},{9,1... | collective-permute-start | bytes 1572872 | tf_op jit(solution)/shard_map/ppermute | solution.py:41
  178.2 38.1 %collective-permute-start.15 = (bf16[1024,512]{1,0:T(8,128)(2,1)}, bf16[1024,512]{1,0:T(8,128)(2,1)S(1)}, u32[]{:S(2)}, u32[]{:S(2)}) collective-permute-start(bf16[1024,512]{1,0:T(8,128)(2,1)} %copy-done.37), channel_id=1, source_target_pairs={{0,4},{4,0},{8,12},{12,8},{16,20},{20,16},{24,28},{28,24},{1,5},{5... | collective-permute-start | bytes 3145736 | tf_op jit(solution)/shard_map/ppermute | solution.py:535
  180.2 36.2 %collective-permute-start.9 = (bf16[2048,256]{1,0:T(8,128)(2,1)S(1)}, bf16[2048,256]{1,0:T(8,128)(2,1)S(1)}, u32[]{:S(2)}, u32[]{:S(2)}) collective-permute-start(bf16[2048,256]{1,0:T(8,128)(2,1)S(1)} %slice.64), channel_id=1, source_target_pairs={{0,1},{1,0},{2,3},{3,2},{4,5},{5,4},{6,7},{7,6},{8,9},{9,8},{10,11... | collective-permute-start | bytes 3145736 | tf_op jit(solution)/shard_map/ppermute | solution.py:37
  180.4 36.0 %collective-permute-start.10 = (bf16[2048,256]{1,0:T(8,128)(2,1)S(1)}, bf16[2048,256]{1,0:T(8,128)(2,1)S(1)}, u32[]{:S(2)}, u32[]{:S(2)}) collective-permute-start(bf16[2048,256]{1,0:T(8,128)(2,1)S(1)} %slice.65), channel_id=1, source_target_pairs={{0,2},{2,0},{1,3},{3,1},{4,6},{6,4},{5,7},{7,5},{8,10},{10,8},{9,1... | collective-permute-start | bytes 3145736 | tf_op jit(solution)/shard_map/ppermute | solution.py:41
  189.5 26.9 %collective-permute-start.11 = (bf16[512,512]{1,0:T(8,128)(2,1)S(1)}, bf16[512,512]{1,0:T(8,128)(2,1)S(1)}, u32[]{:S(2)}, u32[]{:S(2)}) collective-permute-start(bf16[512,512]{1,0:T(8,128)(2,1)S(1)} %slice.66), channel_id=1, source_target_pairs={{0,1},{1,0},{2,3},{3,2},{4,5},{5,4},{6,7},{7,6},{8,9},{9,8},{10,11... | collective-permute-start | bytes 1572872 | tf_op jit(solution)/shard_map/ppermute | solution.py:37
  219.1 90.9 %collective-permute-start.19 = (bf16[2048,512]{1,0:T(8,128)(2,1)S(1)}, bf16[2048,512]{1,0:T(8,128)(2,1)}, u32[]{:S(2)}, u32[]{:S(2)}) collective-permute-start(bf16[2048,512]{1,0:T(8,128)(2,1)S(1)} %copy-done.4), channel_id=1, source_target_pairs={{0,2},{2,0},{1,3},{3,1},{4,6},{6,4},{5,7},{7,5},{8,10},{10,8},{9,1... | collective-permute-start | bytes 6291464 | tf_op jit(solution)/shard_map/ppermute | solution.py:41
  219.3 90.7 %collective-permute-start.18 = (bf16[2048,512]{1,0:T(8,128)(2,1)S(1)}, bf16[2048,512]{1,0:T(8,128)(2,1)}, u32[]{:S(2)}, u32[]{:S(2)}) collective-permute-start(bf16[2048,512]{1,0:T(8,128)(2,1)S(1)} %copy-done.4), channel_id=1, source_target_pairs={{0,1},{1,0},{2,3},{3,2},{4,5},{5,4},{6,7},{7,6},{8,9},{9,8},{10,11... | collective-permute-start | bytes 6291464 | tf_op jit(solution)/shard_map/ppermute | solution.py:37
  220.2 89.7 %collective-permute-start.20 = (bf16[2048,384]{1,0:T(8,128)(2,1)}, bf16[2048,384]{1,0:T(8,128)(2,1)}, u32[]{:S(2)}, u32[]{:S(2)}) collective-permute-start(bf16[2048,384]{1,0:T(8,128)(2,1)} %slice.68), channel_id=1, source_target_pairs={{0,3},{3,0},{1,2},{2,1},{4,7},{7,4},{5,6},{6,5},{8,11},{11,8},{9,1... | collective-permute-start | bytes 4718600 | tf_op jit(solution)/shard_map/ppermute | solution.py:45
  341.0 209.1 %reduce-scatter.7.cloned.1.call-start = ((), (), s32[]{:S(2)}) async-start(), calls=%async_computation.8 | async-start | bytes 9437184 | tf_op jit(solution)/shard_map/reduce_scatter | solution.py:517
  381.9 24.5 %collective-permute-start.21 = (bf16[512,1024]{1,0:T(8,128)(2,1)}, bf16[512,1024]{1,0:T(8,128)(2,1)S(1)}, u32[]{:S(2)}, u32[]{:S(2)}) collective-permute-start(bf16[512,1024]{1,0:T(8,128)(2,1)} %get-tuple-element.236), channel_id=1, source_target_pairs={{0,1},{1,0},{2,3},{3,2},{4,5},{5,4},{6,7},{7,6},{8,9},{9,8},{10,11... | collective-permute-start | bytes 3145736 | tf_op jit(solution)/shard_map/ppermute | solution.py:37
  382.0 24.6 %collective-permute-start.22 = (bf16[512,1024]{1,0:T(8,128)(2,1)}, bf16[512,1024]{1,0:T(8,128)(2,1)S(1)}, u32[]{:S(2)}, u32[]{:S(2)}) collective-permute-start(bf16[512,1024]{1,0:T(8,128)(2,1)} %get-tuple-element.237), channel_id=1, source_target_pairs={{0,2},{2,0},{1,3},{3,1},{4,6},{6,4},{5,7},{7,5},{8,10},{10,8},{9,1... | collective-permute-start | bytes 3145736 | tf_op jit(solution)/shard_map/ppermute | solution.py:41
  406.5 28.5 %collective-permute-start.23 = (bf16[512,1024]{1,0:T(8,128)(2,1)S(1)}, bf16[512,1024]{1,0:T(8,128)(2,1)S(1)}, u32[]{:S(2)}, u32[]{:S(2)}) collective-permute-start(bf16[512,1024]{1,0:T(8,128)(2,1)S(1)} %copy-done.53), channel_id=1, source_target_pairs={{0,1},{1,0},{2,3},{3,2},{4,5},{5,4},{6,7},{7,6},{8,9},{9,8},{10,11... | collective-permute-start | bytes 3145736 | tf_op jit(solution)/shard_map/ppermute | solution.py:37
  408.2 26.9 %collective-permute-start.24 = (bf16[512,1024]{1,0:T(8,128)(2,1)}, bf16[512,1024]{1,0:T(8,128)(2,1)S(1)}, u32[]{:S(2)}, u32[]{:S(2)}) collective-permute-start(bf16[512,1024]{1,0:T(8,128)(2,1)} %get-tuple-element.246), channel_id=1, source_target_pairs={{0,2},{2,0},{1,3},{3,1},{4,6},{6,4},{5,7},{7,5},{8,10},{10,8},{9,1... | collective-permute-start | bytes 3145736 | tf_op jit(solution)/shard_map/ppermute | solution.py:41
  435.1 25.6 %collective-permute-start.25 = (bf16[512,1024]{1,0:T(8,128)(2,1)}, bf16[512,1024]{1,0:T(8,128)(2,1)S(1)}, u32[]{:S(2)}, u32[]{:S(2)}) collective-permute-start(bf16[512,1024]{1,0:T(8,128)(2,1)} %get-tuple-element.259), channel_id=1, source_target_pairs={{0,1},{1,0},{2,3},{3,2},{4,5},{5,4},{6,7},{7,6},{8,9},{9,8},{10,11... | collective-permute-start | bytes 3145736 | tf_op jit(solution)/shard_map/ppermute | solution.py:37
  435.6 25.1 %collective-permute-start.26 = (bf16[512,1024]{1,0:T(8,128)(2,1)}, bf16[512,1024]{1,0:T(8,128)(2,1)}, u32[]{:S(2)}, u32[]{:S(2)}) collective-permute-start(bf16[512,1024]{1,0:T(8,128)(2,1)} %get-tuple-element.260), channel_id=1, source_target_pairs={{0,2},{2,0},{1,3},{3,1},{4,6},{6,4},{5,7},{7,5},{8,10},{10,8},{9,1... | collective-permute-start | bytes 3145736 | tf_op jit(solution)/shard_map/ppermute | solution.py:41
  461.7 187.2 %reduce-scatter.9.cloned.1.call-start = ((), (), s32[]{:S(2)}) async-start(), calls=%async_computation.9 | async-start | bytes 9437184 | tf_op jit(solution)/shard_map/reduce_scatter | solution.py:517
  470.2 44.6 %collective-permute-start.28 = (bf16[512,2048]{1,0:T(8,128)(2,1)}, bf16[512,2048]{1,0:T(8,128)(2,1)}, u32[]{:S(2)}, u32[]{:S(2)}) collective-permute-start(bf16[512,2048]{1,0:T(8,128)(2,1)} %get-tuple-element.267.refs_0_), channel_id=1, source_target_pairs={{0,2},{2,0},{1,3},{3,1},{4,6},{6,4},{5,7},{7,5},{8,10},{10,8},{9,1... | collective-permute-start | bytes 6291464 | tf_op jit(solution)/shard_map/ppermute | solution.py:41
  470.6 44.7 %collective-permute-start.27 = (bf16[512,2048]{1,0:T(8,128)(2,1)}, bf16[512,2048]{1,0:T(8,128)(2,1)}, u32[]{:S(2)}, u32[]{:S(2)}) collective-permute-start(bf16[512,2048]{1,0:T(8,128)(2,1)} %get-tuple-element.267.refs_0_), channel_id=1, source_target_pairs={{0,1},{1,0},{2,3},{3,2},{4,5},{5,4},{6,7},{7,6},{8,9},{9,8},{10,11... | collective-permute-start | bytes 6291464 | tf_op jit(solution)/shard_map/ppermute | solution.py:37
  515.4 223.4 %reduce-scatter.11.cloned.1.call-start = ((), (), s32[]{:S(2)}) async-start(), calls=%async_computation.10 | async-start | bytes 7077888 | tf_op jit(solution)/shard_map/reduce_scatter | solution.py:517
  518.8 26.9 %collective-permute-start.30 = (bf16[256,2048]{1,0:T(8,128)(2,1)S(1)}, bf16[256,2048]{1,0:T(8,128)(2,1)S(1)}, u32[]{:S(2)}, u32[]{:S(2)}) collective-permute-start(bf16[256,2048]{1,0:T(8,128)(2,1)S(1)} %slice.71), channel_id=1, source_target_pairs={{0,2},{2,0},{1,3},{3,1},{4,6},{6,4},{5,7},{7,5},{8,10},{10,8},{9,1... | collective-permute-start | bytes 3145736 | tf_op jit(solution)/shard_map/ppermute | solution.py:41
  520.0 25.7 %collective-permute-start.29 = (bf16[256,2048]{1,0:T(8,128)(2,1)S(1)}, bf16[256,2048]{1,0:T(8,128)(2,1)S(1)}, u32[]{:S(2)}, u32[]{:S(2)}) collective-permute-start(bf16[256,2048]{1,0:T(8,128)(2,1)S(1)} %slice.70), channel_id=1, source_target_pairs={{0,1},{1,0},{2,3},{3,2},{4,5},{5,4},{6,7},{7,6},{8,9},{9,8},{10,11... | collective-permute-start | bytes 3145736 | tf_op jit(solution)/shard_map/ppermute | solution.py:37
  550.0 41.8 %collective-permute-start.34 = (bf16[2048,256]{1,0:T(8,128)(2,1)}, bf16[2048,256]{1,0:T(8,128)(2,1)S(1)}, u32[]{:S(2)}, u32[]{:S(2)}) collective-permute-start(bf16[2048,256]{1,0:T(8,128)(2,1)} %get-tuple-element.302), channel_id=1, source_target_pairs={{0,2},{2,0},{1,3},{3,1},{4,6},{6,4},{5,7},{7,5},{8,10},{10,8},{9,1... | collective-permute-start | bytes 3145736 | tf_op jit(solution)/shard_map/ppermute | solution.py:41
  551.5 40.4 %collective-permute-start.33 = (bf16[2048,256]{1,0:T(8,128)(2,1)}, bf16[2048,256]{1,0:T(8,128)(2,1)S(1)}, u32[]{:S(2)}, u32[]{:S(2)}) collective-permute-start(bf16[2048,256]{1,0:T(8,128)(2,1)} %get-tuple-element.300), channel_id=1, source_target_pairs={{0,1},{1,0},{2,3},{3,2},{4,5},{5,4},{6,7},{7,6},{8,9},{9,8},{10,11... | collective-permute-start | bytes 3145736 | tf_op jit(solution)/shard_map/ppermute | solution.py:37
  553.0 42.5 %collective-permute-start.32 = (bf16[2048,256]{1,0:T(8,128)(2,1)}, bf16[2048,256]{1,0:T(8,128)(2,1)S(1)}, u32[]{:S(2)}, u32[]{:S(2)}) collective-permute-start(bf16[2048,256]{1,0:T(8,128)(2,1)} %get-tuple-element.298), channel_id=1, source_target_pairs={{0,2},{2,0},{1,3},{3,1},{4,6},{6,4},{5,7},{7,5},{8,10},{10,8},{9,1... | collective-permute-start | bytes 3145736 | tf_op jit(solution)/shard_map/ppermute | solution.py:41
  553.5 43.2 %collective-permute-start.31 = (bf16[2048,256]{1,0:T(8,128)(2,1)}, bf16[2048,256]{1,0:T(8,128)(2,1)}, u32[]{:S(2)}, u32[]{:S(2)}) collective-permute-start(bf16[2048,256]{1,0:T(8,128)(2,1)} %get-tuple-element.296), channel_id=1, source_target_pairs={{0,1},{1,0},{2,3},{3,2},{4,5},{5,4},{6,7},{7,6},{8,9},{9,8},{10,11... | collective-permute-start | bytes 3145736 | tf_op jit(solution)/shard_map/ppermute | solution.py:37
  597.5 28.0 %collective-permute-start.37 = (f32[16,128]{1,0:T(8,128)S(1)}, f32[16,128]{1,0:T(8,128)S(1)}, u32[]{:S(2)}, u32[]{:S(2)}) collective-permute-start(f32[16,128]{1,0:T(8,128)S(1)} %bitcast.74), channel_id=1, source_target_pairs={{0,1},{1,0},{2,3},{3,2},{4,5},{5,4},{6,7},{7,6},{8,9},{9,8},{10,11... | collective-permute-start | bytes 24584 | tf_op jit(solution)/shard_map/ppermute | solution.py:37
  599.1 26.5 %collective-permute-start.38 = (f32[2,4,512]{2,1,0:T(4,128)S(1)}, f32[2,4,512]{2,1,0:T(4,128)S(1)}, u32[]{:S(2)}, u32[]{:S(2)}) collective-permute-start(f32[2,4,512]{2,1,0:T(4,128)S(1)} %reshape.69), channel_id=1, source_target_pairs={{0,1},{1,0},{2,3},{3,2},{4,5},{5,4},{6,7},{7,6},{8,9},{9,8},{10,11... | collective-permute-start | bytes 49160 | tf_op jit(solution)/shard_map/ppermute | solution.py:37
  599.6 25.9 %collective-permute-start.35 = (bf16[2048,256]{1,0:T(8,128)(2,1)}, bf16[2048,256]{1,0:T(8,128)(2,1)}, u32[]{:S(2)}, u32[]{:S(2)}) collective-permute-start(bf16[2048,256]{1,0:T(8,128)(2,1)} %get-tuple-element.322), channel_id=1, source_target_pairs={{0,1},{1,0},{2,3},{3,2},{4,5},{5,4},{6,7},{7,6},{8,9},{9,8},{10,11... | collective-permute-start | bytes 3145736 | tf_op jit(solution)/shard_map/ppermute | solution.py:37
  601.1 24.5 %collective-permute-start.36 = (bf16[2048,256]{1,0:T(8,128)(2,1)}, bf16[2048,256]{1,0:T(8,128)(2,1)}, u32[]{:S(2)}, u32[]{:S(2)}) collective-permute-start(bf16[2048,256]{1,0:T(8,128)(2,1)} %get-tuple-element.323), channel_id=1, source_target_pairs={{0,2},{2,0},{1,3},{3,1},{4,6},{6,4},{5,7},{7,5},{8,10},{10,8},{9,1... | collective-permute-start | bytes 3145736 | tf_op jit(solution)/shard_map/ppermute | solution.py:41
  657.5 25.9 %collective-permute-start.43 = (bf16[2048,256]{1,0:T(8,128)(2,1)}, bf16[2048,256]{1,0:T(8,128)(2,1)}, u32[]{:S(2)}, u32[]{:S(2)}) collective-permute-start(bf16[2048,256]{1,0:T(8,128)(2,1)} %add_convert_fusion.3), channel_id=1, source_target_pairs={{0,1},{1,0},{2,3},{3,2},{4,5},{5,4},{6,7},{7,6},{8,9},{9,8},{10,11... | collective-permute-start | bytes 3145736 | tf_op jit(solution)/shard_map/ppermute | solution.py:37
  658.1 25.4 %collective-permute-start.44 = (bf16[2048,256]{1,0:T(8,128)(2,1)S(1)}, bf16[2048,256]{1,0:T(8,128)(2,1)}, u32[]{:S(2)}, u32[]{:S(2)}) collective-permute-start(bf16[2048,256]{1,0:T(8,128)(2,1)S(1)} %copy-done.20), channel_id=1, source_target_pairs={{0,2},{2,0},{1,3},{3,1},{4,6},{6,4},{5,7},{7,5},{8,10},{10,8},{9,1... | collective-permute-start | bytes 3145736 | tf_op jit(solution)/shard_map/ppermute | solution.py:41
  690.8 24.2 %collective-permute-start.53 = (bf16[2048,256]{1,0:T(8,128)(2,1)S(1)}, bf16[2048,256]{1,0:T(8,128)(2,1)S(1)}, u32[]{:S(2)}, u32[]{:S(2)}) collective-permute-start(bf16[2048,256]{1,0:T(8,128)(2,1)S(1)} %copy-done.19), channel_id=1, source_target_pairs={{0,2},{2,0},{1,3},{3,1},{4,6},{6,4},{5,7},{7,5},{8,10},{10,8},{9,1... | collective-permute-start | bytes 3145736 | tf_op jit(solution)/shard_map/ppermute | solution.py:41
  691.5 24.1 %collective-permute-start.52 = (bf16[2048,256]{1,0:T(8,128)(2,1)S(1)}, bf16[2048,256]{1,0:T(8,128)(2,1)S(1)}, u32[]{:S(2)}, u32[]{:S(2)}) collective-permute-start(bf16[2048,256]{1,0:T(8,128)(2,1)S(1)} %copy-done.18), channel_id=1, source_target_pairs={{0,1},{1,0},{2,3},{3,2},{4,5},{5,4},{6,7},{7,6},{8,9},{9,8},{10,11... | collective-permute-start | bytes 3145736 | tf_op jit(solution)/shard_map/ppermute | solution.py:37
  (75 other events, 1120.8 us)
Sparse Core Ops, SparseCore 0:
  10.5 84.7 all-gather.3
  97.5 149.6 all-gather.5
  248.8 80.7 all-gather.7
  341.1 88.5 reduce-scatter.4
  460.9 89.0 reduce-scatter.6
  552.2 87.9 reduce-scatter.8
  649.0 89.6 reduce-scatter.10

commit v4 on v3

--- a/solution.py
+++ b/solution.py
@@ -634,9 +634,7 @@
                 to_y(halves(x_mix, 1)[1]),
                 low_out,
                 high_out,
-                to_core(own_out),
-                to_core(x_out),
-                to_core(y_out),
+                *[to_core(after(block, x_mix, y_mix)) for block in (own_out, x_out, y_out)],
             )
         )
         far = [to_core(low_out), to_core(high_out)]

time: 751 us -> 746 us (level)
    unnamed x119 -> x121, local copies, waits for them, and re-layouts: 15.1 us -> 14.6 us
  transfers between devices with their start and end apart: 65 -> 65, of which waited for: 25 -> 27; matrix products, arithmetic and copies ran while one was open for 22% -> 22% of each run, Pallas kernels for 37% -> 37%
where the time goes in v4:
time: 746 us; the launch traced here: 743 us
  Pallas kernels  276 us (37%)
  waiting for transfers between devices  198 us (27%)
  matrix products  100 us (13%)
  starting transfers between devices  72.8 us (10%)
  other arithmetic  42.4 us (6%)
  local copies, waits for them, and re-layouts  38.4 us (5%)
  between operations  15.2 us (2%)
    pallas_call x11, Pallas kernels, run(): pl.pallas_call(kernel, grid_spec=pltpu.PrefetchScalarGridSpec(num_scalar_...  276 us
    ppermute x20, waiting for transfers between devices, to_y(): return lax.ppermute(values, 'narrow', ALONG_Y)  114 us
    dot_general x5, matrix products, contract_rows(): lax.dot_general(left, right, (((0,), (0,)), ((), ())), preferred_element_...  100 us
    ppermute x20, waiting for transfers between devices, to_x(): return lax.ppermute(values, 'narrow', ALONG_X)  58.7 us
    ppermute x20, starting transfers between devices, to_x(): return lax.ppermute(values, 'narrow', ALONG_X)  21.7 us
    ppermute x20, starting transfers between devices, to_y(): return lax.ppermute(values, 'narrow', ALONG_Y)  21 us
    ppermute x3, starting transfers between devices, line_step(): lax.ppermute(with_own(right, z + 4 - step), 'wide', [(w, w + 2) for w in...  16 us
  transfers between devices with their start and end apart: 65, of which 27 were waited for; matrix products, arithmetic and copies ran while one was open for 22% of the time, Pallas kernels for 37%

profile of v4, /device:TPU:0, one launch (start us, length us, event | category | flops | bytes accessed | tf_op | source)
XLA Modules:
  0.0 743.5 jit_solution(8036389226996944864)
XLA Ops:
  11.3 3.0 collective-permute-start.3
  15.8 44.1 %collective-permute-done.3.refs_2_ = bf16[2048,512]{1,0:T(8,128)(2,1)S(1)} collective-permute-done((bf16[2048,512]{1,0:T(8,128)(2,1)S(1)}, bf16[2048,512]{1,0:T(8,128)(2,1)S(1)}, u32[]{:S(2)}, u32[]{:S(2)}) %collective-permute-start.3) | collective-permute-done | bytes 2097184 | tf_op jit(solution)/shard_map/ppermute | solution.py:41
  66.3 20.5 %collective-permute-done.4.refs_3_ = bf16[2048,256]{1,0:T(8,128)(2,1)} collective-permute-done((bf16[2048,256]{1,0:T(8,128)(2,1)}, bf16[2048,256]{1,0:T(8,128)(2,1)}, u32[]{:S(2)}, u32[]{:S(2)}) %collective-permute-start.4) | collective-permute-done | bytes 1048608 | tf_op jit(solution)/shard_map/ppermute | solution.py:37
  92.4 2.9 all-gather.4.cloned.1.call-done.refs_6_.refs_10_
  99.7 27.6 %shard_map.187 = (bf16[2048,2048]{1,0:T(8,128)(2,1)}, bf16[2048,2048]{1,0:T(8,128)(2,1)}, f32[2048,1536]{1,0:T(8,128)}, f32[2048,512]{1,0:T(8,128)}, bf16[2048,512]{1,0:T(8,128)(2,1)}, /*index=5*/f32[2048,1]{1,0:T(8,128)}) custom-call(s32[1]{0:T(128)} %bitcast.2.me_ref._, bf16[2048,512]{1,0:T(8,128)(2,1)} %refs_0_.2, bf16[2048,512]{1,0:T(8,128)(2,1)} %copy-done.34, ...), custom_call_target="tpu_custom_call" | custom-call | flops 12884901888 | bytes 52467712 | tf_op jit(solution)/shard_map/pallas_call | solution.py:80
  133.9 1.9 collective-permute-start.11
  135.8 42.4 %collective-permute-done.8.refs_2_ = bf16[2048,512]{1,0:T(8,128)(2,1)S(1)} collective-permute-done((bf16[2048,512]{1,0:T(8,128)(2,1)}, bf16[2048,512]{1,0:T(8,128)(2,1)S(1)}, u32[]{:S(2)}, u32[]{:S(2)}) %collective-permute-start.8) | collective-permute-done | bytes 2097184 | tf_op jit(solution)/shard_map/ppermute | solution.py:41
  181.8 7.7 %collective-permute-done.12.refs_9_ = bf16[512,512]{1,0:T(8,128)(2,1)S(1)} collective-permute-done((bf16[512,512]{1,0:T(8,128)(2,1)S(1)}, bf16[512,512]{1,0:T(8,128)(2,1)S(1)}, u32[]{:S(2)}, u32[]{:S(2)}) %collective-permute-start.12) | collective-permute-done | bytes 524320 | tf_op jit(solution)/shard_map/ppermute | solution.py:41
  190.0 20.7 %collective-permute-done.9.refs_3_ = bf16[2048,256]{1,0:T(8,128)(2,1)S(1)} collective-permute-done((bf16[2048,256]{1,0:T(8,128)(2,1)S(1)}, bf16[2048,256]{1,0:T(8,128)(2,1)S(1)}, u32[]{:S(2)}, u32[]{:S(2)}) %collective-permute-start.9) | collective-permute-done | bytes 1048608 | tf_op jit(solution)/shard_map/ppermute | solution.py:37
  218.1 39.3 %shard_map.188 = (f32[2048,2048]{1,0:T(8,128)}, bf16[2048,2048]{1,0:T(8,128)(2,1)}, f32[2048,1]{1,0:T(8,128)}) custom-call(s32[1]{0:T(128)} %bitcast.core_ref, bf16[2048,512]{1,0:T(8,128)(2,1)} %get-tuple-element.208.refs_0_, bf16[2048,512]{1,0:T(8,128)(2,1)} %copy-done.36, bf16[2048,512]{1,0:T(8,128)(2,1)} %copy-done.35, bf16[2048,256]{1,0:T(8,128)(2,1)} %copy-done.47, ...), custom_call_target="tpu_custom_call" | custom-call | flops 17179869184 | bytes 50348032 | tf_op jit(solution)/shard_map/pallas_call | solution.py:80
  257.4 47.0 %shard_map.189 = (bf16[2048,2048]{1,0:T(8,128)(2,1)}, bf16[2048,2048]{1,0:T(8,128)(2,1)}, bf16[2048,2048]{1,0:T(8,128)(2,1)}) custom-call(s32[1]{0:T(128)} %bitcast.2.me_ref._, bf16[2048,2048]{1,0:T(8,128)(2,1)} %get-tuple-element.274.n_ref, bf16[2048,4096]{1,0:T(8,128)(2,1)} %all-gather.6.cloned.1.call-done.w_ref.wg_ref.wu_ref), custom_call_target="tpu_custom_call" | custom-call | flops 34359738368 | bytes 50331648 | tf_op jit(solution)/shard_map/pallas_call | solution.py:80
  304.5 7.1 shard_map.190.g_ref.refs_8_
  311.6 23.7 %convolution_convert_fusion.2 = bf16[2048,2048]{1,0:T(8,128)(2,1)} fusion(bf16[2048,2048]{1,0:T(8,128)(2,1)} %get-tuple-element.280.l_ref, bf16[2048,2048]{1,0:T(8,128)(2,1)} %shard_map.190.g_ref.refs_8_), kind=kOutput, calls=%fused_computation.2 | convolution fusion | flops 17184063488 | bytes 25165824 | tf_op jit(solution)/shard_map/dot_general | solution.py:19
  336.0 39.9 %shard_map.191 = (bf16[512,1024]{1,0:T(8,128)(2,1)}, bf16[512,1024]{1,0:T(8,128)(2,1)}, bf16[512,1024]{1,0:T(8,128)(2,1)}, bf16[512,1024]{1,0:T(8,128)(2,1)}, bf...) custom-call(s32[2]{0:T(128)} %pad_add_fusion.1._, bf16[2048,2048]{1,0:T(8,128)(2,1)} %shard_map.190.g_ref.refs_8_, ...), custom_call_target="tpu_custom_call" | custom-call | flops 25769803776 | bytes 88080384 | tf_op jit(solution)/shard_map/pallas_call | solution.py:80
  378.0 22.6 %shard_map.192 = (bf16[512,1024]{1,0:T(8,128)(2,1)}, bf16[512,1024]{1,0:T(8,128)(2,1)}, bf16[2048,2048]{1,0:T(8,128)(2,1)}, bf16[2048,2048]{1,0:T(8,128)(2,1)}) custom-call(s32[1]{0:T(128)} %bitcast.7._, bf16[2048,2048]{1,0:T(8,128)(2,1)} %shard_map.190.g_ref.refs_8_, ...), custom_call_target="tpu_custom_call", output_to_operand_aliasing={{2}: (7, {}), {3}: (8, {})} | custom-call | flops 12884901888 | bytes 102760448 | tf_op jit(solution)/shard_map/pallas_call | solution.py:80
  403.7 3.6 add_convert_fusion.4
  407.2 22.7 %shard_map.193 = (bf16[512,1024]{1,0:T(8,128)(2,1)}, bf16[512,1024]{1,0:T(8,128)(2,1)}, bf16[2048,2048]{1,0:T(8,128)(2,1)}, bf16[2048,2048]{1,0:T(8,128)(2,1)}) custom-call(s32[1]{0:T(128)} %bitcast.2.me_ref._, bf16[2048,2048]{1,0:T(8,128)(2,1)} %shard_map.190.g_ref.refs_8_, ...), custom_call_target="tpu_custom_call", output_to_operand_aliasing={{2}: (7, {}), {3}: (8, {})} | custom-call | flops 12884901888 | bytes 102760448 | tf_op jit(solution)/shard_map/pallas_call | solution.py:80
  432.0 23.8 %convolution_convert_fusion.1 = bf16[2048,2048]{1,0:T(8,128)(2,1)} fusion(bf16[2048,2048]{1,0:T(8,128)(2,1)} %get-tuple-element.274.n_ref, bf16[2048,2048]{1,0:T(8,128)(2,1)} %get-tuple-element.267), kind=kOutput, calls=%fused_computation.1 | convolution fusion | flops 17184063488 | bytes 25165824 | tf_op jit(solution)/shard_map/dot_general | solution.py:19
  456.7 8.5 %shard_map.194 = (bf16[512,2048]{1,0:T(8,128)(2,1)}, f32[1,2048]{1,0:T(1,128)}) custom-call(s32[1]{0:T(128)} %bitcast.2.me_ref._, bf16[512,1024]{1,0:T(8,128)(2,1)} %get-tuple-element.262.refs_0_, bf16[512,1024]{1,0:T(8,128)(2,1)} %get-tuple-element.263.refs_1_, bf16[512,1024]{1,0:T(8,128)(2,1)} %copy-done.26, bf16[512,1024]{1,0:T(8,128)(2,1)} %copy-done.28, ...), custom_call_target="tpu_custom_call" | custom-call | bytes 33579008 | tf_op jit(solution)/shard_map/pallas_call | solution.py:80
  466.7 3.0 slice.69
  469.8 2.5 reshape.66
  473.5 2.0 copy.39
  475.5 23.9 %convolution_convert_fusion = bf16[2048,2048]{1,0:T(8,128)(2,1)} fusion(bf16[2048,2048]{1,0:T(8,128)(2,1)} %get-tuple-element.274.n_ref, bf16[2048,2048]{1,0:T(8,128)(2,1)} %get-tuple-element.275), kind=kOutput, calls=%fused_computation | convolution fusion | flops 17184063488 | bytes 25165824 | tf_op jit(solution)/shard_map/dot_general | solution.py:19
  499.4 10.3 %collective-permute-done.28.refs_2_ = bf16[512,2048]{1,0:T(8,128)(2,1)} collective-permute-done((bf16[512,2048]{1,0:T(8,128)(2,1)}, bf16[512,2048]{1,0:T(8,128)(2,1)}, u32[]{:S(2)}, u32[]{:S(2)}) %collective-permute-start.28) | collective-permute-done | bytes 2097184 | tf_op jit(solution)/shard_map/ppermute | solution.py:41
  515.8 24.4 %shard_map.195 = (bf16[2048,256]{1,0:T(8,128)(2,1)}, bf16[2048,256]{1,0:T(8,128)(2,1)}, bf16[2048,256]{1,0:T(8,128)(2,1)}, bf16[2048,256]{1,0:T(8,128)(2,1)}, bf...) custom-call(s32[4]{0:T(128)} %pad_add_fusion.2.own_ref, ...), custom_call_target="tpu_custom_call" | custom-call | flops 17179869184 | bytes 25165824 | tf_op jit(solution)/shard_map/pallas_call | solution.py:80
  541.6 3.8 reduce-scatter.7.cloned.1.call-done
  549.5 36.2 %shard_map.196 = (bf16[2048,256]{1,0:T(8,128)(2,1)}, bf16[2048,256]{1,0:T(8,128)(2,1)}, bf16[2048,256]{1,0:T(8,128)(2,1)}, bf16[2048,256]{1,0:T(8,128)(2,1)}, bf...) custom-call(s32[4]{0:T(128)} %pad_add_fusion.2.own_ref, ...), custom_call_target="tpu_custom_call" | custom-call | flops 17179869184 | bytes 67170304 | tf_op jit(solution)/shard_map/pallas_call | solution.py:80
  587.3 3.6 collective-permute-done.32
  597.0 19.6 %convolution_convert_fusion.3 = bf16[2048,1536]{1,0:T(8,128)(2,1)} fusion(bf16[2048,2048]{1,0:T(8,128)(2,1)} %get-tuple-element.333, bf16[2048,1536]{1,0:T(8,128)(2,1)} %get-tuple-element.334), kind=kOutput, calls=%fused_computation.3 | convolution fusion | flops 12888047616 | bytes 20971520 | tf_op jit(solution)/shard_map/dot_general | solution.py:19
  616.6 2.9 add_convert_fusion
  625.0 9.5 %convolution_convert_fusion.4 = bf16[2048,512]{1,0:T(8,128)(2,1)} fusion(bf16[2048,2048]{1,0:T(8,128)(2,1)} %get-tuple-element.350, bf16[2048,512]{1,0:T(8,128)(2,1)S(1)} %copy-done.44), kind=kOutput, calls=%fused_computation.11 | convolution fusion | flops 4296015872 | bytes 12582912 | tf_op jit(solution)/shard_map/dot_general | solution.py:19
  634.5 2.6 add_convert_fusion.2
  637.1 2.5 add_convert_fusion.3
  639.7 3.6 collective-permute-done.40
  644.2 1.8 constant_dynamic-slice_fusion.1
  657.1 7.8 %collective-permute-start.46 = (bf16[256,512]{0,1:T(8,128)(2,1)S(1)}, bf16[256,512]{0,1:T(8,128)(2,1)S(1)}, u32[]{:S(2)}, u32[]{:S(2)}) collective-permute-start(bf16[256,512]{0,1:T(8,128)(2,1)S(1)} %get-tuple-element.391), channel_id=1, source_target_pairs={{0,8},{4,12},{1,9},{5,13},{2,10},{6,14},{3,11},{7,15}} | collective-permute-start | bytes 786440 | tf_op jit(solution)/shard_map/ppermute | solution.py:548
  666.5 12.1 %collective-permute-done.43 = bf16[2048,256]{1,0:T(8,128)(2,1)} collective-permute-done((bf16[2048,256]{1,0:T(8,128)(2,1)}, bf16[2048,256]{1,0:T(8,128)(2,1)}, u32[]{:S(2)}, u32[]{:S(2)}) %collective-permute-start.43) | collective-permute-done | bytes 1048608 | tf_op jit(solution)/shard_map/ppermute | solution.py:37
  678.8 5.0 collective-permute-start.51
  683.8 2.2 collective-permute-start.50
  688.2 2.0 convert_add_fusion.1
  690.2 2.2 convert_add_fusion.2
  693.3 4.5 collective-permute-start.54
  697.8 3.9 fusion.4
  701.7 7.6 %collective-permute-done.54 = bf16[256,512]{0,1:T(8,128)(2,1)S(1)} collective-permute-done((bf16[256,512]{0,1:T(8,128)(2,1)S(1)}, bf16[256,512]{0,1:T(8,128)(2,1)S(1)}, u32[]{:S(2)}, u32[]{:S(2)}) %collective-permute-start.54) | collective-permute-done | bytes 262176 | tf_op jit(solution)/shard_map/ppermute | solution.py:548
  711.6 3.7 collective-permute-start.56
  719.1 4.1 fusion
  723.1 3.5 collective-permute-done.56
  729.0 5.0 reduce-scatter.11.cloned.1.call-done
  (287 shorter events, 103.5 us)
Async XLA Ops:
  7.2 88.1 %all-gather.4.cloned.1.call-start = ((), (), s32[]{:S(2)}) async-start(), calls=%async_computation.4 | async-start | bytes 9437184 | tf_op jit(solution)/shard_map/all_gather | solution.py:513
  10.4 247.0 %all-gather.6.cloned.1.call-start = ((), (), s32[]{:S(2)}) async-start(), calls=%async_computation.5 | async-start | bytes 18874368 | tf_op jit(solution)/shard_map/all_gather | solution.py:513
  11.3 48.6 %collective-permute-start.3 = (bf16[2048,512]{1,0:T(8,128)(2,1)S(1)}, bf16[2048,512]{1,0:T(8,128)(2,1)S(1)}, u32[]{:S(2)}, u32[]{:S(2)}) collective-permute-start(bf16[2048,512]{1,0:T(8,128)(2,1)S(1)} %copy-done.5), channel_id=1, source_target_pairs={{0,2},{2,0},{1,3},{3,1},{4,6},{6,4},{5,7},{7,5},{8,10},{10,8},{9,1... | collective-permute-start | bytes 6291464 | tf_op jit(solution)/shard_map/ppermute | solution.py:41
  14.3 47.1 %collective-permute-start.2 = (bf16[2048,512]{1,0:T(8,128)(2,1)S(1)}, bf16[2048,512]{1,0:T(8,128)(2,1)S(1)}, u32[]{:S(2)}, u32[]{:S(2)}) collective-permute-start(bf16[2048,512]{1,0:T(8,128)(2,1)S(1)} %copy-done.5), channel_id=1, source_target_pairs={{0,1},{1,0},{2,3},{3,2},{4,5},{5,4},{6,7},{7,6},{8,9},{9,8},{10,11... | collective-permute-start | bytes 6291464 | tf_op jit(solution)/shard_map/ppermute | solution.py:37
  62.7 24.1 %collective-permute-start.4 = (bf16[2048,256]{1,0:T(8,128)(2,1)}, bf16[2048,256]{1,0:T(8,128)(2,1)}, u32[]{:S(2)}, u32[]{:S(2)}) collective-permute-start(bf16[2048,256]{1,0:T(8,128)(2,1)} %slice.60), channel_id=1, source_target_pairs={{0,1},{1,0},{2,3},{3,2},{4,5},{5,4},{6,7},{7,6},{8,9},{9,8},{10,11... | collective-permute-start | bytes 3145736 | tf_op jit(solution)/shard_map/ppermute | solution.py:37
  64.1 23.6 %collective-permute-start.5 = (bf16[2048,256]{1,0:T(8,128)(2,1)S(1)}, bf16[2048,256]{1,0:T(8,128)(2,1)}, u32[]{:S(2)}, u32[]{:S(2)}) collective-permute-start(bf16[2048,256]{1,0:T(8,128)(2,1)S(1)} %slice.61), channel_id=1, source_target_pairs={{0,2},{2,0},{1,3},{3,1},{4,6},{6,4},{5,7},{7,5},{8,10},{10,8},{9,1... | collective-permute-start | bytes 3145736 | tf_op jit(solution)/shard_map/ppermute | solution.py:41
  87.8 248.2 %all-gather.8.cloned.1.call-start = ((), (), s32[]{:S(2)}) async-start(), calls=%async_computation.6 | async-start | bytes 9437184 | tf_op jit(solution)/shard_map/all_gather | solution.py:513
  91.0 36.2 %collective-permute-start.6 = (bf16[2048,128]{1,0:T(8,128)(2,1)}, bf16[2048,128]{1,0:T(8,128)(2,1)}, u32[]{:S(2)}, u32[]{:S(2)}) collective-permute-start(bf16[2048,128]{1,0:T(8,128)(2,1)} %slice.59), channel_id=1, source_target_pairs={{0,3},{3,0},{1,2},{2,1},{4,7},{7,4},{5,6},{6,5},{8,11},{11,8},{9,1... | collective-permute-start | bytes 1572872 | tf_op jit(solution)/shard_map/ppermute | solution.py:45
  96.6 30.7 %collective-permute-start.1 = (bf16[1024,512]{1,0:T(8,128)(2,1)S(1)}, bf16[1024,512]{1,0:T(8,128)(2,1)S(1)}, u32[]{:S(2)}, u32[]{:S(2)}) collective-permute-start(bf16[1024,512]{1,0:T(8,128)(2,1)S(1)} %constant_dynamic-slice_fusion.3.refs_5_), channel_id=1, source_target_pairs={{0,2},{2,0},{1,3},{3,1},{4,6},{6,4},{5,7},{7,5},{8,10},{10,8},{9,1... | collective-permute-start | bytes 3145736 | tf_op jit(solution)/shard_map/ppermute | solution.py:41
  98.2 29.1 %collective-permute-start = (bf16[1024,512]{1,0:T(8,128)(2,1)S(1)}, bf16[1024,512]{1,0:T(8,128)(2,1)S(1)}, u32[]{:S(2)}, u32[]{:S(2)}) collective-permute-start(bf16[1024,512]{1,0:T(8,128)(2,1)S(1)} %constant_dynamic-slice_fusion.3.refs_5_), channel_id=1, source_target_pairs={{0,1},{1,0},{2,3},{3,2},{4,5},{5,4},{6,7},{7,6},{8,9},{9,8},{10,11... | collective-permute-start | bytes 3145736 | tf_op jit(solution)/shard_map/ppermute | solution.py:37
  129.3 327.4 %reduce-scatter.5.cloned.1.call-start = ((), (), s32[]{:S(2)}) async-start(), calls=%async_computation.7 | async-start | bytes 9437184 | tf_op jit(solution)/shard_map/reduce_scatter | solution.py:517
  129.4 48.8 %collective-permute-start.8 = (bf16[2048,512]{1,0:T(8,128)(2,1)}, bf16[2048,512]{1,0:T(8,128)(2,1)S(1)}, u32[]{:S(2)}, u32[]{:S(2)}) collective-permute-start(bf16[2048,512]{1,0:T(8,128)(2,1)} %get-tuple-element.208.refs_0_), channel_id=1, source_target_pairs={{0,2},{2,0},{1,3},{3,1},{4,6},{6,4},{5,7},{7,5},{8,10},{10,8},{9,1... | collective-permute-start | bytes 6291464 | tf_op jit(solution)/shard_map/ppermute | solution.py:41
  129.7 48.8 %collective-permute-start.7 = (bf16[2048,512]{1,0:T(8,128)(2,1)}, bf16[2048,512]{1,0:T(8,128)(2,1)S(1)}, u32[]{:S(2)}, u32[]{:S(2)}) collective-permute-start(bf16[2048,512]{1,0:T(8,128)(2,1)} %get-tuple-element.208.refs_0_), channel_id=1, source_target_pairs={{0,1},{1,0},{2,3},{3,2},{4,5},{5,4},{6,7},{7,6},{8,9},{9,8},{10,11... | collective-permute-start | bytes 6291464 | tf_op jit(solution)/shard_map/ppermute | solution.py:37
  131.7 57.7 %collective-permute-start.12 = (bf16[512,512]{1,0:T(8,128)(2,1)S(1)}, bf16[512,512]{1,0:T(8,128)(2,1)S(1)}, u32[]{:S(2)}, u32[]{:S(2)}) collective-permute-start(bf16[512,512]{1,0:T(8,128)(2,1)S(1)} %slice.67), channel_id=1, source_target_pairs={{0,2},{2,0},{1,3},{3,1},{4,6},{6,4},{5,7},{7,5},{8,10},{10,8},{9,1... | collective-permute-start | bytes 1572872 | tf_op jit(solution)/shard_map/ppermute | solution.py:41
  133.9 55.7 %collective-permute-start.11 = (bf16[512,512]{1,0:T(8,128)(2,1)S(1)}, bf16[512,512]{1,0:T(8,128)(2,1)S(1)}, u32[]{:S(2)}, u32[]{:S(2)}) collective-permute-start(bf16[512,512]{1,0:T(8,128)(2,1)S(1)} %slice.66), channel_id=1, source_target_pairs={{0,1},{1,0},{2,3},{3,2},{4,5},{5,4},{6,7},{7,6},{8,9},{9,8},{10,11... | collective-permute-start | bytes 1572872 | tf_op jit(solution)/shard_map/ppermute | solution.py:37
  180.2 30.5 %collective-permute-start.9 = (bf16[2048,256]{1,0:T(8,128)(2,1)S(1)}, bf16[2048,256]{1,0:T(8,128)(2,1)S(1)}, u32[]{:S(2)}, u32[]{:S(2)}) collective-permute-start(bf16[2048,256]{1,0:T(8,128)(2,1)S(1)} %slice.64), channel_id=1, source_target_pairs={{0,1},{1,0},{2,3},{3,2},{4,5},{5,4},{6,7},{7,6},{8,9},{9,8},{10,11... | collective-permute-start | bytes 3145736 | tf_op jit(solution)/shard_map/ppermute | solution.py:37
  180.7 30.0 %collective-permute-start.10 = (bf16[2048,256]{1,0:T(8,128)(2,1)S(1)}, bf16[2048,256]{1,0:T(8,128)(2,1)S(1)}, u32[]{:S(2)}, u32[]{:S(2)}) collective-permute-start(bf16[2048,256]{1,0:T(8,128)(2,1)S(1)} %slice.65), channel_id=1, source_target_pairs={{0,2},{2,0},{1,3},{3,1},{4,6},{6,4},{5,7},{7,5},{8,10},{10,8},{9,1... | collective-permute-start | bytes 3145736 | tf_op jit(solution)/shard_map/ppermute | solution.py:41
  181.8 28.9 %collective-permute-start.13 = (bf16[1024,512]{1,0:T(8,128)(2,1)S(1)}, bf16[1024,512]{1,0:T(8,128)(2,1)S(1)}, u32[]{:S(2)}, u32[]{:S(2)}) collective-permute-start(bf16[1024,512]{1,0:T(8,128)(2,1)S(1)} %constant_dynamic-slice_fusion.3.refs_5_), channel_id=1, source_target_pairs={{0,4},{4,0},{8,12},{12,8},{16,20},{20,16},{24,28},{28,24},{1,5},{5... | collective-permute-start | bytes 3145736 | tf_op jit(solution)/shard_map/ppermute | solution.py:535
  213.6 90.9 %collective-permute-start.19 = (bf16[2048,512]{1,0:T(8,128)(2,1)S(1)}, bf16[2048,512]{1,0:T(8,128)(2,1)}, u32[]{:S(2)}, u32[]{:S(2)}) collective-permute-start(bf16[2048,512]{1,0:T(8,128)(2,1)S(1)} %copy-done.4), channel_id=1, source_target_pairs={{0,2},{2,0},{1,3},{3,1},{4,6},{6,4},{5,7},{7,5},{8,10},{10,8},{9,1... | collective-permute-start | bytes 6291464 | tf_op jit(solution)/shard_map/ppermute | solution.py:41
  214.9 89.6 %collective-permute-start.18 = (bf16[2048,512]{1,0:T(8,128)(2,1)S(1)}, bf16[2048,512]{1,0:T(8,128)(2,1)}, u32[]{:S(2)}, u32[]{:S(2)}) collective-permute-start(bf16[2048,512]{1,0:T(8,128)(2,1)S(1)} %copy-done.4), channel_id=1, source_target_pairs={{0,1},{1,0},{2,3},{3,2},{4,5},{5,4},{6,7},{7,6},{8,9},{9,8},{10,11... | collective-permute-start | bytes 6291464 | tf_op jit(solution)/shard_map/ppermute | solution.py:37
  215.4 89.1 %collective-permute-start.20 = (bf16[2048,384]{1,0:T(8,128)(2,1)}, bf16[2048,384]{1,0:T(8,128)(2,1)}, u32[]{:S(2)}, u32[]{:S(2)}) collective-permute-start(bf16[2048,384]{1,0:T(8,128)(2,1)} %slice.68), channel_id=1, source_target_pairs={{0,3},{3,0},{1,2},{2,1},{4,7},{7,4},{5,6},{6,5},{8,11},{11,8},{9,1... | collective-permute-start | bytes 4718600 | tf_op jit(solution)/shard_map/ppermute | solution.py:45
  335.4 210.1 %reduce-scatter.7.cloned.1.call-start = ((), (), s32[]{:S(2)}) async-start(), calls=%async_computation.8 | async-start | bytes 9437184 | tf_op jit(solution)/shard_map/reduce_scatter | solution.py:517
  375.9 24.8 %collective-permute-start.21 = (bf16[512,1024]{1,0:T(8,128)(2,1)}, bf16[512,1024]{1,0:T(8,128)(2,1)S(1)}, u32[]{:S(2)}, u32[]{:S(2)}) collective-permute-start(bf16[512,1024]{1,0:T(8,128)(2,1)} %get-tuple-element.242), channel_id=1, source_target_pairs={{0,1},{1,0},{2,3},{3,2},{4,5},{5,4},{6,7},{7,6},{8,9},{9,8},{10,11... | collective-permute-start | bytes 3145736 | tf_op jit(solution)/shard_map/ppermute | solution.py:37
  377.2 24.4 %collective-permute-start.22 = (bf16[512,1024]{1,0:T(8,128)(2,1)}, bf16[512,1024]{1,0:T(8,128)(2,1)S(1)}, u32[]{:S(2)}, u32[]{:S(2)}) collective-permute-start(bf16[512,1024]{1,0:T(8,128)(2,1)} %get-tuple-element.243), channel_id=1, source_target_pairs={{0,2},{2,0},{1,3},{3,1},{4,6},{6,4},{5,7},{7,5},{8,10},{10,8},{9,1... | collective-permute-start | bytes 3145736 | tf_op jit(solution)/shard_map/ppermute | solution.py:41
  401.6 28.4 %collective-permute-start.23 = (bf16[512,1024]{1,0:T(8,128)(2,1)S(1)}, bf16[512,1024]{1,0:T(8,128)(2,1)S(1)}, u32[]{:S(2)}, u32[]{:S(2)}) collective-permute-start(bf16[512,1024]{1,0:T(8,128)(2,1)S(1)} %copy-done.54), channel_id=1, source_target_pairs={{0,1},{1,0},{2,3},{3,2},{4,5},{5,4},{6,7},{7,6},{8,9},{9,8},{10,11... | collective-permute-start | bytes 3145736 | tf_op jit(solution)/shard_map/ppermute | solution.py:37
  402.4 27.5 %collective-permute-start.24 = (bf16[512,1024]{1,0:T(8,128)(2,1)}, bf16[512,1024]{1,0:T(8,128)(2,1)S(1)}, u32[]{:S(2)}, u32[]{:S(2)}) collective-permute-start(bf16[512,1024]{1,0:T(8,128)(2,1)} %get-tuple-element.252), channel_id=1, source_target_pairs={{0,2},{2,0},{1,3},{3,1},{4,6},{6,4},{5,7},{7,5},{8,10},{10,8},{9,1... | collective-permute-start | bytes 3145736 | tf_op jit(solution)/shard_map/ppermute | solution.py:41
  430.0 25.8 %collective-permute-start.25 = (bf16[512,1024]{1,0:T(8,128)(2,1)}, bf16[512,1024]{1,0:T(8,128)(2,1)S(1)}, u32[]{:S(2)}, u32[]{:S(2)}) collective-permute-start(bf16[512,1024]{1,0:T(8,128)(2,1)} %get-tuple-element.265), channel_id=1, source_target_pairs={{0,1},{1,0},{2,3},{3,2},{4,5},{5,4},{6,7},{7,6},{8,9},{9,8},{10,11... | collective-permute-start | bytes 3145736 | tf_op jit(solution)/shard_map/ppermute | solution.py:37
  430.7 25.1 %collective-permute-start.26 = (bf16[512,1024]{1,0:T(8,128)(2,1)}, bf16[512,1024]{1,0:T(8,128)(2,1)}, u32[]{:S(2)}, u32[]{:S(2)}) collective-permute-start(bf16[512,1024]{1,0:T(8,128)(2,1)} %get-tuple-element.266), channel_id=1, source_target_pairs={{0,2},{2,0},{1,3},{3,1},{4,6},{6,4},{5,7},{7,5},{8,10},{10,8},{9,1... | collective-permute-start | bytes 3145736 | tf_op jit(solution)/shard_map/ppermute | solution.py:41
  456.7 187.4 %reduce-scatter.9.cloned.1.call-start = ((), (), s32[]{:S(2)}) async-start(), calls=%async_computation.9 | async-start | bytes 9437184 | tf_op jit(solution)/shard_map/reduce_scatter | solution.py:517
  465.2 44.4 %collective-permute-start.28 = (bf16[512,2048]{1,0:T(8,128)(2,1)}, bf16[512,2048]{1,0:T(8,128)(2,1)}, u32[]{:S(2)}, u32[]{:S(2)}) collective-permute-start(bf16[512,2048]{1,0:T(8,128)(2,1)} %get-tuple-element.273.refs_0_), channel_id=1, source_target_pairs={{0,2},{2,0},{1,3},{3,1},{4,6},{6,4},{5,7},{7,5},{8,10},{10,8},{9,1... | collective-permute-start | bytes 6291464 | tf_op jit(solution)/shard_map/ppermute | solution.py:41
  465.4 44.9 %collective-permute-start.27 = (bf16[512,2048]{1,0:T(8,128)(2,1)}, bf16[512,2048]{1,0:T(8,128)(2,1)}, u32[]{:S(2)}, u32[]{:S(2)}) collective-permute-start(bf16[512,2048]{1,0:T(8,128)(2,1)} %get-tuple-element.273.refs_0_), channel_id=1, source_target_pairs={{0,1},{1,0},{2,3},{3,2},{4,5},{5,4},{6,7},{7,6},{8,9},{9,8},{10,11... | collective-permute-start | bytes 6291464 | tf_op jit(solution)/shard_map/ppermute | solution.py:37
  510.3 223.7 %reduce-scatter.11.cloned.1.call-start = ((), (), s32[]{:S(2)}) async-start(), calls=%async_computation.10 | async-start | bytes 7077888 | tf_op jit(solution)/shard_map/reduce_scatter | solution.py:517
  513.7 26.5 %collective-permute-start.30 = (bf16[256,2048]{1,0:T(8,128)(2,1)S(1)}, bf16[256,2048]{1,0:T(8,128)(2,1)S(1)}, u32[]{:S(2)}, u32[]{:S(2)}) collective-permute-start(bf16[256,2048]{1,0:T(8,128)(2,1)S(1)} %slice.71), channel_id=1, source_target_pairs={{0,2},{2,0},{1,3},{3,1},{4,6},{6,4},{5,7},{7,5},{8,10},{10,8},{9,1... | collective-permute-start | bytes 3145736 | tf_op jit(solution)/shard_map/ppermute | solution.py:41
  514.9 25.3 %collective-permute-start.29 = (bf16[256,2048]{1,0:T(8,128)(2,1)S(1)}, bf16[256,2048]{1,0:T(8,128)(2,1)S(1)}, u32[]{:S(2)}, u32[]{:S(2)}) collective-permute-start(bf16[256,2048]{1,0:T(8,128)(2,1)S(1)} %slice.70), channel_id=1, source_target_pairs={{0,1},{1,0},{2,3},{3,2},{4,5},{5,4},{6,7},{7,6},{8,9},{9,8},{10,11... | collective-permute-start | bytes 3145736 | tf_op jit(solution)/shard_map/ppermute | solution.py:37
  545.4 41.8 %collective-permute-start.34 = (bf16[2048,256]{1,0:T(8,128)(2,1)}, bf16[2048,256]{1,0:T(8,128)(2,1)S(1)}, u32[]{:S(2)}, u32[]{:S(2)}) collective-permute-start(bf16[2048,256]{1,0:T(8,128)(2,1)} %get-tuple-element.308), channel_id=1, source_target_pairs={{0,2},{2,0},{1,3},{3,1},{4,6},{6,4},{5,7},{7,5},{8,10},{10,8},{9,1... | collective-permute-start | bytes 3145736 | tf_op jit(solution)/shard_map/ppermute | solution.py:41
  546.9 40.4 %collective-permute-start.33 = (bf16[2048,256]{1,0:T(8,128)(2,1)}, bf16[2048,256]{1,0:T(8,128)(2,1)S(1)}, u32[]{:S(2)}, u32[]{:S(2)}) collective-permute-start(bf16[2048,256]{1,0:T(8,128)(2,1)} %get-tuple-element.306), channel_id=1, source_target_pairs={{0,1},{1,0},{2,3},{3,2},{4,5},{5,4},{6,7},{7,6},{8,9},{9,8},{10,11... | collective-permute-start | bytes 3145736 | tf_op jit(solution)/shard_map/ppermute | solution.py:37
  548.3 42.5 %collective-permute-start.32 = (bf16[2048,256]{1,0:T(8,128)(2,1)}, bf16[2048,256]{1,0:T(8,128)(2,1)S(1)}, u32[]{:S(2)}, u32[]{:S(2)}) collective-permute-start(bf16[2048,256]{1,0:T(8,128)(2,1)} %get-tuple-element.304), channel_id=1, source_target_pairs={{0,2},{2,0},{1,3},{3,1},{4,6},{6,4},{5,7},{7,5},{8,10},{10,8},{9,1... | collective-permute-start | bytes 3145736 | tf_op jit(solution)/shard_map/ppermute | solution.py:41
  548.9 43.2 %collective-permute-start.31 = (bf16[2048,256]{1,0:T(8,128)(2,1)}, bf16[2048,256]{1,0:T(8,128)(2,1)}, u32[]{:S(2)}, u32[]{:S(2)}) collective-permute-start(bf16[2048,256]{1,0:T(8,128)(2,1)} %get-tuple-element.302), channel_id=1, source_target_pairs={{0,1},{1,0},{2,3},{3,2},{4,5},{5,4},{6,7},{7,6},{8,9},{9,8},{10,11... | collective-permute-start | bytes 3145736 | tf_op jit(solution)/shard_map/ppermute | solution.py:37
  592.9 27.9 %collective-permute-start.37 = (f32[16,128]{1,0:T(8,128)S(1)}, f32[16,128]{1,0:T(8,128)S(1)}, u32[]{:S(2)}, u32[]{:S(2)}) collective-permute-start(f32[16,128]{1,0:T(8,128)S(1)} %bitcast.74), channel_id=1, source_target_pairs={{0,1},{1,0},{2,3},{3,2},{4,5},{5,4},{6,7},{7,6},{8,9},{9,8},{10,11... | collective-permute-start | bytes 24584 | tf_op jit(solution)/shard_map/ppermute | solution.py:37
  594.4 26.4 %collective-permute-start.38 = (f32[2,4,512]{2,1,0:T(4,128)S(1)}, f32[2,4,512]{2,1,0:T(4,128)S(1)}, u32[]{:S(2)}, u32[]{:S(2)}) collective-permute-start(f32[2,4,512]{2,1,0:T(4,128)S(1)} %reshape.69), channel_id=1, source_target_pairs={{0,1},{1,0},{2,3},{3,2},{4,5},{5,4},{6,7},{7,6},{8,9},{9,8},{10,11... | collective-permute-start | bytes 49160 | tf_op jit(solution)/shard_map/ppermute | solution.py:37
  595.0 25.8 %collective-permute-start.35 = (bf16[2048,256]{1,0:T(8,128)(2,1)}, bf16[2048,256]{1,0:T(8,128)(2,1)}, u32[]{:S(2)}, u32[]{:S(2)}) collective-permute-start(bf16[2048,256]{1,0:T(8,128)(2,1)} %get-tuple-element.328), channel_id=1, source_target_pairs={{0,1},{1,0},{2,3},{3,2},{4,5},{5,4},{6,7},{7,6},{8,9},{9,8},{10,11... | collective-permute-start | bytes 3145736 | tf_op jit(solution)/shard_map/ppermute | solution.py:37
  596.4 24.4 %collective-permute-start.36 = (bf16[2048,256]{1,0:T(8,128)(2,1)}, bf16[2048,256]{1,0:T(8,128)(2,1)}, u32[]{:S(2)}, u32[]{:S(2)}) collective-permute-start(bf16[2048,256]{1,0:T(8,128)(2,1)} %get-tuple-element.329), channel_id=1, source_target_pairs={{0,2},{2,0},{1,3},{3,1},{4,6},{6,4},{5,7},{7,5},{8,10},{10,8},{9,1... | collective-permute-start | bytes 3145736 | tf_op jit(solution)/shard_map/ppermute | solution.py:41
  652.8 25.9 %collective-permute-start.43 = (bf16[2048,256]{1,0:T(8,128)(2,1)}, bf16[2048,256]{1,0:T(8,128)(2,1)}, u32[]{:S(2)}, u32[]{:S(2)}) collective-permute-start(bf16[2048,256]{1,0:T(8,128)(2,1)} %add_convert_fusion.3), channel_id=1, source_target_pairs={{0,1},{1,0},{2,3},{3,2},{4,5},{5,4},{6,7},{7,6},{8,9},{9,8},{10,11... | collective-permute-start | bytes 3145736 | tf_op jit(solution)/shard_map/ppermute | solution.py:37
  653.4 25.4 %collective-permute-start.44 = (bf16[2048,256]{1,0:T(8,128)(2,1)S(1)}, bf16[2048,256]{1,0:T(8,128)(2,1)}, u32[]{:S(2)}, u32[]{:S(2)}) collective-permute-start(bf16[2048,256]{1,0:T(8,128)(2,1)S(1)} %copy-done.20), channel_id=1, source_target_pairs={{0,2},{2,0},{1,3},{3,1},{4,6},{6,4},{5,7},{7,5},{8,10},{10,8},{9,1... | collective-permute-start | bytes 3145736 | tf_op jit(solution)/shard_map/ppermute | solution.py:41
  656.3 22.5 %collective-permute-start.47 = (bf16[256,512]{0,1:T(8,128)(2,1)S(1)}, bf16[256,512]{0,1:T(8,128)(2,1)S(1)}, u32[]{:S(2)}, u32[]{:S(2)}) collective-permute-start(bf16[256,512]{0,1:T(8,128)(2,1)S(1)} %get-tuple-element.390), channel_id=1, source_target_pairs={{24,16},{28,20},{25,17},{29,21},{26,18},{30,22},{27,19},{31,23}} | collective-permute-start | bytes 786440 | tf_op jit(solution)/shard_map/ppermute | solution.py:549
  657.1 21.7 %collective-permute-start.46 = (bf16[256,512]{0,1:T(8,128)(2,1)S(1)}, bf16[256,512]{0,1:T(8,128)(2,1)S(1)}, u32[]{:S(2)}, u32[]{:S(2)}) collective-permute-start(bf16[256,512]{0,1:T(8,128)(2,1)S(1)} %get-tuple-element.391), channel_id=1, source_target_pairs={{0,8},{4,12},{1,9},{5,13},{2,10},{6,14},{3,11},{7,15}} | collective-permute-start | bytes 786440 | tf_op jit(solution)/shard_map/ppermute | solution.py:548
  686.0 24.2 %collective-permute-start.53 = (bf16[2048,256]{1,0:T(8,128)(2,1)S(1)}, bf16[2048,256]{1,0:T(8,128)(2,1)S(1)}, u32[]{:S(2)}, u32[]{:S(2)}) collective-permute-start(bf16[2048,256]{1,0:T(8,128)(2,1)S(1)} %copy-done.19), channel_id=1, source_target_pairs={{0,2},{2,0},{1,3},{3,1},{4,6},{6,4},{5,7},{7,5},{8,10},{10,8},{9,1... | collective-permute-start | bytes 3145736 | tf_op jit(solution)/shard_map/ppermute | solution.py:41
  686.7 24.1 %collective-permute-start.52 = (bf16[2048,256]{1,0:T(8,128)(2,1)S(1)}, bf16[2048,256]{1,0:T(8,128)(2,1)S(1)}, u32[]{:S(2)}, u32[]{:S(2)}) collective-permute-start(bf16[2048,256]{1,0:T(8,128)(2,1)S(1)} %copy-done.18), channel_id=1, source_target_pairs={{0,1},{1,0},{2,3},{3,2},{4,5},{5,4},{6,7},{7,6},{8,9},{9,8},{10,11... | collective-permute-start | bytes 3145736 | tf_op jit(solution)/shard_map/ppermute | solution.py:37
  (76 other events, 1216.9 us)
Sparse Core Ops, SparseCore 0:
  10.5 84.7 all-gather.3
  97.5 149.6 all-gather.5
  248.8 80.7 all-gather.7
  335.5 89.8 reduce-scatter.4
  455.9 89.4 reduce-scatter.6
  547.6 87.9 reduce-scatter.8
  644.3 89.6 reduce-scatter.10
